TPU v7x, 128 devices: a whole 4x4x4 slice. The times are simulated.
128 devices in a mesh: section: 2 (over core), dp: 16 (over y, x), mp: 4 (over z).
Axes of the slice: x: 4, y: 4, z: 4, core: 2. Of those that a mesh axis runs over, the one named last changes fastest.
Arguments:
- out_grad: bfloat16 [512, 8192], P('dp', 'mp'), may hold values from -6 to 6
- upper_w: bfloat16 [2, 14336, 8192], P('section', 'dp', 'mp'), may hold values from -0.0625 to 0.0625
- lower_w: bfloat16 [2, 8192, 14336], P('section', 'mp', 'dp'), may hold values from -0.046875 to 0.046875
- upper_in: bfloat16 [2, 512, 14336], P('section', None, 'mp'), may hold values from -6 to 6
- lower_in: bfloat16 [2, 512, 8192], P('section', None, 'dp'), may hold values from -6 to 6
- upper_deriv: bfloat16 [2, 512, 14336], P('section', 'mp', 'dp'), may hold values from 0.3984375 to 1.5
- lower_deriv: bfloat16 [2, 512, 8192], P('section', 'dp', 'mp'), may hold values from 0.3984375 to 1.5
- proj_upper_in: bfloat16 [2, 64, 14336], P('section', None, 'mp'), may hold values from -0.046875 to 0.046875
- proj_upper_out: bfloat16 [2, 64, 8192], P('section', None, 'mp'), may hold values from -0.0625 to 0.0625
- proj_lower_in: bfloat16 [2, 64, 8192], P('section', None, 'dp'), may hold values from -0.0625 to 0.0625
- proj_lower_out: bfloat16 [2, 64, 14336], P('section', None, 'dp'), may hold values from -0.046875 to 0.046875
- window_ids: int32 [512], replicated, may hold values from 0 to 255
- window_slot: int32 [256], replicated, may hold values from 0 to 255, each once
Outputs:
- section_grads: bfloat16 [2, 512, 8192], P('section', 'dp', 'mp')
- sketches: float32 [2, 2, 256, 4096], P('section', None, ('dp', 'mp'))
Inputs may be any that keep to these rules, and one draw needn't show every extreme that they name: Each window has exactly one row: window_slot is a permutation.
All inputs are finite; a program needn't handle non-finite values.
Results may differ from a plain program's by a relative error of at most 0.0075.
Values may be sent and summed in bfloat16 or wider, within the bound.
No kernel may reach another device: no remote copies, remote signals or barrier semaphores. Data moves between devices by JAX's collectives and lax.ppermute only.
A program may use at most 128 MiB of HBM per device.

v0:
```python
import jax
import jax.numpy as jnp
from jax import lax
from jax.sharding import PartitionSpec as P


def from_behind(block, axis, distance):
    devices = range(lax.axis_size(axis))
    route = [(i - distance, i) for i in devices if i - distance in devices]
    return lax.ppermute(block, axis, route)


def times_t(left, right):
    return lax.dot_general(
        left, right, (((1,), (1,)), ((), ())), preferred_element_type=jnp.float32
    )


def token_lower(dp_src, mp_src, block_id, inner, tokens_dev, rows_block, quota):
    return dp_src * tokens_dev + block_id * rows_block + mp_src * quota + inner


def token_upper(dp_src, mp_src, block_id, inner, tokens_dev, rows_block, quota, ratio):
    flat_row = dp_src * quota + inner
    return (
        (mp_src * ratio + flat_row // rows_block) * tokens_dev
        + block_id * rows_block
        + flat_row % rows_block
    )


def slots_of(token_rows, window_ids, window_slot):
    total_tokens = window_ids.shape[0]
    picked = token_rows[:, None] == jnp.arange(total_tokens, dtype=jnp.int32)[None, :]
    window_row = jnp.sum(jnp.where(picked, window_ids[None, :], 0), axis=1)
    window_count = window_slot.shape[0]
    matched = window_row[:, None] == jnp.arange(window_count, dtype=jnp.int32)[None, :]
    return jnp.sum(jnp.where(matched, window_slot[None, :], 0), axis=1)


def outer_rows(factors, rank_size):
    left = factors[:, :rank_size]
    right = factors[:, rank_size:]
    return (left[:, :, None] * right[:, None, :]).reshape(factors.shape[0], rank_size * rank_size)


def window_sums(targets, factors, window_count, rank_size):
    matched = (targets[:, None] == jnp.arange(window_count, dtype=jnp.int32)[None, :]).astype(
        jnp.float32
    )
    return lax.dot_general(
        matched,
        outer_rows(factors, rank_size),
        (((0,), (0,)), ((), ())),
        precision=lax.Precision.HIGHEST,
        preferred_element_type=jnp.float32,
    )


def body(
    out_grad,
    upper_w,
    lower_w,
    upper_in,
    lower_in,
    upper_deriv,
    lower_deriv,
    proj_upper_in,
    proj_upper_out,
    proj_lower_in,
    proj_lower_out,
    window_ids,
    window_slot,
):
    section_count = lax.axis_size("section")
    dp_count = lax.axis_size("dp")
    mp_count = lax.axis_size("mp")
    section_index = lax.axis_index("section")
    dp_index = lax.axis_index("dp")
    mp_index = lax.axis_index("mp")
    tokens_dev = out_grad.shape[0]
    width_mp = out_grad.shape[1]
    width_ff = upper_deriv.shape[2]
    width_hidden = upper_in.shape[2]
    width_low = lower_in.shape[2]
    rank_size = proj_upper_in.shape[1]
    ratio = dp_count // mp_count
    block_count = 4
    rows_block = tokens_dev // block_count
    quota = rows_block // mp_count
    weight_up = upper_w[0]
    weight_low = lower_w[0]
    acts_upper = upper_in[0].reshape(dp_count, tokens_dev, width_hidden)
    acts_lower = lower_in[0].reshape(dp_count, tokens_dev, width_low)
    deriv_up = upper_deriv[0].reshape(ratio, tokens_dev, width_ff)
    deriv_low = lower_deriv[0]
    pin_up = proj_upper_in[0]
    pout_up = proj_upper_out[0]
    pin_low = proj_lower_in[0]
    pout_low = proj_lower_out[0]

    def advance(turn, carry):
        received, grads, factors_low, factors_up = carry
        block_id = turn - (section_count - 1 - section_index)
        is_live = (block_id >= 0) & (block_id < block_count)
        block_safe = jnp.clip(block_id, 0, block_count - 1)
        first_row = block_safe * rows_block
        top_block = lax.dynamic_slice_in_dim(out_grad, first_row, rows_block, 0)
        grad_up = jnp.where(section_index == section_count - 1, top_block, received)
        gathered_up = lax.all_gather(grad_up, "dp", axis=0, tiled=True)
        inputs_up = lax.dynamic_slice_in_dim(acts_upper, first_row, rows_block, 1).reshape(
            dp_count * rows_block, width_hidden
        )
        grad_rows = gathered_up
        input_rows = inputs_up
        summed_up = lax.psum_scatter(
            jnp.concatenate(
                [
                    times_t(grad_rows, weight_up),
                    times_t(input_rows, pin_up),
                    times_t(grad_rows, pout_up),
                ],
                axis=1,
            ),
            "mp",
            scatter_dimension=0,
            tiled=True,
        )
        scale_up = lax.dynamic_slice_in_dim(deriv_up, first_row, rows_block, 1).reshape(
            ratio * rows_block, width_ff
        )
        grad_mid = (summed_up[:, :width_ff] * scale_up.astype(jnp.float32)).astype(jnp.bfloat16)
        owned_up = lax.dynamic_slice_in_dim(summed_up[:, width_ff:], dp_index * quota, quota, 0)
        gathered_low = lax.all_gather(grad_mid, "mp", axis=0, tiled=True)
        inputs_low = lax.dynamic_slice_in_dim(acts_lower, first_row, rows_block, 1).reshape(
            dp_count * rows_block, width_low
        )
        grad_rows = gathered_low
        input_rows = inputs_low
        summed_low = lax.psum_scatter(
            jnp.concatenate(
                [
                    times_t(grad_rows, weight_low),
                    times_t(input_rows, pin_low),
                    times_t(grad_rows, pout_low),
                ],
                axis=1,
            ),
            "dp",
            scatter_dimension=0,
            tiled=True,
        )
        scale_low = lax.dynamic_slice_in_dim(deriv_low, first_row, rows_block, 0)
        grad_out = (summed_low[:, :width_mp] * scale_low.astype(jnp.float32)).astype(jnp.bfloat16)
        owned_low = lax.dynamic_slice_in_dim(summed_low[:, width_mp:], mp_index * quota, quota, 0)
        previous = lax.dynamic_slice_in_dim(grads, first_row, rows_block, 0)
        grads = lax.dynamic_update_slice_in_dim(
            grads, jnp.where(is_live, grad_out, previous), first_row, 0
        )
        prev_low = lax.dynamic_slice_in_dim(factors_low, block_safe, 1, 0)
        factors_low = lax.dynamic_update_slice_in_dim(
            factors_low, jnp.where(is_live, owned_low[None], prev_low), block_safe, 0
        )
        prev_up = lax.dynamic_slice_in_dim(factors_up, block_safe, 1, 0)
        factors_up = lax.dynamic_update_slice_in_dim(
            factors_up, jnp.where(is_live, owned_up[None], prev_up), block_safe, 0
        )
        received = from_behind(grad_out, "section", -1)
        return (received, grads, factors_low, factors_up)

    start_carry = (
        jnp.zeros((rows_block, width_mp), jnp.bfloat16),
        jnp.zeros((tokens_dev, width_mp), jnp.bfloat16),
        jnp.zeros((block_count, quota, 2 * rank_size), jnp.float32),
        jnp.zeros((block_count, quota, 2 * rank_size), jnp.float32),
    )
    _, grads, factors_low, factors_up = lax.fori_loop(
        0, block_count + section_count - 1, advance, start_carry
    )
    flat_low = factors_low.reshape(block_count * quota, 2 * rank_size)
    flat_up = factors_up.reshape(block_count * quota, 2 * rank_size)
    window_count = window_slot.shape[0]
    block_grid = jnp.arange(block_count, dtype=jnp.int32)[:, None]
    inner_grid = jnp.arange(quota, dtype=jnp.int32)[None, :]
    tokens_low = token_lower(
        dp_index, mp_index, block_grid, inner_grid, tokens_dev, rows_block, quota
    ).reshape(-1)
    tokens_up = token_upper(
        dp_index, mp_index, block_grid, inner_grid, tokens_dev, rows_block, quota, ratio
    ).reshape(-1)
    low_part = window_sums(
        slots_of(tokens_low, window_ids, window_slot), flat_low, window_count, rank_size
    )
    up_part = window_sums(
        slots_of(tokens_up, window_ids, window_slot), flat_up, window_count, rank_size
    )
    sketch = lax.psum_scatter(
        jnp.stack([low_part, up_part]), ("dp", "mp"), scatter_dimension=1, tiled=True
    )
    return (grads[None], sketch[None])


def solution(mesh):
    placed = (
        P("dp", "mp"),
        P("section", "dp", "mp"),
        P("section", "mp", "dp"),
        P("section", None, "mp"),
        P("section", None, "dp"),
        P("section", "mp", "dp"),
        P("section", "dp", "mp"),
        P("section", None, "mp"),
        P("section", None, "mp"),
        P("section", None, "dp"),
        P("section", None, "dp"),
        P(),
        P(),
    )
    return jax.shard_map(
        body,
        mesh=mesh,
        in_specs=placed,
        out_specs=(P("section", "dp", "mp"), P("section", None, ("dp", "mp"), None)),
        check_vma=False,
    )
```

profile of v0, /device:TPU:1, one launch (start us, length us, event | category | flops | bytes accessed | tf_op | source)
XLA Modules:
  0.0 993.9 jit_solution(14661798061254032778)
XLA Ops:
  8.1 802.5 %while.21 = (s32[]{:T(128)}, bf16[8,2048]{1,0:T(8,128)(2,1)S(1)}, bf16[32,2048]{1,0:T(8,128)(2,1)S(1)}, f32[4,2,128]{2,1,0:T(2,128)S(1)}, f32[4,2,128]{2,1,0:T(2...) while((s32[]{:T(128)}, bf16[8,2048]{1,0:T(8,128)(2,1)S(1)}, ...), condition=%wide.region_3.4_spmd, body=%wide.region_0.3_spmd.sunk | while | flops 1055576576 | bytes 28484304 | solution.py:177
  9.0 20.0 %all_gather.20 = bf16[128,2048]{1,0:T(8,128)(2,1)S(1)} all-gather(bf16[8,2048]{1,0:T(8,128)(2,1)S(1)} %dynamic-slice_select_fusion.2), channel_id=1, replica_groups=mesh['section'=2,'dp'=16,'mp'=4] {'dp'}, dimensions={0}, use_global_device_ids=true | all-gather | bytes 557056 | tf_op jit(solution)/shard_map/while/body/eval_jaxpr/all_gather | solution.py:110
  37.2 24.4 %reduce-scatter.3.cloned.1.call-done = f32[32,1024]{1,0:T(8,128)} async-done(((f32[128,1024]{1,0:T(8,128)}), f32[32,1024]{1,0:T(8,128)}) %reduce-scatter.3.cloned.1.call-update) | async-done | bytes 131088 | tf_op jit(solution)/shard_map/while/body/eval_jaxpr/reduce_scatter | solution.py:116
  62.5 9.3 all_gather.21
  78.0 88.1 %all-reduce.9.cloned.1.call-done = f32[128,2176]{1,0:T(8,128)} async-done(((f32[128,2176]{1,0:T(8,128)}), f32[128,2176]{1,0:T(8,128)}) %all-reduce.9.cloned.1.call-update) | async-done | bytes 1114128 | tf_op jit(solution)/shard_map/while
  167.0 4.1 collective-permute-start
  172.8 17.6 %all_gather.20 = bf16[128,2048]{1,0:T(8,128)(2,1)S(1)} all-gather(bf16[8,2048]{1,0:T(8,128)(2,1)S(1)} %dynamic-slice_select_fusion.2), channel_id=1, replica_groups=mesh['section'=2,'dp'=16,'mp'=4] {'dp'}, dimensions={0}, use_global_device_ids=true | all-gather | bytes 557056 | tf_op jit(solution)/shard_map/while/body/eval_jaxpr/all_gather | solution.py:110
  198.7 22.7 %reduce-scatter.3.cloned.1.call-done = f32[32,1024]{1,0:T(8,128)} async-done(((f32[128,1024]{1,0:T(8,128)}), f32[32,1024]{1,0:T(8,128)}) %reduce-scatter.3.cloned.1.call-update) | async-done | bytes 131088 | tf_op jit(solution)/shard_map/while/body/eval_jaxpr/reduce_scatter | solution.py:116
  222.2 9.6 all_gather.21
  238.0 87.8 %all-reduce.9.cloned.1.call-done = f32[128,2176]{1,0:T(8,128)} async-done(((f32[128,2176]{1,0:T(8,128)}), f32[128,2176]{1,0:T(8,128)}) %all-reduce.9.cloned.1.call-update) | async-done | bytes 1114128 | tf_op jit(solution)/shard_map/while
  326.6 4.1 collective-permute-start
  332.4 17.6 %all_gather.20 = bf16[128,2048]{1,0:T(8,128)(2,1)S(1)} all-gather(bf16[8,2048]{1,0:T(8,128)(2,1)S(1)} %dynamic-slice_select_fusion.2), channel_id=1, replica_groups=mesh['section'=2,'dp'=16,'mp'=4] {'dp'}, dimensions={0}, use_global_device_ids=true | all-gather | bytes 557056 | tf_op jit(solution)/shard_map/while/body/eval_jaxpr/all_gather | solution.py:110
  358.3 22.7 %reduce-scatter.3.cloned.1.call-done = f32[32,1024]{1,0:T(8,128)} async-done(((f32[128,1024]{1,0:T(8,128)}), f32[32,1024]{1,0:T(8,128)}) %reduce-scatter.3.cloned.1.call-update) | async-done | bytes 131088 | tf_op jit(solution)/shard_map/while/body/eval_jaxpr/reduce_scatter | solution.py:116
  381.9 9.6 all_gather.21
  397.7 87.7 %all-reduce.9.cloned.1.call-done = f32[128,2176]{1,0:T(8,128)} async-done(((f32[128,2176]{1,0:T(8,128)}), f32[128,2176]{1,0:T(8,128)}) %all-reduce.9.cloned.1.call-update) | async-done | bytes 1114128 | tf_op jit(solution)/shard_map/while
  492.1 17.6 %all_gather.20 = bf16[128,2048]{1,0:T(8,128)(2,1)S(1)} all-gather(bf16[8,2048]{1,0:T(8,128)(2,1)S(1)} %dynamic-slice_select_fusion.2), channel_id=1, replica_groups=mesh['section'=2,'dp'=16,'mp'=4] {'dp'}, dimensions={0}, use_global_device_ids=true | all-gather | bytes 557056 | tf_op jit(solution)/shard_map/while/body/eval_jaxpr/all_gather | solution.py:110
  518.0 22.7 %reduce-scatter.3.cloned.1.call-done = f32[32,1024]{1,0:T(8,128)} async-done(((f32[128,1024]{1,0:T(8,128)}), f32[32,1024]{1,0:T(8,128)}) %reduce-scatter.3.cloned.1.call-update) | async-done | bytes 131088 | tf_op jit(solution)/shard_map/while/body/eval_jaxpr/reduce_scatter | solution.py:116
  541.6 9.6 all_gather.21
  557.3 87.8 %all-reduce.9.cloned.1.call-done = f32[128,2176]{1,0:T(8,128)} async-done(((f32[128,2176]{1,0:T(8,128)}), f32[128,2176]{1,0:T(8,128)}) %all-reduce.9.cloned.1.call-update) | async-done | bytes 1114128 | tf_op jit(solution)/shard_map/while
  651.8 17.6 %all_gather.20 = bf16[128,2048]{1,0:T(8,128)(2,1)S(1)} all-gather(bf16[8,2048]{1,0:T(8,128)(2,1)S(1)} %dynamic-slice_select_fusion.2), channel_id=1, replica_groups=mesh['section'=2,'dp'=16,'mp'=4] {'dp'}, dimensions={0}, use_global_device_ids=true | all-gather | bytes 557056 | tf_op jit(solution)/shard_map/while/body/eval_jaxpr/all_gather | solution.py:110
  677.7 22.7 %reduce-scatter.3.cloned.1.call-done = f32[32,1024]{1,0:T(8,128)} async-done(((f32[128,1024]{1,0:T(8,128)}), f32[32,1024]{1,0:T(8,128)}) %reduce-scatter.3.cloned.1.call-update) | async-done | bytes 131088 | tf_op jit(solution)/shard_map/while/body/eval_jaxpr/reduce_scatter | solution.py:116
  701.3 9.6 all_gather.21
  717.0 87.7 %all-reduce.9.cloned.1.call-done = f32[128,2176]{1,0:T(8,128)} async-done(((f32[128,2176]{1,0:T(8,128)}), f32[128,2176]{1,0:T(8,128)}) %all-reduce.9.cloned.1.call-update) | async-done | bytes 1114128 | tf_op jit(solution)/shard_map/while
  821.6 163.2 %all-reduce.7.cloned.1.call-done = f32[2,256,4096]{2,1,0:T(8,128)} async-done(((f32[2,256,4096]{2,1,0:T(8,128)}), f32[2,256,4096]{2,1,0:T(8,128)}) %all-reduce.7.cloned.1.call-update) | async-done | bytes 8388624
  (187 shorter events, 109.6 us)
Async XLA Ops:
  8.1 803.5 %copy-start.4 = (s32[512]{0:T(512)S(1)}, s32[512]{0:T(512)}, u32[]{:S(2)}) copy-start(s32[512]{0:T(512)} %param.26) | copy-start | bytes 6148
  8.1 803.7 %copy-start.5 = (s32[256]{0:T(256)S(1)}, s32[256]{0:T(256)}, u32[]{:S(2)}) copy-start(s32[256]{0:T(256)} %param.27) | copy-start | bytes 3076
  8.1 25.5 %copy-start = (bf16[64,3584]{1,0:T(8,128)(2,1)S(1)}, bf16[64,3584]{1,0:T(8,128)(2,1)}, u32[]{:S(2)}) copy-start(bf16[64,3584]{1,0:T(8,128)(2,1)} %get-tuple-element.691) | copy-start | bytes 1376260 | tf_op jit(solution)/shard_map/while
  8.1 53.5 %reduce-scatter.3.cloned.1.call-start = ((), (), s32[]{:S(2)}) async-start(), calls=%async_computation.2 | async-start | bytes 655360 | tf_op jit(solution)/shard_map/while/body/eval_jaxpr/reduce_scatter | solution.py:116
  35.2 40.0 %copy-start.1 = (bf16[64,896]{1,0:T(8,128)(2,1)S(1)}, bf16[64,896]{1,0:T(8,128)(2,1)}, u32[]{:S(2)}) copy-start(bf16[64,896]{1,0:T(8,128)(2,1)} %get-tuple-element.697) | copy-start | bytes 344068 | tf_op jit(solution)/shard_map/while
  36.1 130.0 %all-reduce.9.cloned.1.call-start = ((), (), s32[]{:S(2)}) async-start(), calls=%async_computation.3 | async-start | bytes 2228224 | tf_op jit(solution)/shard_map/while
  167.0 5.0 collective-permute-start
  171.9 49.4 %reduce-scatter.3.cloned.1.call-start = ((), (), s32[]{:S(2)}) async-start(), calls=%async_computation.2 | async-start | bytes 655360 | tf_op jit(solution)/shard_map/while/body/eval_jaxpr/reduce_scatter | solution.py:116
  196.6 38.6 %copy-start.1 = (bf16[64,896]{1,0:T(8,128)(2,1)S(1)}, bf16[64,896]{1,0:T(8,128)(2,1)}, u32[]{:S(2)}) copy-start(bf16[64,896]{1,0:T(8,128)(2,1)} %get-tuple-element.697) | copy-start | bytes 344068 | tf_op jit(solution)/shard_map/while
  197.5 128.3 %all-reduce.9.cloned.1.call-start = ((), (), s32[]{:S(2)}) async-start(), calls=%async_computation.3 | async-start | bytes 2228224 | tf_op jit(solution)/shard_map/while
  326.6 5.0 collective-permute-start
  331.6 49.4 %reduce-scatter.3.cloned.1.call-start = ((), (), s32[]{:S(2)}) async-start(), calls=%async_computation.2 | async-start | bytes 655360 | tf_op jit(solution)/shard_map/while/body/eval_jaxpr/reduce_scatter | solution.py:116
  356.3 38.6 %copy-start.1 = (bf16[64,896]{1,0:T(8,128)(2,1)S(1)}, bf16[64,896]{1,0:T(8,128)(2,1)}, u32[]{:S(2)}) copy-start(bf16[64,896]{1,0:T(8,128)(2,1)} %get-tuple-element.697) | copy-start | bytes 344068 | tf_op jit(solution)/shard_map/while
  357.2 128.2 %all-reduce.9.cloned.1.call-start = ((), (), s32[]{:S(2)}) async-start(), calls=%async_computation.3 | async-start | bytes 2228224 | tf_op jit(solution)/shard_map/while
  486.3 5.0 collective-permute-start
  491.3 49.4 %reduce-scatter.3.cloned.1.call-start = ((), (), s32[]{:S(2)}) async-start(), calls=%async_computation.2 | async-start | bytes 655360 | tf_op jit(solution)/shard_map/while/body/eval_jaxpr/reduce_scatter | solution.py:116
  515.9 38.6 %copy-start.1 = (bf16[64,896]{1,0:T(8,128)(2,1)S(1)}, bf16[64,896]{1,0:T(8,128)(2,1)}, u32[]{:S(2)}) copy-start(bf16[64,896]{1,0:T(8,128)(2,1)} %get-tuple-element.697) | copy-start | bytes 344068 | tf_op jit(solution)/shard_map/while
  516.8 128.3 %all-reduce.9.cloned.1.call-start = ((), (), s32[]{:S(2)}) async-start(), calls=%async_computation.3 | async-start | bytes 2228224 | tf_op jit(solution)/shard_map/while
  646.0 5.0 collective-permute-start
  650.9 49.4 %reduce-scatter.3.cloned.1.call-start = ((), (), s32[]{:S(2)}) async-start(), calls=%async_computation.2 | async-start | bytes 655360 | tf_op jit(solution)/shard_map/while/body/eval_jaxpr/reduce_scatter | solution.py:116
  675.6 38.6 %copy-start.1 = (bf16[64,896]{1,0:T(8,128)(2,1)S(1)}, bf16[64,896]{1,0:T(8,128)(2,1)}, u32[]{:S(2)}) copy-start(bf16[64,896]{1,0:T(8,128)(2,1)} %get-tuple-element.697) | copy-start | bytes 344068 | tf_op jit(solution)/shard_map/while
  676.5 128.2 %all-reduce.9.cloned.1.call-start = ((), (), s32[]{:S(2)}) async-start(), calls=%async_computation.3 | async-start | bytes 2228224 | tf_op jit(solution)/shard_map/while
  805.6 5.0 collective-permute-start
  810.6 174.2 %all-reduce.7.cloned.1.call-start = ((), (), s32[]{:S(2)}) async-start(), calls=%async_computation.1 | async-start | bytes 16777216
  (21 other events, 182.6 us)
Sparse Core Ops, SparseCore 0:
  36.2 25.3 reduce-scatter.2
  76.8 89.2 all-reduce.8
  197.6 23.6 reduce-scatter.2
  236.8 88.9 all-reduce.8
  357.3 23.6 reduce-scatter.2
  396.5 88.8 all-reduce.8
  517.0 23.6 reduce-scatter.2
  556.2 88.9 all-reduce.8
  676.6 23.6 reduce-scatter.2
  715.8 88.8 all-reduce.8
Sparse Core Ops, SparseCore 1:
  819.8 165.0 all-reduce.6
where the time goes:
time: 998 us; the launch traced here: 994 us
  waiting for transfers between devices  718 us (72%)
  blocking collectives  138 us (14%)
  matrix products  57.7 us (6%)
  other arithmetic  22.3 us (2%)
  starting transfers between devices  20.8 us (2%)
  local copies, waits for them, and re-layouts  16.5 us (2%)
  between operations  16.2 us (2%)
    while x15, waiting for transfers between devices  439 us
    unnamed x2, waiting for transfers between devices  163 us
    reduce_scatter x5, waiting for transfers between devices, advance(): lax.psum_scatter(jnp.concatenate([times_t(grad_rows, weight_up), times_t(...  115 us
    all_gather x5, blocking collectives, advance(): gathered_up = lax.all_gather(grad_up, 'dp', axis=0, tiled=True)  90.5 us
    dot_general x30, matrix products, times_t(): lax.dot_general(left, right, (((1,), (1,)), ((), ())), preferred_element_...  53.9 us
    all_gather x5, blocking collectives, advance(): gathered_low = lax.all_gather(grad_mid, 'mp', axis=0, tiled=True)  47.9 us
    ppermute x5, starting transfers between devices, from_behind(): return lax.ppermute(block, axis, route)  20.6 us
  transfers between devices with their start and end apart: 16, of which 16 were waited for; matrix products, arithmetic and copies ran while one was open for 1% of the time, Pallas kernels for 0%

commit v1 on v0

v1 whole, which is shorter than its diff:
```python
import jax
import jax.numpy as jnp
from jax import lax
from jax.sharding import PartitionSpec as P

BF16 = jnp.bfloat16
F32 = jnp.float32


def times_t(left, right):
    return lax.dot_general(
        left, right, (((1,), (1,)), ((), ())), preferred_element_type=F32
    )


def swap_sections(block):
    return lax.ppermute(block, "section", [(0, 1), (1, 0)])


def shift_mp(block, distance):
    count = lax.axis_size("mp")
    return lax.ppermute(
        block, "mp", [(i, (i + distance) % count) for i in range(count)]
    )


def gather_dp(block):
    count = lax.axis_size("dp")
    copies = jnp.broadcast_to(block[None], (count,) + block.shape)
    got = lax.all_to_all(copies, "dp", 0, 0, tiled=True)
    return got.reshape(count * block.shape[0], block.shape[1])


def scatter_sum_dp(partial):
    count = lax.axis_size("dp")
    got = lax.all_to_all(partial, "dp", 0, 0, tiled=True)
    got = got.reshape(count, partial.shape[0] // count, partial.shape[1])
    return jnp.sum(got.astype(F32), axis=0)


def scatter_sum_mp(partial):
    count = lax.axis_size("mp")
    mine = lax.axis_index("mp")
    rows = partial.shape[0] // count

    def part(distance):
        return lax.dynamic_slice_in_dim(
            partial, ((mine + distance) % count) * rows, rows, 0
        )

    total = part(0).astype(F32)
    for distance in range(1, count):
        total = total + shift_mp(part(distance), distance).astype(F32)
    return total


def gather_mp(block):
    count = lax.axis_size("mp")
    mine = lax.axis_index("mp")
    rows = block.shape[0]
    whole = jnp.zeros((count * rows, block.shape[1]), block.dtype)
    whole = lax.dynamic_update_slice_in_dim(whole, block, mine * rows, 0)
    for distance in range(1, count):
        got = shift_mp(block, distance)
        whole = lax.dynamic_update_slice_in_dim(
            whole, got, ((mine - distance) % count) * rows, 0
        )
    return whole


def body(
    out_grad,
    upper_w,
    lower_w,
    upper_in,
    lower_in,
    upper_deriv,
    lower_deriv,
    proj_upper_in,
    proj_upper_out,
    proj_lower_in,
    proj_lower_out,
    window_ids,
    window_slot,
):
    sections = lax.axis_size("section")
    dp_count = lax.axis_size("dp")
    mp_count = lax.axis_size("mp")
    core = lax.axis_index("section")
    rank = proj_upper_in.shape[1]
    tokens_dp, width = out_grad.shape
    hidden = upper_deriv.shape[2]
    tokens = tokens_dp * dp_count
    half = tokens_dp // sections

    def halves(array):
        cut = array.reshape(
            array.shape[0] // tokens_dp, sections, half, array.shape[1]
        )
        mine = lax.dynamic_index_in_dim(cut, core, 1, keepdims=False)
        other = lax.dynamic_index_in_dim(cut, 1 - core, 1, keepdims=False)
        shape = (array.shape[0] // sections, array.shape[1])
        return mine.reshape(shape), other.reshape(shape)

    def exchanged(array):
        mine, other = halves(array)
        return mine, swap_sections(other)

    def of_section(pair, section):
        own, received = pair
        return jnp.where(core == section, own, received)

    grad, _ = halves(out_grad)
    first = gather_dp(grad)

    weight_up = (upper_w[0], swap_sections(upper_w[0]))
    pout_up = (proj_upper_out[0], swap_sections(proj_upper_out[0]))
    factor_up = exchanged(times_t(upper_in[0], proj_upper_in[0]).astype(BF16))
    deriv_up = exchanged(upper_deriv[0])
    weight_low = (lower_w[0], swap_sections(lower_w[0]))
    pout_low = (proj_lower_out[0], swap_sections(proj_lower_out[0]))
    factor_low = exchanged(times_t(lower_in[0], proj_lower_in[0]).astype(BF16))
    deriv_low = exchanged(lower_deriv[0])

    gathered = first
    grads = [None] * sections
    ups = [None] * sections
    lows = [None] * sections
    for section in range(sections - 1, -1, -1):
        with jax.named_scope(f"up_{section}"):
            partial = jnp.concatenate(
                [
                    times_t(gathered, of_section(weight_up, section)).astype(BF16),
                    of_section(factor_up, section),
                    times_t(gathered, of_section(pout_up, section)).astype(BF16),
                ],
                axis=1,
            )
            summed = scatter_sum_mp(partial)
            scale = of_section(deriv_up, section).astype(F32)
            middle = (summed[:, :hidden] * scale).astype(BF16)
            block = jnp.concatenate([middle, summed[:, hidden:].astype(BF16)], axis=1)
            whole = gather_mp(block)
            middle_all = whole[:, :hidden]
            ups[section] = whole[:, hidden:]
        with jax.named_scope(f"low_{section}"):
            partial = jnp.concatenate(
                [
                    times_t(middle_all, of_section(weight_low, section)).astype(BF16),
                    of_section(factor_low, section),
                    times_t(middle_all, of_section(pout_low, section)).astype(BF16),
                ],
                axis=1,
            )
            summed = scatter_sum_dp(partial)
            scale = of_section(deriv_low, section).astype(F32)
            grad = (summed[:, :width] * scale).astype(BF16)
            grads[section] = grad
            low = summed[:, width:].astype(BF16)
            if section > 0:
                got = gather_dp(jnp.concatenate([grad, low], axis=1))
                gathered = got[:, :width]
                lows[section] = got[:, width:]
            else:
                lows[section] = gather_dp(low)

    with jax.named_scope("outputs"):
        pair = [jnp.concatenate([lows[s], ups[s]], axis=1) for s in range(sections)]
        mine = jnp.where(core == 0, pair[0], pair[1])
        other = jnp.where(core == 0, pair[1], pair[0])
        got = swap_sections(other)

        def joined(own, received, rows):
            own = own.reshape(-1, rows, own.shape[1])
            received = received.reshape(-1, rows, received.shape[1])
            stack = jnp.stack(
                [
                    jnp.where(core == 0, own, received),
                    jnp.where(core == 0, received, own),
                ],
                axis=1,
            )
            return stack.reshape(-1, own.shape[2])

        factors = joined(mine, got, half)
        mine = jnp.where(core == 0, grads[0], grads[1])
        other = jnp.where(core == 0, grads[1], grads[0])
        grads_out = joined(mine, swap_sections(other), half)

        windows = window_slot.shape[0]
        owned = windows // (dp_count * mp_count)
        position = lax.axis_index("dp") * mp_count + lax.axis_index("mp")
        rows = position * owned + jnp.arange(owned, dtype=jnp.int32)
        holds = window_slot[None, :] == rows[:, None]
        window = jnp.sum(
            jnp.where(holds, jnp.arange(windows, dtype=jnp.int32)[None, :], 0), axis=1
        )
        hits = window_ids[None, :] == window[:, None]
        sketches = []
        for place in range(2):
            pair = factors[:, 2 * rank * place : 2 * rank * (place + 1)]
            left = pair[:, :rank]
            right = pair[:, rank:]
            masked = jnp.where(hits[:, :, None], left[None], jnp.zeros((), BF16))
            sums = lax.dot_general(
                masked, right, (((1,), (0,)), ((), ())), preferred_element_type=F32
            )
            sketches.append(sums.reshape(owned, rank * rank))
        sketch = jnp.stack(sketches)
    return (grads_out[None], sketch[None])


def solution(mesh):
    placed = (
        P("dp", "mp"),
        P("section", "dp", "mp"),
        P("section", "mp", "dp"),
        P("section", None, "mp"),
        P("section", None, "dp"),
        P("section", "mp", "dp"),
        P("section", "dp", "mp"),
        P("section", None, "mp"),
        P("section", None, "mp"),
        P("section", None, "dp"),
        P("section", None, "dp"),
        P(),
        P(),
    )
    return jax.shard_map(
        body,
        mesh=mesh,
        in_specs=placed,
        out_specs=(P("section", "dp", "mp"), P("section", None, ("dp", "mp"), None)),
        check_vma=False,
    )
```

time: 998 us -> 175 us (0.18)
  waiting for transfers between devices: 718 us -> 60.1 us
  blocking collectives: 138 us -> 19.2 us
  starting transfers between devices: 20.8 us -> 56.4 us
  matrix products: 57.7 us -> 24 us
  other arithmetic: 22.3 us -> 3.54 us
  between operations: 16.2 us -> 1.24 us
    while x15 -> x0, waiting for transfers between devices: 439 us -> none
    unnamed x2 -> x0, waiting for transfers between devices: 163 us -> none
    all_gather x10 -> x0, blocking collectives: 138 us -> none  [the longest x5 90.5 us: advance(): gathered_up = lax.all_gather(grad_up, 'dp', axis=0, tiled=True)]
    reduce_scatter x5 -> x0, waiting for transfers between devices: 115 us -> none  [advance(): lax.psum_scatter(jnp.concatenate([times_t(grad_rows, weight_up), times_t(...]
    all_to_all x0 -> x4, waiting for transfers between devices: none -> 42.7 us  [the longest x2 28.9 us: scatter_sum_dp(): got = lax.all_to_all(partial, 'dp', 0, 0, tiled=True)]
    dot_general x30 -> x10, matrix products: 53.9 us -> 23.4 us  [times_t(): lax.dot_general(left, right, (((1,), (1,)), ((), ())), preferred_element_...]
    all_to_all x0 -> x4, starting transfers between devices: none -> 19.4 us  [the longest x2 11.7 us: gather_dp(): got = lax.all_to_all(copies, 'dp', 0, 0, tiled=True)]
    all_to_all x0 -> x1, blocking collectives: none -> 19.2 us  [gather_dp(): got = lax.all_to_all(copies, 'dp', 0, 0, tiled=True)]
  transfers between devices with their start and end apart: 16 -> 26, of which waited for: 16 -> 13; matrix products, arithmetic and copies ran while one was open for 1% -> 9% of each run, Pallas kernels for 0% -> 0%
where the time goes in v1:
time: 175 us; the launch traced here: 174 us
  waiting for transfers between devices  60.1 us (34%)
  starting transfers between devices  56.4 us (32%)
  matrix products  24 us (14%)
  blocking collectives  19.2 us (11%)
  local copies, waits for them, and re-layouts  9.54 us (5%)
  other arithmetic  3.54 us (2%)
    all_to_all x2, waiting for transfers between devices, scatter_sum_dp(): got = lax.all_to_all(partial, 'dp', 0, 0, tiled=True)  28.9 us
    dot_general x10, matrix products, times_t(): lax.dot_general(left, right, (((1,), (1,)), ((), ())), preferred_element_...  23.4 us
    ppermute x12, starting transfers between devices, shift_mp(): lax.ppermute(block, 'mp', [(i, (i + distance) % count) for i in range(cou...  21.2 us
    all_to_all x1, blocking collectives, gather_dp(): got = lax.all_to_all(copies, 'dp', 0, 0, tiled=True)  19.2 us
    ppermute x10, starting transfers between devices, swap_sections(): return lax.ppermute(block, 'section', [(0, 1), (1, 0)])  15.8 us
    ppermute x12, waiting for transfers between devices, shift_mp(): lax.ppermute(block, 'mp', [(i, (i + distance) % count) for i in range(cou...  15.7 us
    all_to_all x2, waiting for transfers between devices, gather_dp(): got = lax.all_to_all(copies, 'dp', 0, 0, tiled=True)  13.8 us
    all_to_all x2, starting transfers between devices, gather_dp(): got = lax.all_to_all(copies, 'dp', 0, 0, tiled=True)  11.7 us
  transfers between devices with their start and end apart: 26, of which 13 were waited for; matrix products, arithmetic and copies ran while one was open for 9% of the time, Pallas kernels for 0%

profile of v1, /device:TPU:1, one launch (start us, length us, event | category | flops | bytes accessed | tf_op | source)
XLA Modules:
  0.0 174.0 jit_solution(13133440804992180782)
XLA Ops:
  4.3 7.0 %all-to-all-start = ((bf16[16,16,2048]{2,1,0:T(8,128)(2,1)}), bf16[16,16,2048]{2,1,0:T(8,128)(2,1)S(1)}, u32[]{:S(2)}, u32[]{:S(2)}) async-start(bf16[16,16,2048]{2,1,0:T(8,128)(2,1)} %broadcast_in_dim.73), calls=%async_computation | async-start | bytes 2097152 | tf_op jit(solution)/shard_map/all_to_all | solution.py:30
  12.5 3.3 %fusion.26 = bf16[512,64]{0,1:T(8,128)(2,1)S(1)} fusion(bf16[1,512,3584]{2,1,0:T(8,128)(2,1)} %param.16, bf16[1,64,3584]{2,1,0:T(8,128)(2,1)S(1)} %copy-done.2), kind=kOutput, calls=%fused_computation.20 | convolution fusion | flops 234913792 | bytes 4194304 | tf_op jit(solution)/shard_map/dot_general | solution.py:11
  18.3 9.3 %all-to-all-done = bf16[16,16,2048]{2,1,0:T(8,128)(2,1)S(1)} async-done(((bf16[16,16,2048]{2,1,0:T(8,128)(2,1)}), bf16[16,16,2048]{2,1,0:T(8,128)(2,1)S(1)}, u32[]{:S(2)}, u32[]{:S(2)}) %all-to-all-start) | async-done | bytes 1048608 | tf_op jit(solution)/shard_map/all_to_all | solution.py:30
  28.1 3.4 %fusion.20 = bf16[256,896]{1,0:T(8,128)(2,1)S(1)} fusion(bf16[256,2048]{1,0:T(8,128)(2,1)S(1)} %bitcast.116, bf16[896,2048]{1,0:T(8,128)(2,1)} %collective-permute-done, pred[]{:T(512)S(6)} %eq.36, bf16[1,896,2048]{2,1,0:T(8,128)(2,1)} %param.14), kind=kOutput, calls=%fused_computation.18 | convolution fusion | flops 941588480 | bytes 8847361 | tf_op jit(solution)/shard_map/up_1/dot_general | solution.py:11
  33.4 3.3 %collective-permute-start.4 = (bf16[64,1024]{1,0:T(8,128)(2,1)S(1)}, bf16[64,1024]{1,0:T(8,128)(2,1)S(1)}, u32[]{:S(2)}, u32[]{:S(2)}) collective-permute-start(bf16[64,1024]{1,0:T(8,128)(2,1)S(1)} %get-tuple-element.9), channel_id=1, source_target_pairs={{0,2},{1,3},{2,0},{3,1},{4,6},{5,7},{6,4},{7,5},{8,10},{9,11},{10,... | collective-permute-start | bytes 393224 | tf_op jit(solution)/shard_map/up_1/ppermute | solution.py:22
  37.4 4.2 %collective-permute-start.6 = (bf16[64,896]{1,0:T(8,128)(2,1)S(1)}, bf16[64,896]{1,0:T(8,128)(2,1)S(1)}, u32[]{:S(2)}, u32[]{:S(2)}) collective-permute-start(bf16[64,896]{1,0:T(8,128)(2,1)S(1)} %bitcast.137), channel_id=1, source_target_pairs={{0,64},{64,0},{1,65},{65,1},{2,66},{66,2},{3,67},{67,3},{4,68},{68... | collective-permute-start | bytes 344072 | tf_op jit(solution)/shard_map/ppermute | solution.py:17
  42.5 2.4 %collective-permute-start.11 = (bf16[256,64]{1,0:T(8,128)(2,1)S(1)}, bf16[256,64]{1,0:T(8,128)(2,1)S(1)}, u32[]{:S(2)}, u32[]{:S(2)}) collective-permute-start(bf16[256,64]{1,0:T(8,128)(2,1)S(1)} %bitcast.138), channel_id=1, source_target_pairs={{0,64},{64,0},{1,65},{65,1},{2,66},{66,2},{3,67},{67,3},{4,68},{68... | collective-permute-start | bytes 98312 | tf_op jit(solution)/shard_map/ppermute | solution.py:17
  49.2 4.8 %collective-permute-done.7 = bf16[64,1024]{1,0:T(8,128)(2,1)S(1)} collective-permute-done((bf16[64,1024]{1,0:T(8,128)(2,1)S(1)}, bf16[64,1024]{1,0:T(8,128)(2,1)S(1)}, u32[]{:S(2)}, u32[]{:S(2)}) %collective-permute-start.7) | collective-permute-done | bytes 131104 | tf_op jit(solution)/shard_map/up_1/ppermute | solution.py:22
  55.6 3.3 %fusion.14 = bf16[256,2048]{1,0:T(8,128)(2,1)S(1)} fusion(bf16[2048,896]{1,0:T(8,128)(2,1)} %collective-permute-done.10, pred[]{:T(512)S(6)} %eq.36, bf16[256,1024]{1,0:T(8,128)(2,1)S(1)} %constant_dynamic-update-slice_fusion.4, bf16[1,2048,896]{2,1,0:T(8,128)(2,1)} %param.15), kind=kOutput, calls=%fused_computation.14 | convolution fusion | flops 941883392 | bytes 8847361 | tf_op jit(solution)/shard_map/low_1/dot_general | solution.py:11
  60.9 4.0 %all-to-all-start.1 = ((bf16[16,16,2176]{2,1,0:T(8,128)(2,1)}), bf16[16,16,2176]{2,1,0:T(8,128)(2,1)S(1)}, u32[]{:S(2)}, u32[]{:S(2)}) async-start(bf16[16,16,2176]{2,1,0:T(8,128)(2,1)} %bitcast.20), calls=%async_computation.1 | async-start | bytes 2228224 | tf_op jit(solution)/shard_map/low_1/all_to_all | solution.py:36
  65.0 2.6 %collective-permute-start.13 = (bf16[16,2048]{1,0:T(8,128)(2,1)S(1)}, bf16[16,2048]{1,0:T(8,128)(2,1)S(1)}, u32[]{:S(2)}, u32[]{:S(2)}) collective-permute-start(bf16[16,2048]{1,0:T(8,128)(2,1)S(1)} %dynamic-slice_bitcast_fusion), channel_id=1, source_target_pairs={{0,64},{64,0},{1,65},{65,1},{2,66},{66,2},{3,67},{67,3},{4,68},{68... | collective-permute-start | bytes 196616 | tf_op jit(solution)/shard_map/ppermute | solution.py:17
  67.6 12.9 %all-to-all-done.1 = bf16[16,16,2176]{2,1,0:T(8,128)(2,1)S(1)} async-done(((bf16[16,16,2176]{2,1,0:T(8,128)(2,1)}), bf16[16,16,2176]{2,1,0:T(8,128)(2,1)S(1)}, u32[]{:S(2)}, u32[]{:S(2)}) %all-to-all-start.1) | async-done | bytes 1114144 | tf_op jit(solution)/shard_map/low_1/all_to_all | solution.py:36
  81.4 19.2 %all_to_all.33 = bf16[16,16,2176]{2,1,0:T(8,128)(2,1)S(1)} all-to-all(bf16[16,16,2176]{2,1,0:T(8,128)(2,1)S(1)} %broadcast_in_dim.74), channel_id=1, replica_groups=mesh['section'=2,'dp'=16,'mp'=4] {'dp'}, dimensions={0} | all-to-all | bytes 2228224 | tf_op jit(solution)/shard_map/low_1/all_to_all | solution.py:30
  101.2 4.5 %fusion.23 = bf16[256,896]{1,0:T(8,128)(2,1)S(1)} fusion(bf16[896,2048]{1,0:T(8,128)(2,1)} %collective-permute-done, pred[]{:T(512)S(6)} %eq.35, bf16[256,2176]{1,0:T(8,128)(2,1)S(1)} %bitcast.118, bf16[1,896,2048]{2,1,0:T(8,128)(2,1)} %param.14), kind=kOutput, calls=%fused_computation.19 | convolution fusion | flops 941588480 | bytes 8847361 | tf_op jit(solution)/shard_map/up_0/dot_general | solution.py:11
  105.8 4.4 %collective-permute-start.14 = (bf16[64,1024]{1,0:T(8,128)(2,1)S(1)}, bf16[64,1024]{1,0:T(8,128)(2,1)S(1)}, u32[]{:S(2)}, u32[]{:S(2)}) collective-permute-start(bf16[64,1024]{1,0:T(8,128)(2,1)S(1)} %get-tuple-element.4), channel_id=1, source_target_pairs={{0,1},{1,2},{2,3},{3,0},{4,5},{5,6},{6,7},{7,4},{8,9},{9,10},{10,1... | collective-permute-start | bytes 393224 | tf_op jit(solution)/shard_map/up_0/ppermute | solution.py:22
  110.3 2.6 %collective-permute-start.15 = (bf16[64,1024]{1,0:T(8,128)(2,1)S(1)}, bf16[64,1024]{1,0:T(8,128)(2,1)S(1)}, u32[]{:S(2)}, u32[]{:S(2)}) collective-permute-start(bf16[64,1024]{1,0:T(8,128)(2,1)S(1)} %get-tuple-element.6), channel_id=1, source_target_pairs={{0,2},{1,3},{2,0},{3,1},{4,6},{5,7},{6,4},{7,5},{8,10},{9,11},{10,... | collective-permute-start | bytes 393224 | tf_op jit(solution)/shard_map/up_0/ppermute | solution.py:22
  114.6 3.4 %collective-permute-done.15 = bf16[64,1024]{1,0:T(8,128)(2,1)S(1)} collective-permute-done((bf16[64,1024]{1,0:T(8,128)(2,1)S(1)}, bf16[64,1024]{1,0:T(8,128)(2,1)S(1)}, u32[]{:S(2)}, u32[]{:S(2)}) %collective-permute-start.15) | collective-permute-done | bytes 131104 | tf_op jit(solution)/shard_map/up_0/ppermute | solution.py:22
  120.2 2.6 %collective-permute-start.18 = (bf16[64,1024]{1,0:T(8,128)(2,1)S(1)}, bf16[64,1024]{1,0:T(8,128)(2,1)S(1)}, u32[]{:S(2)}, u32[]{:S(2)}) collective-permute-start(bf16[64,1024]{1,0:T(8,128)(2,1)S(1)} %get-tuple-element.20), channel_id=1, source_target_pairs={{0,2},{1,3},{2,0},{3,1},{4,6},{5,7},{6,4},{7,5},{8,10},{9,11},{10,... | collective-permute-start | bytes 393224 | tf_op jit(solution)/shard_map/up_0/ppermute | solution.py:22
  124.0 4.3 %collective-permute-done.18 = bf16[64,1024]{1,0:T(8,128)(2,1)S(1)} collective-permute-done((bf16[64,1024]{1,0:T(8,128)(2,1)S(1)}, bf16[64,1024]{1,0:T(8,128)(2,1)S(1)}, u32[]{:S(2)}, u32[]{:S(2)}) %collective-permute-start.18) | collective-permute-done | bytes 131104 | tf_op jit(solution)/shard_map/up_0/ppermute | solution.py:22
  129.7 4.5 %fusion.17 = bf16[256,2048]{1,0:T(8,128)(2,1)S(1)} fusion(bf16[2048,896]{1,0:T(8,128)(2,1)} %collective-permute-done.10, pred[]{:T(512)S(6)} %eq.35, bf16[256,1024]{1,0:T(8,128)(2,1)S(1)} %constant_dynamic-update-slice_fusion, bf16[1,2048,896]{2,1,0:T(8,128)(2,1)} %param.15), kind=kOutput, calls=%fused_computation.15 | convolution fusion | flops 941883392 | bytes 8847361 | tf_op jit(solution)/shard_map/low_0/dot_general | solution.py:11
  136.1 3.7 %all-to-all-start.3 = ((bf16[16,16,2176]{2,1,0:T(8,128)(2,1)}), bf16[16,16,2176]{2,1,0:T(8,128)(2,1)S(1)}, u32[]{:S(2)}, u32[]{:S(2)}) async-start(bf16[16,16,2176]{2,1,0:T(8,128)(2,1)} %bitcast.25), calls=%async_computation.3 | async-start | bytes 2228224 | tf_op jit(solution)/shard_map/low_0/all_to_all | solution.py:36
  141.0 15.9 %all-to-all-done.3 = bf16[16,16,2176]{2,1,0:T(8,128)(2,1)S(1)} async-done(((bf16[16,16,2176]{2,1,0:T(8,128)(2,1)}), bf16[16,16,2176]{2,1,0:T(8,128)(2,1)S(1)}, u32[]{:S(2)}, u32[]{:S(2)}) %all-to-all-start.3) | async-done | bytes 1114144 | tf_op jit(solution)/shard_map/low_0/all_to_all | solution.py:36
  157.7 4.7 %all-to-all-start.4 = ((bf16[16,16,128]{2,1,0:T(8,128)(2,1)}), bf16[16,16,128]{2,1,0:T(8,128)(2,1)S(1)}, u32[]{:S(2)}, u32[]{:S(2)}) async-start(bf16[16,16,128]{2,1,0:T(8,128)(2,1)} %broadcast_in_dim.78), calls=%async_computation.4 | async-start | bytes 131072 | tf_op jit(solution)/shard_map/low_0/all_to_all | solution.py:30
  164.4 4.5 %all-to-all-done.4 = bf16[16,16,128]{2,1,0:T(8,128)(2,1)S(1)} async-done(((bf16[16,16,128]{2,1,0:T(8,128)(2,1)}), bf16[16,16,128]{2,1,0:T(8,128)(2,1)S(1)}, u32[]{:S(2)}, u32[]{:S(2)}) %all-to-all-start.4) | async-done | bytes 65568 | tf_op jit(solution)/shard_map/low_0/all_to_all | solution.py:30
  (125 shorter events, 37.9 us)
Async XLA Ops:
  0.7 27.5 %collective-permute-start = (bf16[896,2048]{1,0:T(8,128)(2,1)}, bf16[896,2048]{1,0:T(8,128)(2,1)}, u32[]{:S(2)}, u32[]{:S(2)}) collective-permute-start(bf16[896,2048]{1,0:T(8,128)(2,1)} %bitcast.141), channel_id=1, source_target_pairs={{0,64},{64,0},{1,65},{65,1},{2,66},{66,2},{3,67},{67,3},{4,68},{68... | collective-permute-start | bytes 11010056 | tf_op jit(solution)/shard_map/ppermute | solution.py:17
  2.2 53.5 %collective-permute-start.10 = (bf16[2048,896]{1,0:T(8,128)(2,1)}, bf16[2048,896]{1,0:T(8,128)(2,1)}, u32[]{:S(2)}, u32[]{:S(2)}) collective-permute-start(bf16[2048,896]{1,0:T(8,128)(2,1)} %bitcast.142), channel_id=1, source_target_pairs={{0,64},{64,0},{1,65},{65,1},{2,66},{66,2},{3,67},{67,3},{4,68},{68... | collective-permute-start | bytes 11010056 | tf_op jit(solution)/shard_map/ppermute | solution.py:17
  4.3 23.3 %all-to-all-start = ((bf16[16,16,2048]{2,1,0:T(8,128)(2,1)}), bf16[16,16,2048]{2,1,0:T(8,128)(2,1)S(1)}, u32[]{:S(2)}, u32[]{:S(2)}) async-start(bf16[16,16,2048]{2,1,0:T(8,128)(2,1)} %broadcast_in_dim.73), calls=%async_computation | async-start | bytes 2097152 | tf_op jit(solution)/shard_map/all_to_all | solution.py:30
  31.7 10.0 %collective-permute-start.3 = (bf16[64,1024]{1,0:T(8,128)(2,1)S(1)}, bf16[64,1024]{1,0:T(8,128)(2,1)S(1)}, u32[]{:S(2)}, u32[]{:S(2)}) collective-permute-start(bf16[64,1024]{1,0:T(8,128)(2,1)S(1)} %get-tuple-element.7), channel_id=1, source_target_pairs={{0,1},{1,2},{2,3},{3,0},{4,5},{5,6},{6,7},{7,4},{8,9},{9,10},{10,1... | collective-permute-start | bytes 393224 | tf_op jit(solution)/shard_map/up_1/ppermute | solution.py:22
  33.4 9.2 %collective-permute-start.4 = (bf16[64,1024]{1,0:T(8,128)(2,1)S(1)}, bf16[64,1024]{1,0:T(8,128)(2,1)S(1)}, u32[]{:S(2)}, u32[]{:S(2)}) collective-permute-start(bf16[64,1024]{1,0:T(8,128)(2,1)S(1)} %get-tuple-element.9), channel_id=1, source_target_pairs={{0,2},{1,3},{2,0},{3,1},{4,6},{5,7},{6,4},{7,5},{8,10},{9,11},{10,... | collective-permute-start | bytes 393224 | tf_op jit(solution)/shard_map/up_1/ppermute | solution.py:22
  36.7 8.2 %collective-permute-start.5 = (bf16[64,1024]{1,0:T(8,128)(2,1)S(1)}, bf16[64,1024]{1,0:T(8,128)(2,1)S(1)}, u32[]{:S(2)}, u32[]{:S(2)}) collective-permute-start(bf16[64,1024]{1,0:T(8,128)(2,1)S(1)} %get-tuple-element.8), channel_id=1, source_target_pairs={{0,3},{1,0},{2,1},{3,2},{4,7},{5,4},{6,5},{7,6},{8,11},{9,8},{10,9... | collective-permute-start | bytes 393224 | tf_op jit(solution)/shard_map/up_1/ppermute | solution.py:22
  37.4 7.6 %collective-permute-start.6 = (bf16[64,896]{1,0:T(8,128)(2,1)S(1)}, bf16[64,896]{1,0:T(8,128)(2,1)S(1)}, u32[]{:S(2)}, u32[]{:S(2)}) collective-permute-start(bf16[64,896]{1,0:T(8,128)(2,1)S(1)} %bitcast.137), channel_id=1, source_target_pairs={{0,64},{64,0},{1,65},{65,1},{2,66},{66,2},{3,67},{67,3},{4,68},{68... | collective-permute-start | bytes 344072 | tf_op jit(solution)/shard_map/ppermute | solution.py:17
  41.6 12.5 %collective-permute-start.12 = (bf16[64,896]{1,0:T(8,128)(2,1)}, bf16[64,896]{1,0:T(8,128)(2,1)S(1)}, u32[]{:S(2)}, u32[]{:S(2)}) collective-permute-start(bf16[64,896]{1,0:T(8,128)(2,1)} %bitcast.19), channel_id=1, source_target_pairs={{0,64},{64,0},{1,65},{65,1},{2,66},{66,2},{3,67},{67,3},{4,68},{68... | collective-permute-start | bytes 344072 | tf_op jit(solution)/shard_map/ppermute | solution.py:17
  42.5 4.6 %collective-permute-start.11 = (bf16[256,64]{1,0:T(8,128)(2,1)S(1)}, bf16[256,64]{1,0:T(8,128)(2,1)S(1)}, u32[]{:S(2)}, u32[]{:S(2)}) collective-permute-start(bf16[256,64]{1,0:T(8,128)(2,1)S(1)} %bitcast.138), channel_id=1, source_target_pairs={{0,64},{64,0},{1,65},{65,1},{2,66},{66,2},{3,67},{67,3},{4,68},{68... | collective-permute-start | bytes 98312 | tf_op jit(solution)/shard_map/ppermute | solution.py:17
  45.1 8.9 %collective-permute-start.7 = (bf16[64,1024]{1,0:T(8,128)(2,1)S(1)}, bf16[64,1024]{1,0:T(8,128)(2,1)S(1)}, u32[]{:S(2)}, u32[]{:S(2)}) collective-permute-start(bf16[64,1024]{1,0:T(8,128)(2,1)S(1)} %get-tuple-element.26), channel_id=1, source_target_pairs={{0,1},{1,2},{2,3},{3,0},{4,5},{5,6},{6,7},{7,4},{8,9},{9,10},{10,1... | collective-permute-start | bytes 393224 | tf_op jit(solution)/shard_map/up_1/ppermute | solution.py:22
  45.5 8.6 %collective-permute-start.8 = (bf16[64,1024]{1,0:T(8,128)(2,1)S(1)}, bf16[64,1024]{1,0:T(8,128)(2,1)S(1)}, u32[]{:S(2)}, u32[]{:S(2)}) collective-permute-start(bf16[64,1024]{1,0:T(8,128)(2,1)S(1)} %get-tuple-element.26), channel_id=1, source_target_pairs={{0,2},{1,3},{2,0},{3,1},{4,6},{5,7},{6,4},{7,5},{8,10},{9,11},{10,... | collective-permute-start | bytes 393224 | tf_op jit(solution)/shard_map/up_1/ppermute | solution.py:22
  47.2 6.9 %collective-permute-start.9 = (bf16[64,1024]{1,0:T(8,128)(2,1)S(1)}, bf16[64,1024]{1,0:T(8,128)(2,1)S(1)}, u32[]{:S(2)}, u32[]{:S(2)}) collective-permute-start(bf16[64,1024]{1,0:T(8,128)(2,1)S(1)} %get-tuple-element.26), channel_id=1, source_target_pairs={{0,3},{1,0},{2,1},{3,2},{4,7},{5,4},{6,5},{7,6},{8,11},{9,8},{10,9... | collective-permute-start | bytes 393224 | tf_op jit(solution)/shard_map/up_1/ppermute | solution.py:22
  60.9 19.6 %all-to-all-start.1 = ((bf16[16,16,2176]{2,1,0:T(8,128)(2,1)}), bf16[16,16,2176]{2,1,0:T(8,128)(2,1)S(1)}, u32[]{:S(2)}, u32[]{:S(2)}) async-start(bf16[16,16,2176]{2,1,0:T(8,128)(2,1)} %bitcast.20), calls=%async_computation.1 | async-start | bytes 2228224 | tf_op jit(solution)/shard_map/low_1/all_to_all | solution.py:36
  65.0 15.8 %collective-permute-start.13 = (bf16[16,2048]{1,0:T(8,128)(2,1)S(1)}, bf16[16,2048]{1,0:T(8,128)(2,1)S(1)}, u32[]{:S(2)}, u32[]{:S(2)}) collective-permute-start(bf16[16,2048]{1,0:T(8,128)(2,1)S(1)} %dynamic-slice_bitcast_fusion), channel_id=1, source_target_pairs={{0,64},{64,0},{1,65},{65,1},{2,66},{66,2},{3,67},{67,3},{4,68},{68... | collective-permute-start | bytes 196616 | tf_op jit(solution)/shard_map/ppermute | solution.py:17
  105.8 8.8 %collective-permute-start.14 = (bf16[64,1024]{1,0:T(8,128)(2,1)S(1)}, bf16[64,1024]{1,0:T(8,128)(2,1)S(1)}, u32[]{:S(2)}, u32[]{:S(2)}) collective-permute-start(bf16[64,1024]{1,0:T(8,128)(2,1)S(1)} %get-tuple-element.4), channel_id=1, source_target_pairs={{0,1},{1,2},{2,3},{3,0},{4,5},{5,6},{6,7},{7,4},{8,9},{9,10},{10,1... | collective-permute-start | bytes 393224 | tf_op jit(solution)/shard_map/up_0/ppermute | solution.py:22
  110.3 7.7 %collective-permute-start.15 = (bf16[64,1024]{1,0:T(8,128)(2,1)S(1)}, bf16[64,1024]{1,0:T(8,128)(2,1)S(1)}, u32[]{:S(2)}, u32[]{:S(2)}) collective-permute-start(bf16[64,1024]{1,0:T(8,128)(2,1)S(1)} %get-tuple-element.6), channel_id=1, source_target_pairs={{0,2},{1,3},{2,0},{3,1},{4,6},{5,7},{6,4},{7,5},{8,10},{9,11},{10,... | collective-permute-start | bytes 393224 | tf_op jit(solution)/shard_map/up_0/ppermute | solution.py:22
  112.8 5.4 %collective-permute-start.16 = (bf16[64,1024]{1,0:T(8,128)(2,1)S(1)}, bf16[64,1024]{1,0:T(8,128)(2,1)S(1)}, u32[]{:S(2)}, u32[]{:S(2)}) collective-permute-start(bf16[64,1024]{1,0:T(8,128)(2,1)S(1)} %get-tuple-element.5), channel_id=1, source_target_pairs={{0,3},{1,0},{2,1},{3,2},{4,7},{5,4},{6,5},{7,6},{8,11},{9,8},{10,9... | collective-permute-start | bytes 393224 | tf_op jit(solution)/shard_map/up_0/ppermute | solution.py:22
  118.5 5.5 %collective-permute-start.17 = (bf16[64,1024]{1,0:T(8,128)(2,1)S(1)}, bf16[64,1024]{1,0:T(8,128)(2,1)S(1)}, u32[]{:S(2)}, u32[]{:S(2)}) collective-permute-start(bf16[64,1024]{1,0:T(8,128)(2,1)S(1)} %get-tuple-element.20), channel_id=1, source_target_pairs={{0,1},{1,2},{2,3},{3,0},{4,5},{5,6},{6,7},{7,4},{8,9},{9,10},{10,1... | collective-permute-start | bytes 393224 | tf_op jit(solution)/shard_map/up_0/ppermute | solution.py:22
  120.2 8.1 %collective-permute-start.18 = (bf16[64,1024]{1,0:T(8,128)(2,1)S(1)}, bf16[64,1024]{1,0:T(8,128)(2,1)S(1)}, u32[]{:S(2)}, u32[]{:S(2)}) collective-permute-start(bf16[64,1024]{1,0:T(8,128)(2,1)S(1)} %get-tuple-element.20), channel_id=1, source_target_pairs={{0,2},{1,3},{2,0},{3,1},{4,6},{5,7},{6,4},{7,5},{8,10},{9,11},{10,... | collective-permute-start | bytes 393224 | tf_op jit(solution)/shard_map/up_0/ppermute | solution.py:22
  122.8 5.6 %collective-permute-start.19 = (bf16[64,1024]{1,0:T(8,128)(2,1)S(1)}, bf16[64,1024]{1,0:T(8,128)(2,1)S(1)}, u32[]{:S(2)}, u32[]{:S(2)}) collective-permute-start(bf16[64,1024]{1,0:T(8,128)(2,1)S(1)} %get-tuple-element.20), channel_id=1, source_target_pairs={{0,3},{1,0},{2,1},{3,2},{4,7},{5,4},{6,5},{7,6},{8,11},{9,8},{10,9... | collective-permute-start | bytes 393224 | tf_op jit(solution)/shard_map/up_0/ppermute | solution.py:22
  136.1 20.8 %all-to-all-start.3 = ((bf16[16,16,2176]{2,1,0:T(8,128)(2,1)}), bf16[16,16,2176]{2,1,0:T(8,128)(2,1)S(1)}, u32[]{:S(2)}, u32[]{:S(2)}) async-start(bf16[16,16,2176]{2,1,0:T(8,128)(2,1)} %bitcast.25), calls=%async_computation.3 | async-start | bytes 2228224 | tf_op jit(solution)/shard_map/low_0/all_to_all | solution.py:36
  157.7 11.2 %all-to-all-start.4 = ((bf16[16,16,128]{2,1,0:T(8,128)(2,1)}), bf16[16,16,128]{2,1,0:T(8,128)(2,1)S(1)}, u32[]{:S(2)}, u32[]{:S(2)}) async-start(bf16[16,16,128]{2,1,0:T(8,128)(2,1)} %broadcast_in_dim.78), calls=%async_computation.4 | async-start | bytes 131072 | tf_op jit(solution)/shard_map/low_0/all_to_all | solution.py:30
  163.3 7.8 %collective-permute-start.20 = (bf16[16,2048]{1,0:T(8,128)(2,1)S(1)}, bf16[16,2048]{1,0:T(8,128)(2,1)S(1)}, u32[]{:S(2)}, u32[]{:S(2)}) collective-permute-start(bf16[16,2048]{1,0:T(8,128)(2,1)S(1)} %get-tuple-element.2), channel_id=1, source_target_pairs={{0,64},{64,0},{1,65},{65,1},{2,66},{66,2},{3,67},{67,3},{4,68},{68... | collective-permute-start | bytes 196616 | tf_op jit(solution)/shard_map/outputs/ppermute | solution.py:17
  168.9 3.2 %collective-permute-start.21 = (bf16[256,256]{1,0:T(8,128)(2,1)S(1)}, bf16[256,256]{1,0:T(8,128)(2,1)S(1)}, u32[]{:S(2)}, u32[]{:S(2)}) collective-permute-start(bf16[256,256]{1,0:T(8,128)(2,1)S(1)} %maximum_select_fusion.1), channel_id=1, source_target_pairs={{0,64},{64,0},{1,65},{65,1},{2,66},{66,2},{3,67},{67,3},{4,68},{68... | collective-permute-start | bytes 393224 | tf_op jit(solution)/shard_map/outputs/ppermute | solution.py:17
  (13 other events, 94.5 us)

commit v2 on v1

--- a/solution.py
+++ b/solution.py
@@ -1,6 +1,8 @@
 import jax
 import jax.numpy as jnp
 from jax import lax
+from jax.experimental import pallas as pl
+from jax.experimental.pallas import tpu as pltpu
 from jax.sharding import PartitionSpec as P
 
 BF16 = jnp.bfloat16
@@ -36,22 +38,6 @@
     got = lax.all_to_all(partial, "dp", 0, 0, tiled=True)
     got = got.reshape(count, partial.shape[0] // count, partial.shape[1])
     return jnp.sum(got.astype(F32), axis=0)
-
-
-def scatter_sum_mp(partial):
-    count = lax.axis_size("mp")
-    mine = lax.axis_index("mp")
-    rows = partial.shape[0] // count
-
-    def part(distance):
-        return lax.dynamic_slice_in_dim(
-            partial, ((mine + distance) % count) * rows, rows, 0
-        )
-
-    total = part(0).astype(F32)
-    for distance in range(1, count):
-        total = total + shift_mp(part(distance), distance).astype(F32)
-    return total
 
 
 def gather_mp(block):
@@ -66,6 +52,129 @@
             whole, got, ((mine - distance) % count) * rows, 0
         )
     return whole
+
+
+def upper_product(place, rows, own, received, tail, side, count):
+    tokens, depth = rows.shape
+    width = own.shape[0]
+    extra = tail.shape[0]
+    size = tokens // count
+    step = depth // 4
+
+    def kernel(place_ref, x_ref, own_ref, got_ref, tail_ref, side_ref, *rest):
+        outs, acc = rest[:count], rest[count]
+        k = pl.program_id(0)
+
+        @pl.when(k == 0)
+        def _():
+            acc[:, :width] = jnp.zeros((tokens, width), F32)
+            acc[:, width:] = side_ref[...].astype(F32)
+
+        @pl.when(place_ref[0] == 1)
+        def _():
+            acc[:, :width] += times_t(x_ref[...], own_ref[...])
+
+        @pl.when(place_ref[0] != 1)
+        def _():
+            acc[:, :width] += times_t(x_ref[...], got_ref[...])
+
+        acc[:, width:] += times_t(x_ref[...], tail_ref[...])
+
+        @pl.when(k == pl.num_programs(0) - 1)
+        def _():
+            for d in range(count):
+                first = pl.multiple_of(lax.rem(place_ref[1] + d, count) * size, size)
+                outs[d][...] = acc[pl.ds(first, size), :].astype(BF16)
+
+    return pl.pallas_call(
+        kernel,
+        out_shape=[jax.ShapeDtypeStruct((size, width + extra), BF16)] * count,
+        grid_spec=pltpu.PrefetchScalarGridSpec(
+            num_scalar_prefetch=1,
+            grid=(4,),
+            in_specs=[
+                pl.BlockSpec((tokens, step), lambda k, p: (0, k)),
+                pl.BlockSpec((width, step), lambda k, p: (0, k * p[0])),
+                pl.BlockSpec((width, step), lambda k, p: (0, k * (1 - p[0]))),
+                pl.BlockSpec((extra, step), lambda k, p: (0, k)),
+                pl.BlockSpec((tokens, extra), lambda k, p: (0, 0)),
+            ],
+            out_specs=[pl.BlockSpec((size, width + extra), lambda k, p: (0, 0))]
+            * count,
+            scratch_shapes=[pltpu.VMEM((tokens, width + extra), F32)],
+        ),
+        name="upper_product",
+    )(place, rows, own, received, tail, side)
+
+
+def lower_product(place, blocks, own, received, tail=None, side=None):
+    count = len(blocks)
+    size = blocks[0].shape[0]
+    width, depth = own.shape
+    rest_width = blocks[0].shape[1] - depth
+    tokens = count * size
+    extra = 0 if tail is None else tail.shape[0]
+    step = width // 4
+
+    def kernel(place_ref, *refs):
+        block_refs = refs[:count]
+        own_ref, got_ref = refs[count : count + 2]
+        more = refs[count + 2 :]
+        if extra:
+            tail_ref, side_ref = more[:2]
+            more = more[2:]
+        out, rest_out, x_ref = more
+        n = pl.program_id(0)
+
+        @pl.when(n == 0)
+        def _():
+            for d in range(count):
+                first = lax.rem(place_ref[1] + count - d, count) * size
+                first = pl.multiple_of(first, size)
+                x_ref[pl.ds(first, size), :] = block_refs[d][:, :depth]
+                rest_out[pl.ds(first, size), :] = block_refs[d][:, depth:]
+            if extra:
+                out[:, width:] = (
+                    side_ref[...].astype(F32) + times_t(x_ref[...], tail_ref[...])
+                ).astype(BF16)
+
+        here = pl.ds(pl.multiple_of(n * step, step), step)
+
+        @pl.when(place_ref[0] == 1)
+        def _():
+            out[:, here] = times_t(x_ref[...], own_ref[...]).astype(BF16)
+
+        @pl.when(place_ref[0] != 1)
+        def _():
+            out[:, here] = times_t(x_ref[...], got_ref[...]).astype(BF16)
+
+    whole = lambda n, p: (0, 0)
+    in_specs = [pl.BlockSpec(blocks[0].shape, whole)] * count + [
+        pl.BlockSpec((step, depth), lambda n, p: (n * p[0], 0)),
+        pl.BlockSpec((step, depth), lambda n, p: (n * (1 - p[0]), 0)),
+    ]
+    operands = list(blocks) + [own, received]
+    if extra:
+        in_specs += [pl.BlockSpec(tail.shape, whole), pl.BlockSpec(side.shape, whole)]
+        operands += [tail, side]
+    return pl.pallas_call(
+        kernel,
+        out_shape=[
+            jax.ShapeDtypeStruct((tokens, width + extra), BF16),
+            jax.ShapeDtypeStruct((tokens, rest_width), BF16),
+        ],
+        grid_spec=pltpu.PrefetchScalarGridSpec(
+            num_scalar_prefetch=1,
+            grid=(4,),
+            in_specs=in_specs,
+            out_specs=[
+                pl.BlockSpec((tokens, width + extra), whole),
+                pl.BlockSpec((tokens, rest_width), whole),
+            ],
+            scratch_shapes=[pltpu.VMEM((tokens, depth), BF16)],
+        ),
+        name="lower_product",
+    )(place, *operands)
 
 
 def body(
@@ -111,58 +220,74 @@
         return jnp.where(core == section, own, received)
 
     grad, _ = halves(out_grad)
-    first = gather_dp(grad)
+    gathered = gather_dp(grad)
+    mp_index = lax.axis_index("mp")
+
+    def padded(array, before, after, axis):
+        pads = [(0, 0), (0, 0)]
+        pads[axis] = (before, after)
+        return jnp.pad(array, pads)
 
     weight_up = (upper_w[0], swap_sections(upper_w[0]))
     pout_up = (proj_upper_out[0], swap_sections(proj_upper_out[0]))
     factor_up = exchanged(times_t(upper_in[0], proj_upper_in[0]).astype(BF16))
+    factor_low = exchanged(times_t(lower_in[0], proj_lower_in[0]).astype(BF16))
     deriv_up = exchanged(upper_deriv[0])
-    weight_low = (lower_w[0], swap_sections(lower_w[0]))
-    pout_low = (proj_lower_out[0], swap_sections(proj_lower_out[0]))
-    factor_low = exchanged(times_t(lower_in[0], proj_lower_in[0]).astype(BF16))
-    deriv_low = exchanged(lower_deriv[0])
-
-    gathered = first
+    low_w, pout_w, deriv_w, gathered = lax.optimization_barrier(
+        (lower_w[0], proj_lower_out[0], lower_deriv[0], gathered)
+    )
+    weight_low = (low_w, swap_sections(low_w))
+    pout_low = (pout_w, swap_sections(pout_w))
+    deriv_low = exchanged(deriv_w)
+
     grads = [None] * sections
     ups = [None] * sections
     lows = [None] * sections
     for section in range(sections - 1, -1, -1):
+        place = jnp.stack([(core == section).astype(jnp.int32), mp_index])
         with jax.named_scope(f"up_{section}"):
-            partial = jnp.concatenate(
-                [
-                    times_t(gathered, of_section(weight_up, section)).astype(BF16),
-                    of_section(factor_up, section),
-                    times_t(gathered, of_section(pout_up, section)).astype(BF16),
-                ],
-                axis=1,
+            parts = upper_product(
+                place,
+                gathered[:, :width],
+                *weight_up,
+                padded(of_section(pout_up, section), rank, 0, 0),
+                padded(of_section(factor_up, section), 0, rank, 1),
+                mp_count,
             )
-            summed = scatter_sum_mp(partial)
+            summed = parts[0].astype(F32)
+            for distance in range(1, mp_count):
+                summed += shift_mp(parts[distance], distance).astype(F32)
             scale = of_section(deriv_up, section).astype(F32)
             middle = (summed[:, :hidden] * scale).astype(BF16)
             block = jnp.concatenate([middle, summed[:, hidden:].astype(BF16)], axis=1)
-            whole = gather_mp(block)
-            middle_all = whole[:, :hidden]
-            ups[section] = whole[:, hidden:]
+            blocks = [block] + [shift_mp(block, d) for d in range(1, mp_count)]
         with jax.named_scope(f"low_{section}"):
-            partial = jnp.concatenate(
-                [
-                    times_t(middle_all, of_section(weight_low, section)).astype(BF16),
-                    of_section(factor_low, section),
-                    times_t(middle_all, of_section(pout_low, section)).astype(BF16),
-                ],
-                axis=1,
-            )
-            summed = scatter_sum_dp(partial)
             scale = of_section(deriv_low, section).astype(F32)
-            grad = (summed[:, :width] * scale).astype(BF16)
+            pout = of_section(pout_low, section)
+            if section > 0:
+                side = [of_section(factor_low, s) for s in range(section, -1, -1)]
+                side = jnp.concatenate(
+                    [padded(part, 0, rank, 1) for part in side], axis=1
+                )
+                tail = padded(pout, rank, side.shape[1] - 2 * rank, 0)
+                partial, ups[section] = lower_product(
+                    place, blocks, *weight_low, tail, side
+                )
+                summed = scatter_sum_dp(partial)
+                grad = (summed[:, :width] * scale).astype(BF16)
+                low = summed[:, width:].astype(BF16)
+                gathered = gather_dp(jnp.concatenate([grad, low], axis=1))
+                lows[section] = gathered[:, width : width + 2 * rank]
+                left_low = gathered[:, width + 2 * rank : width + 3 * rank]
+            else:
+                right = gather_dp(times_t(middle, pout).astype(BF16))
+                right = right.reshape(dp_count, middle.shape[0], rank)
+                right = jnp.sum(right.astype(F32), axis=0).astype(BF16)
+                partial, ups[section] = lower_product(place, blocks, *weight_low)
+                summed = scatter_sum_dp(partial)
+                grad = (summed * scale).astype(BF16)
+                lows[section] = jnp.concatenate([left_low, gather_mp(right)], axis=1)
             grads[section] = grad
-            low = summed[:, width:].astype(BF16)
-            if section > 0:
-                got = gather_dp(jnp.concatenate([grad, low], axis=1))
-                gathered = got[:, :width]
-                lows[section] = got[:, width:]
-            else:
-                lows[section] = gather_dp(low)
 
     with jax.named_scope("outputs"):
         pair = [jnp.concatenate([lows[s], ups[s]], axis=1) for s in range(sections)]

time: 175 us -> 202 us (1.15)
  Pallas kernels: 0 us -> 26.7 us
  matrix products: 24 us -> 4.4 us
  waiting for transfers between devices: 60.1 us -> 78.6 us
  starting transfers between devices: 56.4 us -> 47.2 us
  other arithmetic: 3.54 us -> 8.1 us
  blocking collectives: 19.2 us -> 23.6 us
    pallas_call x0 -> x4, Pallas kernels: none -> 26.7 us  [the longest x2 14 us: upper_product(): pl.pallas_call(kernel, out_shape=[jax.ShapeDtypeStruct((size, width + ext...]
    dot_general x10 -> x3, matrix products: 23.4 us -> 3.8 us  [times_t(): lax.dot_general(left, right, (((1,), (1,)), ((), ())), preferred_element_...]
    ppermute x12 -> x15, waiting for transfers between devices: 15.7 us -> 25.4 us  [shift_mp(): lax.ppermute(block, 'mp', [(i, (i + distance) % count) for i in range(cou...]
    all_to_all x2, waiting for transfers between devices: 28.9 us -> 34.1 us  [scatter_sum_dp(): got = lax.all_to_all(partial, 'dp', 0, 0, tiled=True)]
    ppermute x10, starting transfers between devices: 15.8 us -> 11 us  [swap_sections(): return lax.ppermute(block, 'section', [(0, 1), (1, 0)])]
    all_to_all x1, blocking collectives: 19.2 us -> 23.6 us  [gather_dp(): got = lax.all_to_all(copies, 'dp', 0, 0, tiled=True)]
    all_to_all x2, waiting for transfers between devices: 13.8 us -> 17.9 us  [gather_dp(): got = lax.all_to_all(copies, 'dp', 0, 0, tiled=True)]
    concatenate x2 -> x0, local copies, waits for them, and re-layouts: 3.79 us -> none  [body(): jnp.concatenate([times_t(middle_all, of_section(weight_low, section)).ast...]
  transfers between devices with their start and end apart: 26 -> 29, of which waited for: 13 -> 16; matrix products, arithmetic and copies ran while one was open for 9% -> 8% of each run, Pallas kernels for 0% -> 7%
where the time goes in v2:
time: 202 us; the launch traced here: 201 us
  waiting for transfers between devices  78.6 us (39%)
  starting transfers between devices  47.2 us (23%)
  Pallas kernels  26.7 us (13%)
  blocking collectives  23.6 us (12%)
  local copies, waits for them, and re-layouts  11 us (5%)
  other arithmetic  8.1 us (4%)
  matrix products  4.4 us (2%)
    all_to_all x2, waiting for transfers between devices, scatter_sum_dp(): got = lax.all_to_all(partial, 'dp', 0, 0, tiled=True)  34.1 us
    ppermute x15, waiting for transfers between devices, shift_mp(): lax.ppermute(block, 'mp', [(i, (i + distance) % count) for i in range(cou...  25.4 us
    all_to_all x1, blocking collectives, gather_dp(): got = lax.all_to_all(copies, 'dp', 0, 0, tiled=True)  23.6 us
    all_to_all x2, waiting for transfers between devices, gather_dp(): got = lax.all_to_all(copies, 'dp', 0, 0, tiled=True)  17.9 us
    ppermute x15, starting transfers between devices, shift_mp(): lax.ppermute(block, 'mp', [(i, (i + distance) % count) for i in range(cou...  17.6 us
    pallas_call x2, Pallas kernels, upper_product(): pl.pallas_call(kernel, out_shape=[jax.ShapeDtypeStruct((size, width + ext...  14 us
    pallas_call x2, Pallas kernels, lower_product(): pl.pallas_call(kernel, out_shape=[jax.ShapeDtypeStruct((tokens, width + e...  12.7 us
    all_to_all x2, starting transfers between devices, gather_dp(): got = lax.all_to_all(copies, 'dp', 0, 0, tiled=True)  11.2 us
  transfers between devices with their start and end apart: 29, of which 16 were waited for; matrix products, arithmetic and copies ran while one was open for 8% of the time, Pallas kernels for 7%

profile of v2, /device:TPU:1, one launch (start us, length us, event | category | flops | bytes accessed | tf_op | source)
XLA Modules:
  0.0 200.7 jit_solution(15562809312706355916)
XLA Ops:
  3.1 23.6 %all_to_all.33 = bf16[16,16,2048]{2,1,0:T(8,128)(2,1)} all-to-all(bf16[16,16,2048]{2,1,0:T(8,128)(2,1)S(1)} %broadcast_in_dim.76), channel_id=1, replica_groups=mesh['section'=2,'dp'=16,'mp'=4] {'dp'}, dimensions={0} | all-to-all | bytes 2097152 | tf_op jit(solution)/shard_map/all_to_all | solution.py:32
  28.2 3.3 %fusion.2 = bf16[512,64]{0,1:T(8,128)(2,1)S(1)} fusion(bf16[1,512,3584]{2,1,0:T(8,128)(2,1)} %param.16, bf16[1,64,3584]{2,1,0:T(8,128)(2,1)} %param.20), kind=kOutput, calls=%fused_computation.4 | convolution fusion | flops 234913792 | bytes 4194304 | tf_op jit(solution)/shard_map/dot_general | solution.py:13
  36.3 7.1 %upper_product.2 = (bf16[64,1024]{1,0:T(8,128)(2,1)}, bf16[64,1024]{1,0:T(8,128)(2,1)}, bf16[64,1024]{1,0:T(8,128)(2,1)}, bf16[64,1024]{1,0:T(8,128)(2,1)}) custom-call(s32[2]{0:T(128)} %pad_add_fusion.1.place_ref, bf16[256,2048]{1,0:T(8,128)(2,1)} %bitcast.110, bf16[896,2048]{1,0:T(8,128)(2,1)} %bitcast.102, ...), custom_call_target="tpu_custom_call" | custom-call | tf_op jit(solution)/shard_map/up_1/upper_product/pallas_call | solution.py:89
  45.0 3.3 %collective-permute-start.4 = (bf16[64,1024]{1,0:T(8,128)(2,1)}, bf16[64,1024]{1,0:T(8,128)(2,1)S(1)}, u32[]{:S(2)}, u32[]{:S(2)}) collective-permute-start(bf16[64,1024]{1,0:T(8,128)(2,1)} %get-tuple-element.21), channel_id=1, source_target_pairs={{0,2},{1,3},{2,0},{3,1},{4,6},{5,7},{6,4},{7,5},{8,10},{9,11},{10,... | collective-permute-start | bytes 393224 | tf_op jit(solution)/shard_map/up_1/ppermute | solution.py:24
  51.8 3.3 %collective-permute-done.4 = bf16[64,1024]{1,0:T(8,128)(2,1)S(1)} collective-permute-done((bf16[64,1024]{1,0:T(8,128)(2,1)}, bf16[64,1024]{1,0:T(8,128)(2,1)S(1)}, u32[]{:S(2)}, u32[]{:S(2)}) %collective-permute-start.4) | collective-permute-done | bytes 131104 | tf_op jit(solution)/shard_map/up_1/ppermute | solution.py:24
  61.4 2.7 %collective-permute-done.8.refs_2_ = bf16[64,1024]{1,0:T(8,128)(2,1)S(1)} collective-permute-done((bf16[64,1024]{1,0:T(8,128)(2,1)S(1)}, bf16[64,1024]{1,0:T(8,128)(2,1)S(1)}, u32[]{:S(2)}, u32[]{:S(2)}) %collective-permute-start.8) | collective-permute-done | bytes 131104 | tf_op jit(solution)/shard_map/up_1/ppermute | solution.py:24
  64.1 3.8 %collective-permute-done.7.refs_1_ = bf16[64,1024]{1,0:T(8,128)(2,1)S(1)} collective-permute-done((bf16[64,1024]{1,0:T(8,128)(2,1)S(1)}, bf16[64,1024]{1,0:T(8,128)(2,1)S(1)}, u32[]{:S(2)}, u32[]{:S(2)}) %collective-permute-start.7) | collective-permute-done | bytes 131104 | tf_op jit(solution)/shard_map/up_1/ppermute | solution.py:24
  68.6 6.7 %lower_product.2 = (bf16[256,2304]{1,0:T(8,128)(2,1)}, bf16[256,128]{1,0:T(8,128)(2,1)}) custom-call(s32[2]{0:T(128)} %pad_add_fusion.1.place_ref, bf16[64,1024]{1,0:T(8,128)(2,1)} %copy-done.2, bf16[64,1024]{1,0:T(8,128)(2,1)} %copy-done.13, bf16[64,1024]{1,0:T(8,128)(2,1)} %copy-done.12, bf16[64,1024]{1,0:T(8,128)(2,1)} %copy-done.11, ...), custom_call_target="tpu_custom_call" | custom-call | tf_op jit(solution)/shard_map/low_1/lower_product/pallas_call | solution.py:160
  75.3 3.7 %all-to-all-start.1 = ((bf16[16,16,2304]{2,1,0:T(8,128)(2,1)}), bf16[16,16,2304]{2,1,0:T(8,128)(2,1)S(1)}, u32[]{:S(2)}, u32[]{:S(2)}) async-start(bf16[16,16,2304]{2,1,0:T(8,128)(2,1)} %bitcast.111), calls=%async_computation.1 | async-start | bytes 2359296 | tf_op jit(solution)/shard_map/low_1/all_to_all | solution.py:38
  79.7 17.2 %all-to-all-done.1 = bf16[16,16,2304]{2,1,0:T(8,128)(2,1)S(1)} async-done(((bf16[16,16,2304]{2,1,0:T(8,128)(2,1)}), bf16[16,16,2304]{2,1,0:T(8,128)(2,1)S(1)}, u32[]{:S(2)}, u32[]{:S(2)}) %all-to-all-start.1) | async-done | bytes 1179680 | tf_op jit(solution)/shard_map/low_1/all_to_all | solution.py:38
  98.3 4.8 %all-to-all-start.2 = ((bf16[16,16,2304]{2,1,0:T(8,128)(2,1)}), bf16[16,16,2304]{2,1,0:T(8,128)(2,1)S(1)}, u32[]{:S(2)}, u32[]{:S(2)}) async-start(bf16[16,16,2304]{2,1,0:T(8,128)(2,1)} %broadcast_in_dim.77), calls=%async_computation.2 | async-start | bytes 2359296 | tf_op jit(solution)/shard_map/low_1/all_to_all | solution.py:32
  105.1 15.1 %all-to-all-done.2 = bf16[16,16,2304]{2,1,0:T(8,128)(2,1)S(1)} async-done(((bf16[16,16,2304]{2,1,0:T(8,128)(2,1)}), bf16[16,16,2304]{2,1,0:T(8,128)(2,1)S(1)}, u32[]{:S(2)}, u32[]{:S(2)}) %all-to-all-start.2) | async-done | bytes 1179680 | tf_op jit(solution)/shard_map/low_1/all_to_all | solution.py:32
  121.3 6.9 %upper_product.3 = (bf16[64,1024]{1,0:T(8,128)(2,1)}, bf16[64,1024]{1,0:T(8,128)(2,1)}, bf16[64,1024]{1,0:T(8,128)(2,1)}, bf16[64,1024]{1,0:T(8,128)(2,1)}) custom-call(s32[2]{0:T(128)} %pad_add_fusion.place_ref, bf16[256,2048]{1,0:T(8,128)(2,1)} %slice.65.x_ref, bf16[896,2048]{1,0:T(8,128)(2,1)} %bitcast.103, ...), custom_call_target="tpu_custom_call" | custom-call | tf_op jit(solution)/shard_map/up_0/upper_product/pallas_call | solution.py:89
  130.9 3.6 %collective-permute-done.14 = bf16[64,1024]{1,0:T(8,128)(2,1)S(1)} collective-permute-done((bf16[64,1024]{1,0:T(8,128)(2,1)}, bf16[64,1024]{1,0:T(8,128)(2,1)S(1)}, u32[]{:S(2)}, u32[]{:S(2)}) %collective-permute-start.14) | collective-permute-done | bytes 131104 | tf_op jit(solution)/shard_map/up_0/ppermute | solution.py:24
  137.6 6.4 %all-to-all-start.4 = ((bf16[16,2,2048]{2,1,0:T(2,128)(2,1)}), bf16[16,2,2048]{2,1,0:T(2,128)(2,1)S(1)}, u32[]{:S(2)}, u32[]{:S(2)}) async-start(bf16[16,2,2048]{2,1,0:T(2,128)(2,1)} %reshape.282), calls=%async_computation.4 | async-start | bytes 262144 | tf_op jit(solution)/shard_map/low_0/all_to_all | solution.py:32
  144.4 3.0 %collective-permute-start.19 = (bf16[64,1024]{1,0:T(8,128)(2,1)S(1)}, bf16[64,1024]{1,0:T(8,128)(2,1)S(1)}, u32[]{:S(2)}, u32[]{:S(2)}) collective-permute-start(bf16[64,1024]{1,0:T(8,128)(2,1)S(1)} %pad_maximum_fusion.2.refs_0_), channel_id=1, source_target_pairs={{0,3},{1,0},{2,1},{3,2},{4,7},{5,4},{6,5},{7,6},{8,11},{9,8},{10,9... | collective-permute-start | bytes 393224 | tf_op jit(solution)/shard_map/up_0/ppermute | solution.py:24
  148.0 2.8 %all-to-all-done.4 = bf16[16,2,2048]{2,1,0:T(2,128)(2,1)S(1)} async-done(((bf16[16,2,2048]{2,1,0:T(2,128)(2,1)}), bf16[16,2,2048]{2,1,0:T(2,128)(2,1)S(1)}, u32[]{:S(2)}, u32[]{:S(2)}) %all-to-all-start.4) | async-done | bytes 131104 | tf_op jit(solution)/shard_map/low_0/all_to_all | solution.py:32
  151.1 2.8 %collective-permute-start.23 = (bf16[64,64]{1,0:T(8,128)(2,1)S(1)}, bf16[64,64]{1,0:T(8,128)(2,1)S(1)}, u32[]{:S(2)}, u32[]{:S(2)}) collective-permute-start(bf16[64,64]{1,0:T(8,128)(2,1)S(1)} %reduce_sum.42), channel_id=1, source_target_pairs={{0,3},{1,0},{2,1},{3,2},{4,7},{5,4},{6,5},{7,6},{8,11},{9,8},{10,9... | collective-permute-start | bytes 24584 | tf_op jit(solution)/shard_map/low_0/ppermute | solution.py:24
  154.0 3.8 %collective-permute-done.21 = bf16[64,64]{1,0:T(8,128)(2,1)S(1)} collective-permute-done((bf16[64,64]{1,0:T(8,128)(2,1)S(1)}, bf16[64,64]{1,0:T(8,128)(2,1)S(1)}, u32[]{:S(2)}, u32[]{:S(2)}) %collective-permute-start.21) | collective-permute-done | bytes 8224 | tf_op jit(solution)/shard_map/low_0/ppermute | solution.py:24
  157.8 4.1 %collective-permute-done.22 = bf16[64,64]{1,0:T(8,128)(2,1)S(1)} collective-permute-done((bf16[64,64]{1,0:T(8,128)(2,1)S(1)}, bf16[64,64]{1,0:T(8,128)(2,1)S(1)}, u32[]{:S(2)}, u32[]{:S(2)}) %collective-permute-start.22) | collective-permute-done | bytes 8224 | tf_op jit(solution)/shard_map/low_0/ppermute | solution.py:24
  163.3 6.0 %lower_product.3 = (bf16[256,2048]{1,0:T(8,128)(2,1)}, bf16[256,128]{1,0:T(8,128)(2,1)}) custom-call(s32[2]{0:T(128)} %pad_add_fusion.place_ref, bf16[64,1024]{1,0:T(8,128)(2,1)} %copy-done.1, bf16[64,1024]{1,0:T(8,128)(2,1)} %copy-done.10, bf16[64,1024]{1,0:T(8,128)(2,1)} %copy-done.9, bf16[64,1024]{1,0:T(8,128)(2,1)} %copy-done.8, ...), custom_call_target="tpu_custom_call" | custom-call | tf_op jit(solution)/shard_map/low_0/lower_product/pallas_call | solution.py:160
  170.3 4.9 %collective-permute-start.24 = (bf16[256,256]{1,0:T(8,128)(2,1)S(1)}, bf16[256,256]{1,0:T(8,128)(2,1)S(1)}, u32[]{:S(2)}, u32[]{:S(2)}) collective-permute-start(bf16[256,256]{1,0:T(8,128)(2,1)S(1)} %maximum_select_fusion.1), channel_id=1, source_target_pairs={{0,64},{64,0},{1,65},{65,1},{2,66},{66,2},{3,67},{67,3},{4,68},{68... | collective-permute-start | bytes 393224 | tf_op jit(solution)/shard_map/outputs/ppermute | solution.py:19
  175.3 3.7 %all-to-all-start.3 = ((bf16[16,16,2048]{2,1,0:T(8,128)(2,1)}), bf16[16,16,2048]{2,1,0:T(8,128)(2,1)S(1)}, u32[]{:S(2)}, u32[]{:S(2)}) async-start(bf16[16,16,2048]{2,1,0:T(8,128)(2,1)} %bitcast.112), calls=%async_computation.3 | async-start | bytes 2097152 | tf_op jit(solution)/shard_map/low_0/all_to_all | solution.py:38
  181.1 16.9 %all-to-all-done.3 = bf16[16,16,2048]{2,1,0:T(8,128)(2,1)S(1)} async-done(((bf16[16,16,2048]{2,1,0:T(8,128)(2,1)}), bf16[16,16,2048]{2,1,0:T(8,128)(2,1)S(1)}, u32[]{:S(2)}, u32[]{:S(2)}) %all-to-all-start.3) | async-done | bytes 1048608 | tf_op jit(solution)/shard_map/low_0/all_to_all | solution.py:38
  (138 shorter events, 40.2 us)
Async XLA Ops:
  0.6 35.7 %collective-permute-start = (bf16[896,2048]{1,0:T(8,128)(2,1)}, bf16[896,2048]{1,0:T(8,128)(2,1)}, u32[]{:S(2)}, u32[]{:S(2)}) collective-permute-start(bf16[896,2048]{1,0:T(8,128)(2,1)} %bitcast.101), channel_id=1, source_target_pairs={{0,64},{64,0},{1,65},{65,1},{2,66},{66,2},{3,67},{67,3},{4,68},{68... | collective-permute-start | bytes 11010056 | tf_op jit(solution)/shard_map/ppermute | solution.py:19
  26.7 41.2 %collective-permute-start.10 = (bf16[2048,896]{1,0:T(8,128)(2,1)}, bf16[2048,896]{1,0:T(8,128)(2,1)}, u32[]{:S(2)}, u32[]{:S(2)}) collective-permute-start(bf16[2048,896]{1,0:T(8,128)(2,1)} %bitcast.104), channel_id=1, source_target_pairs={{0,64},{64,0},{1,65},{65,1},{2,66},{66,2},{3,67},{67,3},{4,68},{68... | collective-permute-start | bytes 11010056 | tf_op jit(solution)/shard_map/ppermute | solution.py:19
  32.1 16.2 %collective-permute-start.12 = (bf16[256,64]{1,0:T(8,128)(2,1)S(1)}, bf16[256,64]{1,0:T(8,128)(2,1)S(1)}, u32[]{:S(2)}, u32[]{:S(2)}) collective-permute-start(bf16[256,64]{1,0:T(8,128)(2,1)S(1)} %bitcast.134), channel_id=1, source_target_pairs={{0,64},{64,0},{1,65},{65,1},{2,66},{66,2},{3,67},{67,3},{4,68},{68... | collective-permute-start | bytes 98312 | tf_op jit(solution)/shard_map/ppermute | solution.py:19
  34.4 21.7 %collective-permute-start.6 = (bf16[64,896]{1,0:T(8,128)(2,1)S(1)}, bf16[64,896]{1,0:T(8,128)(2,1)S(1)}, u32[]{:S(2)}, u32[]{:S(2)}) collective-permute-start(bf16[64,896]{1,0:T(8,128)(2,1)S(1)} %bitcast.133), channel_id=1, source_target_pairs={{0,64},{64,0},{1,65},{65,1},{2,66},{66,2},{3,67},{67,3},{4,68},{68... | collective-permute-start | bytes 344072 | tf_op jit(solution)/shard_map/ppermute | solution.py:19
  43.4 7.9 %collective-permute-start.3 = (bf16[64,1024]{1,0:T(8,128)(2,1)}, bf16[64,1024]{1,0:T(8,128)(2,1)S(1)}, u32[]{:S(2)}, u32[]{:S(2)}) collective-permute-start(bf16[64,1024]{1,0:T(8,128)(2,1)} %get-tuple-element.20), channel_id=1, source_target_pairs={{0,1},{1,2},{2,3},{3,0},{4,5},{5,6},{6,7},{7,4},{8,9},{9,10},{10,1... | collective-permute-start | bytes 393224 | tf_op jit(solution)/shard_map/up_1/ppermute | solution.py:24
  45.0 10.1 %collective-permute-start.4 = (bf16[64,1024]{1,0:T(8,128)(2,1)}, bf16[64,1024]{1,0:T(8,128)(2,1)S(1)}, u32[]{:S(2)}, u32[]{:S(2)}) collective-permute-start(bf16[64,1024]{1,0:T(8,128)(2,1)} %get-tuple-element.21), channel_id=1, source_target_pairs={{0,2},{1,3},{2,0},{3,1},{4,6},{5,7},{6,4},{7,5},{8,10},{9,11},{10,... | collective-permute-start | bytes 393224 | tf_op jit(solution)/shard_map/up_1/ppermute | solution.py:24
  48.3 6.8 %collective-permute-start.5 = (bf16[64,1024]{1,0:T(8,128)(2,1)}, bf16[64,1024]{1,0:T(8,128)(2,1)S(1)}, u32[]{:S(2)}, u32[]{:S(2)}) collective-permute-start(bf16[64,1024]{1,0:T(8,128)(2,1)} %get-tuple-element.22), channel_id=1, source_target_pairs={{0,3},{1,0},{2,1},{3,2},{4,7},{5,4},{6,5},{7,6},{8,11},{9,8},{10,9... | collective-permute-start | bytes 393224 | tf_op jit(solution)/shard_map/up_1/ppermute | solution.py:24
  51.3 7.7 %collective-permute-start.11 = (bf16[64,896]{1,0:T(8,128)(2,1)S(1)}, bf16[64,896]{1,0:T(8,128)(2,1)S(1)}, u32[]{:S(2)}, u32[]{:S(2)}) collective-permute-start(bf16[64,896]{1,0:T(8,128)(2,1)S(1)} %bitcast.121), channel_id=1, source_target_pairs={{0,64},{64,0},{1,65},{65,1},{2,66},{66,2},{3,67},{67,3},{4,68},{68... | collective-permute-start | bytes 344072 | tf_op jit(solution)/shard_map/ppermute | solution.py:19
  56.2 5.2 %collective-permute-start.9 = (bf16[64,1024]{1,0:T(8,128)(2,1)S(1)}, bf16[64,1024]{1,0:T(8,128)(2,1)S(1)}, u32[]{:S(2)}, u32[]{:S(2)}) collective-permute-start(bf16[64,1024]{1,0:T(8,128)(2,1)S(1)} %pad_maximum_fusion.1.refs_0_), channel_id=1, source_target_pairs={{0,3},{1,0},{2,1},{3,2},{4,7},{5,4},{6,5},{7,6},{8,11},{9,8},{10,9... | collective-permute-start | bytes 393224 | tf_op jit(solution)/shard_map/up_1/ppermute | solution.py:24
  58.3 5.8 %collective-permute-start.8 = (bf16[64,1024]{1,0:T(8,128)(2,1)S(1)}, bf16[64,1024]{1,0:T(8,128)(2,1)S(1)}, u32[]{:S(2)}, u32[]{:S(2)}) collective-permute-start(bf16[64,1024]{1,0:T(8,128)(2,1)S(1)} %pad_maximum_fusion.1.refs_0_), channel_id=1, source_target_pairs={{0,2},{1,3},{2,0},{3,1},{4,6},{5,7},{6,4},{7,5},{8,10},{9,11},{10,... | collective-permute-start | bytes 393224 | tf_op jit(solution)/shard_map/up_1/ppermute | solution.py:24
  58.9 9.0 %collective-permute-start.7 = (bf16[64,1024]{1,0:T(8,128)(2,1)S(1)}, bf16[64,1024]{1,0:T(8,128)(2,1)S(1)}, u32[]{:S(2)}, u32[]{:S(2)}) collective-permute-start(bf16[64,1024]{1,0:T(8,128)(2,1)S(1)} %pad_maximum_fusion.1.refs_0_), channel_id=1, source_target_pairs={{0,1},{1,2},{2,3},{3,0},{4,5},{5,6},{6,7},{7,4},{8,9},{9,10},{10,1... | collective-permute-start | bytes 393224 | tf_op jit(solution)/shard_map/up_1/ppermute | solution.py:24
  75.3 21.6 %all-to-all-start.1 = ((bf16[16,16,2304]{2,1,0:T(8,128)(2,1)}), bf16[16,16,2304]{2,1,0:T(8,128)(2,1)S(1)}, u32[]{:S(2)}, u32[]{:S(2)}) async-start(bf16[16,16,2304]{2,1,0:T(8,128)(2,1)} %bitcast.111), calls=%async_computation.1 | async-start | bytes 2359296 | tf_op jit(solution)/shard_map/low_1/all_to_all | solution.py:38
  79.0 18.1 %collective-permute-start.13 = (bf16[16,2048]{1,0:T(8,128)(2,1)S(1)}, bf16[16,2048]{1,0:T(8,128)(2,1)S(1)}, u32[]{:S(2)}, u32[]{:S(2)}) collective-permute-start(bf16[16,2048]{1,0:T(8,128)(2,1)S(1)} %dynamic-slice_bitcast_fusion), channel_id=1, source_target_pairs={{0,64},{64,0},{1,65},{65,1},{2,66},{66,2},{3,67},{67,3},{4,68},{68... | collective-permute-start | bytes 196616 | tf_op jit(solution)/shard_map/ppermute | solution.py:19
  98.3 21.8 %all-to-all-start.2 = ((bf16[16,16,2304]{2,1,0:T(8,128)(2,1)}), bf16[16,16,2304]{2,1,0:T(8,128)(2,1)S(1)}, u32[]{:S(2)}, u32[]{:S(2)}) async-start(bf16[16,16,2304]{2,1,0:T(8,128)(2,1)} %broadcast_in_dim.77), calls=%async_computation.2 | async-start | bytes 2359296 | tf_op jit(solution)/shard_map/low_1/all_to_all | solution.py:32
  128.2 6.3 %collective-permute-start.14 = (bf16[64,1024]{1,0:T(8,128)(2,1)}, bf16[64,1024]{1,0:T(8,128)(2,1)S(1)}, u32[]{:S(2)}, u32[]{:S(2)}) collective-permute-start(bf16[64,1024]{1,0:T(8,128)(2,1)} %get-tuple-element.28), channel_id=1, source_target_pairs={{0,1},{1,2},{2,3},{3,0},{4,5},{5,6},{6,7},{7,4},{8,9},{9,10},{10,1... | collective-permute-start | bytes 393224 | tf_op jit(solution)/shard_map/up_0/ppermute | solution.py:24
  128.2 6.9 %collective-permute-start.15 = (bf16[64,1024]{1,0:T(8,128)(2,1)}, bf16[64,1024]{1,0:T(8,128)(2,1)S(1)}, u32[]{:S(2)}, u32[]{:S(2)}) collective-permute-start(bf16[64,1024]{1,0:T(8,128)(2,1)} %get-tuple-element.29), channel_id=1, source_target_pairs={{0,2},{1,3},{2,0},{3,1},{4,6},{5,7},{6,4},{7,5},{8,10},{9,11},{10,... | collective-permute-start | bytes 393224 | tf_op jit(solution)/shard_map/up_0/ppermute | solution.py:24
  128.3 7.2 %collective-permute-start.16 = (bf16[64,1024]{1,0:T(8,128)(2,1)}, bf16[64,1024]{1,0:T(8,128)(2,1)S(1)}, u32[]{:S(2)}, u32[]{:S(2)}) collective-permute-start(bf16[64,1024]{1,0:T(8,128)(2,1)} %get-tuple-element.30), channel_id=1, source_target_pairs={{0,3},{1,0},{2,1},{3,2},{4,7},{5,4},{6,5},{7,6},{8,11},{9,8},{10,9... | collective-permute-start | bytes 393224 | tf_op jit(solution)/shard_map/up_0/ppermute | solution.py:24
  137.6 13.2 %all-to-all-start.4 = ((bf16[16,2,2048]{2,1,0:T(2,128)(2,1)}), bf16[16,2,2048]{2,1,0:T(2,128)(2,1)S(1)}, u32[]{:S(2)}, u32[]{:S(2)}) async-start(bf16[16,2,2048]{2,1,0:T(2,128)(2,1)} %reshape.282), calls=%async_computation.4 | async-start | bytes 262144 | tf_op jit(solution)/shard_map/low_0/all_to_all | solution.py:32
  144.4 17.5 %collective-permute-start.19 = (bf16[64,1024]{1,0:T(8,128)(2,1)S(1)}, bf16[64,1024]{1,0:T(8,128)(2,1)S(1)}, u32[]{:S(2)}, u32[]{:S(2)}) collective-permute-start(bf16[64,1024]{1,0:T(8,128)(2,1)S(1)} %pad_maximum_fusion.2.refs_0_), channel_id=1, source_target_pairs={{0,3},{1,0},{2,1},{3,2},{4,7},{5,4},{6,5},{7,6},{8,11},{9,8},{10,9... | collective-permute-start | bytes 393224 | tf_op jit(solution)/shard_map/up_0/ppermute | solution.py:24
  147.4 14.5 %collective-permute-start.18 = (bf16[64,1024]{1,0:T(8,128)(2,1)S(1)}, bf16[64,1024]{1,0:T(8,128)(2,1)S(1)}, u32[]{:S(2)}, u32[]{:S(2)}) collective-permute-start(bf16[64,1024]{1,0:T(8,128)(2,1)S(1)} %pad_maximum_fusion.2.refs_0_), channel_id=1, source_target_pairs={{0,2},{1,3},{2,0},{3,1},{4,6},{5,7},{6,4},{7,5},{8,10},{9,11},{10,... | collective-permute-start | bytes 393224 | tf_op jit(solution)/shard_map/up_0/ppermute | solution.py:24
  147.4 14.6 %collective-permute-start.17 = (bf16[64,1024]{1,0:T(8,128)(2,1)S(1)}, bf16[64,1024]{1,0:T(8,128)(2,1)S(1)}, u32[]{:S(2)}, u32[]{:S(2)}) collective-permute-start(bf16[64,1024]{1,0:T(8,128)(2,1)S(1)} %pad_maximum_fusion.2.refs_0_), channel_id=1, source_target_pairs={{0,1},{1,2},{2,3},{3,0},{4,5},{5,6},{6,7},{7,4},{8,9},{9,10},{10,1... | collective-permute-start | bytes 393224 | tf_op jit(solution)/shard_map/up_0/ppermute | solution.py:24
  151.1 18.2 %collective-permute-start.23 = (bf16[64,64]{1,0:T(8,128)(2,1)S(1)}, bf16[64,64]{1,0:T(8,128)(2,1)S(1)}, u32[]{:S(2)}, u32[]{:S(2)}) collective-permute-start(bf16[64,64]{1,0:T(8,128)(2,1)S(1)} %reduce_sum.42), channel_id=1, source_target_pairs={{0,3},{1,0},{2,1},{3,2},{4,7},{5,4},{6,5},{7,6},{8,11},{9,8},{10,9... | collective-permute-start | bytes 24584 | tf_op jit(solution)/shard_map/low_0/ppermute | solution.py:24
  170.3 8.7 %collective-permute-start.24 = (bf16[256,256]{1,0:T(8,128)(2,1)S(1)}, bf16[256,256]{1,0:T(8,128)(2,1)S(1)}, u32[]{:S(2)}, u32[]{:S(2)}) collective-permute-start(bf16[256,256]{1,0:T(8,128)(2,1)S(1)} %maximum_select_fusion.1), channel_id=1, source_target_pairs={{0,64},{64,0},{1,65},{65,1},{2,66},{66,2},{3,67},{67,3},{4,68},{68... | collective-permute-start | bytes 393224 | tf_op jit(solution)/shard_map/outputs/ppermute | solution.py:19
  175.3 22.8 %all-to-all-start.3 = ((bf16[16,16,2048]{2,1,0:T(8,128)(2,1)}), bf16[16,16,2048]{2,1,0:T(8,128)(2,1)S(1)}, u32[]{:S(2)}, u32[]{:S(2)}) async-start(bf16[16,16,2048]{2,1,0:T(8,128)(2,1)} %bitcast.112), calls=%async_computation.3 | async-start | bytes 2097152 | tf_op jit(solution)/shard_map/low_0/all_to_all | solution.py:38
  (22 other events, 253.4 us)

commit v3 on v1

--- a/solution.py
+++ b/solution.py
@@ -38,6 +38,11 @@
     return jnp.sum(got.astype(F32), axis=0)
 
 
+def from_all_mp(block):
+    count = lax.axis_size("mp")
+    return [block] + [shift_mp(block, distance) for distance in range(1, count)]
+
+
 def scatter_sum_mp(partial):
     count = lax.axis_size("mp")
     mine = lax.axis_index("mp")
@@ -59,9 +64,7 @@
     mine = lax.axis_index("mp")
     rows = block.shape[0]
     whole = jnp.zeros((count * rows, block.shape[1]), block.dtype)
-    whole = lax.dynamic_update_slice_in_dim(whole, block, mine * rows, 0)
-    for distance in range(1, count):
-        got = shift_mp(block, distance)
+    for distance, got in enumerate(from_all_mp(block)):
         whole = lax.dynamic_update_slice_in_dim(
             whole, got, ((mine - distance) % count) * rows, 0
         )
@@ -102,72 +105,114 @@
         shape = (array.shape[0] // sections, array.shape[1])
         return mine.reshape(shape), other.reshape(shape)
 
-    def exchanged(array):
-        mine, other = halves(array)
-        return mine, swap_sections(other)
+    def swapped(*arrays):
+        got = swap_sections(jnp.concatenate(arrays, axis=0))
+        cuts = []
+        for array in arrays[:-1]:
+            cuts.append((cuts[-1] if cuts else 0) + array.shape[0])
+        return jnp.split(got, cuts, axis=0)
 
     def of_section(pair, section):
         own, received = pair
         return jnp.where(core == section, own, received)
 
+    def held(*arrays):
+        return lax.optimization_barrier(arrays)
+
+    dp_index = lax.axis_index("dp")
+    mp_index = lax.axis_index("mp")
+    tokens_mp = upper_deriv.shape[1]
+
     grad, _ = halves(out_grad)
-    first = gather_dp(grad)
-
+    gathered = gather_dp(grad)
+
+    deriv_up, deriv_up_sent = halves(upper_deriv[0])
+    deriv_low, deriv_low_sent = halves(lower_deriv[0])
+    left_up, left_up_sent = halves(
+        times_t(
+            lax.dynamic_slice_in_dim(upper_in[0], dp_index * tokens_dp, tokens_dp, 0),
+            proj_upper_in[0],
+        ).astype(BF16)
+    )
+    left_low, left_low_sent = halves(
+        times_t(
+            lax.dynamic_slice_in_dim(lower_in[0], mp_index * tokens_mp, tokens_mp, 0),
+            proj_lower_in[0],
+        ).astype(BF16)
+    )
     weight_up = (upper_w[0], swap_sections(upper_w[0]))
-    pout_up = (proj_upper_out[0], swap_sections(proj_upper_out[0]))
-    factor_up = exchanged(times_t(upper_in[0], proj_upper_in[0]).astype(BF16))
-    deriv_up = exchanged(upper_deriv[0])
+    got = swapped(proj_upper_out[0], deriv_low_sent)
+    pout_up = (proj_upper_out[0], got[0])
+    deriv_low = (deriv_low, got[1])
+    got = swapped(left_up_sent, left_low_sent)
+    left_up = (left_up, got[0])
+    left_low = (left_low, got[1])
+    got = swapped(proj_lower_out[0], deriv_up_sent)
+    pout_low = (proj_lower_out[0], got[0])
+    deriv_up = (deriv_up, got[1])
     weight_low = (lower_w[0], swap_sections(lower_w[0]))
-    pout_low = (proj_lower_out[0], swap_sections(proj_lower_out[0]))
-    factor_low = exchanged(times_t(lower_in[0], proj_lower_in[0]).astype(BF16))
-    deriv_low = exchanged(lower_deriv[0])
-
-    gathered = first
+
+    last = sections - 1
     grads = [None] * sections
-    ups = [None] * sections
-    lows = [None] * sections
-    for section in range(sections - 1, -1, -1):
+    ups = []
+    lows = []
+    for section in range(last, -1, -1):
         with jax.named_scope(f"up_{section}"):
-            partial = jnp.concatenate(
-                [
-                    times_t(gathered, of_section(weight_up, section)).astype(BF16),
-                    of_section(factor_up, section),
-                    times_t(gathered, of_section(pout_up, section)).astype(BF16),
-                ],
-                axis=1,
-            )
-            summed = scatter_sum_mp(partial)
+            up = [times_t(grad, of_section(pout_up, section)).astype(BF16)]
+            if section == last:
+                up += [of_section(left_up, s) for s in range(last, -1, -1)]
+            up = from_all_mp(jnp.concatenate(up, axis=1))
+            up = sum(part.astype(F32) for part in up).astype(BF16)
+            weight = of_section(weight_up, section)
+            summed = scatter_sum_mp(times_t(gathered, weight).astype(BF16))
             scale = of_section(deriv_up, section).astype(F32)
-            middle = (summed[:, :hidden] * scale).astype(BF16)
-            block = jnp.concatenate([middle, summed[:, hidden:].astype(BF16)], axis=1)
-            whole = gather_mp(block)
-            middle_all = whole[:, :hidden]
-            ups[section] = whole[:, hidden:]
+            middle = (summed * scale).astype(BF16)
         with jax.named_scope(f"low_{section}"):
-            partial = jnp.concatenate(
-                [
-                    times_t(middle_all, of_section(weight_low, section)).astype(BF16),
-                    of_section(factor_low, section),
-                    times_t(middle_all, of_section(pout_low, section)).astype(BF16),
-                ],
-                axis=1,
-            )
+            low = [times_t(middle, of_section(pout_low, section)).astype(BF16)]
+            if section == last:
+                low += [of_section(left_low, s) for s in range(last, -1, -1)]
+            ups.append(up)
+            lows += low
+            if section == 0:
+                low = jnp.concatenate(lows, axis=1)
+                up = jnp.concatenate(ups, axis=1)
+                rows = low.shape[0]
+                both = gather_dp(jnp.concatenate([low, up], axis=0))
+                both = both.reshape(dp_count, rows + up.shape[0], up.shape[1])
+                low = jnp.sum(both[:, :rows].astype(F32), axis=0).astype(BF16)
+                up = both[:, rows:].reshape(tokens // sections, up.shape[1])
+
+            middle_all = gather_mp(middle)
+            weight = of_section(weight_low, section)
+            partial = times_t(middle_all, weight).astype(BF16)
+            if section == 0:
+                low, up, partial = held(low, up, partial)
             summed = scatter_sum_dp(partial)
             scale = of_section(deriv_low, section).astype(F32)
-            grad = (summed[:, :width] * scale).astype(BF16)
+            grad = (summed * scale).astype(BF16)
             grads[section] = grad
-            low = summed[:, width:].astype(BF16)
             if section > 0:
-                got = gather_dp(jnp.concatenate([grad, low], axis=1))
-                gathered = got[:, :width]
-                lows[section] = got[:, width:]
-            else:
-                lows[section] = gather_dp(low)
+                gathered = gather_dp(grad)
 
     with jax.named_scope("outputs"):
-        pair = [jnp.concatenate([lows[s], ups[s]], axis=1) for s in range(sections)]
+        low = gather_mp(low)
+
+        def columns(array, section):
+            turn = last - section
+            left = 1 + turn
+            right = 0 if turn == 0 else sections + turn
+            return [
+                array[:, left * rank : (left + 1) * rank],
+                array[:, right * rank : (right + 1) * rank],
+            ]
+
+        pair = [
+            jnp.concatenate(columns(low, s) + columns(up, s), axis=1)
+            for s in range(sections)
+        ]
         mine = jnp.where(core == 0, pair[0], pair[1])
         other = jnp.where(core == 0, pair[1], pair[0])
+        other, grads[0] = held(other, grads[0])
         got = swap_sections(other)
 
         def joined(own, received, rows):

time: 175 us -> 160 us (0.914)
  starting transfers between devices: 56.4 us -> 80.4 us
  blocking collectives: 19.2 us -> 0 us
  waiting for transfers between devices: 60.1 us -> 44.2 us
  local copies, waits for them, and re-layouts: 9.54 us -> 6.22 us
  matrix products: 24 us -> 22.2 us
    all_to_all x1 -> x0, blocking collectives: 19.2 us -> none  [gather_dp(): got = lax.all_to_all(copies, 'dp', 0, 0, tiled=True)]
    all_to_all x2, waiting for transfers between devices: 28.9 us -> 17 us  [scatter_sum_dp(): got = lax.all_to_all(partial, 'dp', 0, 0, tiled=True)]
    ppermute x10 -> x7, starting transfers between devices: 15.8 us -> 26.5 us  [swap_sections(): return lax.ppermute(block, 'section', [(0, 1), (1, 0)])]
    ppermute x12 -> x21, waiting for transfers between devices: 15.7 us -> 6.78 us  [shift_mp(): lax.ppermute(block, 'mp', [(i, (i + distance) % count) for i in range(cou...]
    ppermute x12 -> x21, starting transfers between devices: 21.2 us -> 29.8 us  [shift_mp(): lax.ppermute(block, 'mp', [(i, (i + distance) % count) for i in range(cou...]
    all_to_all x2 -> x3, waiting for transfers between devices: 13.8 us -> 19 us  [gather_dp(): got = lax.all_to_all(copies, 'dp', 0, 0, tiled=True)]
    concatenate x2 -> x0, local copies, waits for them, and re-layouts: 3.79 us -> none  [body(): jnp.concatenate([times_t(middle_all, of_section(weight_low, section)).ast...]
    all_to_all x2 -> x3, starting transfers between devices: 11.7 us -> 15.4 us  [gather_dp(): got = lax.all_to_all(copies, 'dp', 0, 0, tiled=True)]
  transfers between devices with their start and end apart: 26 -> 33, of which waited for: 13 -> 14; matrix products, arithmetic and copies ran while one was open for 9% -> 17% of each run, Pallas kernels for 0% -> 0%
where the time goes in v3:
time: 160 us; the launch traced here: 159 us
  starting transfers between devices  80.4 us (50%)
  waiting for transfers between devices  44.2 us (28%)
  matrix products  22.2 us (14%)
  local copies, waits for them, and re-layouts  6.22 us (4%)
  other arithmetic  4.67 us (3%)
    ppermute x21, starting transfers between devices, shift_mp(): lax.ppermute(block, 'mp', [(i, (i + distance) % count) for i in range(cou...  29.8 us
    ppermute x7, starting transfers between devices, swap_sections(): return lax.ppermute(block, 'section', [(0, 1), (1, 0)])  26.5 us
    dot_general x10, matrix products, times_t(): lax.dot_general(left, right, (((1,), (1,)), ((), ())), preferred_element_...  21.6 us
    all_to_all x3, waiting for transfers between devices, gather_dp(): got = lax.all_to_all(copies, 'dp', 0, 0, tiled=True)  19 us
    all_to_all x2, waiting for transfers between devices, scatter_sum_dp(): got = lax.all_to_all(partial, 'dp', 0, 0, tiled=True)  17 us
    all_to_all x3, starting transfers between devices, gather_dp(): got = lax.all_to_all(copies, 'dp', 0, 0, tiled=True)  15.4 us
    all_to_all x2, starting transfers between devices, scatter_sum_dp(): got = lax.all_to_all(partial, 'dp', 0, 0, tiled=True)  8.63 us
    ppermute x21, waiting for transfers between devices, shift_mp(): lax.ppermute(block, 'mp', [(i, (i + distance) % count) for i in range(cou...  6.78 us
  transfers between devices with their start and end apart: 33, of which 14 were waited for; matrix products, arithmetic and copies ran while one was open for 17% of the time, Pallas kernels for 0%

profile of v3, /device:TPU:1, one launch (start us, length us, event | category | flops | bytes accessed | tf_op | source)
XLA Modules:
  0.0 159.0 jit_solution(16576930110519870115)
XLA Ops:
  4.3 6.8 %all-to-all-start = ((bf16[16,16,2048]{2,1,0:T(8,128)(2,1)}), bf16[16,16,2048]{2,1,0:T(8,128)(2,1)S(1)}, u32[]{:S(2)}, u32[]{:S(2)}) async-start(bf16[16,16,2048]{2,1,0:T(8,128)(2,1)} %broadcast_in_dim.77), calls=%async_computation | async-start | bytes 2097152 | tf_op jit(solution)/shard_map/all_to_all | solution.py:30
  14.1 13.3 %all-to-all-done = bf16[16,16,2048]{2,1,0:T(8,128)(2,1)S(1)} async-done(((bf16[16,16,2048]{2,1,0:T(8,128)(2,1)}), bf16[16,16,2048]{2,1,0:T(8,128)(2,1)S(1)}, u32[]{:S(2)}, u32[]{:S(2)}) %all-to-all-start) | async-done | bytes 1048608 | tf_op jit(solution)/shard_map/all_to_all | solution.py:30
  27.4 3.4 %fusion.18 = bf16[256,896]{1,0:T(8,128)(2,1)S(1)} fusion(bf16[256,2048]{1,0:T(8,128)(2,1)S(1)} %bitcast.124, bf16[896,2048]{1,0:T(8,128)(2,1)} %collective-permute-done, pred[]{:T(512)S(6)} %eq.80, bf16[1,896,2048]{2,1,0:T(8,128)(2,1)} %param.14), kind=kOutput, calls=%fused_computation.16 | convolution fusion | flops 941588480 | bytes 8847361 | tf_op jit(solution)/shard_map/up_1/dot_general | solution.py:11
  30.8 1.7 %collective-permute-start.1 = (bf16[64,896]{1,0:T(8,128)(2,1)S(1)}, bf16[64,896]{1,0:T(8,128)(2,1)S(1)}, u32[]{:S(2)}, u32[]{:S(2)}) collective-permute-start(bf16[64,896]{1,0:T(8,128)(2,1)S(1)} %get-tuple-element.17), channel_id=1, source_target_pairs={{0,1},{1,2},{2,3},{3,0},{4,5},{5,6},{6,7},{7,4},{8,9},{9,10},{10,1... | collective-permute-start | bytes 344072 | tf_op jit(solution)/shard_map/up_1/ppermute | solution.py:22
  32.5 3.3 %collective-permute-start.2 = (bf16[64,896]{1,0:T(8,128)(2,1)S(1)}, bf16[64,896]{1,0:T(8,128)(2,1)S(1)}, u32[]{:S(2)}, u32[]{:S(2)}) collective-permute-start(bf16[64,896]{1,0:T(8,128)(2,1)S(1)} %get-tuple-element.19), channel_id=1, source_target_pairs={{0,2},{1,3},{2,0},{3,1},{4,6},{5,7},{6,4},{7,5},{8,10},{9,11},{10,... | collective-permute-start | bytes 344072 | tf_op jit(solution)/shard_map/up_1/ppermute | solution.py:22
  36.7 4.2 %collective-permute-start.10 = (bf16[80,2048]{1,0:T(8,128)(2,1)S(1)}, bf16[80,2048]{1,0:T(8,128)(2,1)}, u32[]{:S(2)}, u32[]{:S(2)}) collective-permute-start(bf16[80,2048]{1,0:T(8,128)(2,1)S(1)} %pad_maximum_fusion), channel_id=1, source_target_pairs={{0,64},{64,0},{1,65},{65,1},{2,66},{66,2},{3,67},{67,3},{4,68},{68... | collective-permute-start | bytes 983048 | tf_op jit(solution)/shard_map/ppermute | solution.py:17
  48.3 4.4 %fusion.12 = bf16[256,2048]{1,0:T(8,128)(2,1)} fusion(bf16[256,896]{1,0:T(8,128)(2,1)S(1)} %constant_dynamic-update-slice_fusion.8, bf16[2048,896]{1,0:T(8,128)(2,1)} %collective-permute-done.9, pred[]{:T(512)S(6)} %eq.80, bf16[1,2048,896]{2,1,0:T(8,128)(2,1)} %param.15), kind=kOutput, calls=%fused_computation.12 | convolution fusion | flops 941883392 | bytes 8847361 | tf_op jit(solution)/shard_map/low_1/dot_general | solution.py:11
  52.7 5.0 %all-to-all-start.1 = ((bf16[16,16,2048]{2,1,0:T(8,128)(2,1)}), bf16[16,16,2048]{2,1,0:T(8,128)(2,1)S(1)}, u32[]{:S(2)}, u32[]{:S(2)}) async-start(bf16[16,16,2048]{2,1,0:T(8,128)(2,1)} %bitcast.18), calls=%async_computation.1 | async-start | bytes 2097152 | tf_op jit(solution)/shard_map/low_1/all_to_all | solution.py:36
  57.7 5.4 %collective-permute-start.5 = (bf16[80,64]{1,0:T(8,128)(2,1)S(1)}, bf16[80,64]{1,0:T(8,128)(2,1)S(1)}, u32[]{:S(2)}, u32[]{:S(2)}) collective-permute-start(bf16[80,64]{1,0:T(8,128)(2,1)S(1)} %pad_maximum_fusion.4), channel_id=1, source_target_pairs={{0,64},{64,0},{1,65},{65,1},{2,66},{66,2},{3,67},{67,3},{4,68},{68... | collective-permute-start | bytes 30728 | tf_op jit(solution)/shard_map/ppermute | solution.py:17
  65.1 5.3 %all-to-all-done.1 = bf16[16,16,2048]{2,1,0:T(8,128)(2,1)S(1)} async-done(((bf16[16,16,2048]{2,1,0:T(8,128)(2,1)}), bf16[16,16,2048]{2,1,0:T(8,128)(2,1)S(1)}, u32[]{:S(2)}, u32[]{:S(2)}) %all-to-all-start.1) | async-done | bytes 1048608 | tf_op jit(solution)/shard_map/low_1/all_to_all | solution.py:36
  72.6 3.8 %all-to-all-start.2 = ((bf16[16,16,2048]{2,1,0:T(8,128)(2,1)}), bf16[16,16,2048]{2,1,0:T(8,128)(2,1)S(1)}, u32[]{:S(2)}, u32[]{:S(2)}) async-start(bf16[16,16,2048]{2,1,0:T(8,128)(2,1)} %broadcast_in_dim.78), calls=%async_computation.2 | async-start | bytes 2097152 | tf_op jit(solution)/shard_map/low_1/all_to_all | solution.py:30
  76.5 2.9 %collective-permute-start.15 = (bf16[16,192]{1,0:T(8,128)(2,1)S(1)}, bf16[16,192]{1,0:T(8,128)(2,1)S(1)}, u32[]{:S(2)}, u32[]{:S(2)}) collective-permute-start(bf16[16,192]{1,0:T(8,128)(2,1)S(1)} %pad_maximum_fusion.5), channel_id=1, source_target_pairs={{0,2},{1,3},{2,0},{3,1},{4,6},{5,7},{6,4},{7,5},{8,10},{9,11},{10,... | collective-permute-start | bytes 18440 | tf_op jit(solution)/shard_map/up_1/ppermute | solution.py:22
  84.0 3.3 %collective-permute-start.18 = (bf16[16,64]{1,0:T(8,128)(2,1)S(1)}, bf16[16,64]{1,0:T(8,128)(2,1)S(1)}, u32[]{:S(2)}, u32[]{:S(2)}) collective-permute-start(bf16[16,64]{1,0:T(8,128)(2,1)S(1)} %convolution_convert_fusion.4), channel_id=1, source_target_pairs={{0,2},{1,3},{2,0},{3,1},{4,6},{5,7},{6,4},{7,5},{8,10},{9,11},{10,... | collective-permute-start | bytes 6152 | tf_op jit(solution)/shard_map/up_0/ppermute | solution.py:22
  87.3 1.6 %all-to-all-done.2 = bf16[16,16,2048]{2,1,0:T(8,128)(2,1)S(1)} async-done(((bf16[16,16,2048]{2,1,0:T(8,128)(2,1)}), bf16[16,16,2048]{2,1,0:T(8,128)(2,1)S(1)}, u32[]{:S(2)}, u32[]{:S(2)}) %all-to-all-start.2) | async-done | bytes 1048608 | tf_op jit(solution)/shard_map/low_1/all_to_all | solution.py:30
  88.9 4.4 %fusion.21 = bf16[256,896]{1,0:T(8,128)(2,1)S(1)} fusion(bf16[256,2048]{1,0:T(8,128)(2,1)S(1)} %bitcast.125, bf16[896,2048]{1,0:T(8,128)(2,1)} %collective-permute-done, pred[]{:T(512)S(6)} %eq.79, bf16[1,896,2048]{2,1,0:T(8,128)(2,1)} %param.14), kind=kOutput, calls=%fused_computation.17 | convolution fusion | flops 941588480 | bytes 8847361 | tf_op jit(solution)/shard_map/up_0/dot_general | solution.py:11
  93.5 2.8 %collective-permute-start.12 = (bf16[64,896]{1,0:T(8,128)(2,1)S(1)}, bf16[64,896]{1,0:T(8,128)(2,1)S(1)}, u32[]{:S(2)}, u32[]{:S(2)}) collective-permute-start(bf16[64,896]{1,0:T(8,128)(2,1)S(1)} %get-tuple-element.16), channel_id=1, source_target_pairs={{0,2},{1,3},{2,0},{3,1},{4,6},{5,7},{6,4},{7,5},{8,10},{9,11},{10,... | collective-permute-start | bytes 344072 | tf_op jit(solution)/shard_map/up_0/ppermute | solution.py:22
  101.8 2.2 %collective-permute-start.21 = (bf16[64,896]{1,0:T(8,128)(2,1)S(1)}, bf16[64,896]{1,0:T(8,128)(2,1)S(1)}, u32[]{:S(2)}, u32[]{:S(2)}) collective-permute-start(bf16[64,896]{1,0:T(8,128)(2,1)S(1)} %get-tuple-element.39), channel_id=1, source_target_pairs={{0,2},{1,3},{2,0},{3,1},{4,6},{5,7},{6,4},{7,5},{8,10},{9,11},{10,... | collective-permute-start | bytes 344072 | tf_op jit(solution)/shard_map/low_0/ppermute | solution.py:22
  105.9 4.8 %all-to-all-start.3 = ((bf16[16,80,256]{2,1,0:T(8,128)(2,1)}), bf16[16,80,256]{2,1,0:T(8,128)(2,1)S(1)}, u32[]{:S(2)}, u32[]{:S(2)}) async-start(bf16[16,80,256]{2,1,0:T(8,128)(2,1)} %broadcast_in_dim.79), calls=%async_computation.3 | async-start | bytes 1310720 | tf_op jit(solution)/shard_map/low_0/all_to_all | solution.py:30
  110.8 5.4 %fusion.15 = bf16[256,2048]{1,0:T(8,128)(2,1)} fusion(bf16[256,896]{1,0:T(8,128)(2,1)S(1)} %constant_dynamic-update-slice_fusion.4, bf16[2048,896]{1,0:T(8,128)(2,1)} %collective-permute-done.9, pred[]{:T(512)S(6)} %eq.79, bf16[1,2048,896]{2,1,0:T(8,128)(2,1)} %param.15), kind=kOutput, calls=%fused_computation.13 | convolution fusion | flops 941883392 | bytes 8847361 | tf_op jit(solution)/shard_map/low_0/dot_general | solution.py:11
  116.2 4.1 %all-to-all-done.3 = bf16[16,80,256]{2,1,0:T(8,128)(2,1)S(1)} async-done(((bf16[16,80,256]{2,1,0:T(8,128)(2,1)}), bf16[16,80,256]{2,1,0:T(8,128)(2,1)S(1)}, u32[]{:S(2)}, u32[]{:S(2)}) %all-to-all-start.3) | async-done | bytes 655392 | tf_op jit(solution)/shard_map/low_0/all_to_all | solution.py:30
  122.3 1.7 %collective-permute-start.25 = (bf16[64,256]{1,0:T(8,128)(2,1)S(1)}, bf16[64,256]{1,0:T(8,128)(2,1)S(1)}, u32[]{:S(2)}, u32[]{:S(2)}) collective-permute-start(bf16[64,256]{1,0:T(8,128)(2,1)S(1)} %slice_reduce_fusion), channel_id=1, source_target_pairs={{0,3},{1,0},{2,1},{3,2},{4,7},{5,4},{6,5},{7,6},{8,11},{9,8},{10,9... | collective-permute-start | bytes 98312 | tf_op jit(solution)/shard_map/outputs/ppermute | solution.py:22
  124.0 3.7 %all-to-all-start.4 = ((bf16[16,16,2048]{2,1,0:T(8,128)(2,1)}), bf16[16,16,2048]{2,1,0:T(8,128)(2,1)S(1)}, u32[]{:S(2)}, u32[]{:S(2)}) async-start(bf16[16,16,2048]{2,1,0:T(8,128)(2,1)} %bitcast.26), calls=%async_computation.4 | async-start | bytes 2097152 | tf_op jit(solution)/shard_map/low_0/all_to_all | solution.py:36
  128.2 11.7 %all-to-all-done.4 = bf16[16,16,2048]{2,1,0:T(8,128)(2,1)S(1)} async-done(((bf16[16,16,2048]{2,1,0:T(8,128)(2,1)}), bf16[16,16,2048]{2,1,0:T(8,128)(2,1)S(1)}, u32[]{:S(2)}, u32[]{:S(2)}) %all-to-all-start.4) | async-done | bytes 1048608 | tf_op jit(solution)/shard_map/low_0/all_to_all | solution.py:36
  140.9 14.5 %collective-permute-start.26 = (bf16[16,2048]{1,0:T(8,128)(2,1)S(1)}, bf16[16,2048]{1,0:T(8,128)(2,1)S(1)}, u32[]{:S(2)}, u32[]{:S(2)}) collective-permute-start(bf16[16,2048]{1,0:T(8,128)(2,1)S(1)} %broadcast_select_fusion.2), channel_id=1, source_target_pairs={{0,64},{64,0},{1,65},{65,1},{2,66},{66,2},{3,67},{67,3},{4,68},{68... | collective-permute-start | bytes 196616 | tf_op jit(solution)/shard_map/outputs/ppermute | solution.py:17
  (137 shorter events, 38.0 us)
Async XLA Ops:
  0.7 26.7 %collective-permute-start = (bf16[896,2048]{1,0:T(8,128)(2,1)}, bf16[896,2048]{1,0:T(8,128)(2,1)}, u32[]{:S(2)}, u32[]{:S(2)}) collective-permute-start(bf16[896,2048]{1,0:T(8,128)(2,1)} %bitcast.151), channel_id=1, source_target_pairs={{0,64},{64,0},{1,65},{65,1},{2,66},{66,2},{3,67},{67,3},{4,68},{68... | collective-permute-start | bytes 11010056 | tf_op jit(solution)/shard_map/ppermute | solution.py:17
  2.2 46.1 %collective-permute-start.9 = (bf16[2048,896]{1,0:T(8,128)(2,1)}, bf16[2048,896]{1,0:T(8,128)(2,1)}, u32[]{:S(2)}, u32[]{:S(2)}) collective-permute-start(bf16[2048,896]{1,0:T(8,128)(2,1)} %bitcast.152), channel_id=1, source_target_pairs={{0,64},{64,0},{1,65},{65,1},{2,66},{66,2},{3,67},{67,3},{4,68},{68... | collective-permute-start | bytes 11010056 | tf_op jit(solution)/shard_map/ppermute | solution.py:17
  4.3 23.1 %all-to-all-start = ((bf16[16,16,2048]{2,1,0:T(8,128)(2,1)}), bf16[16,16,2048]{2,1,0:T(8,128)(2,1)S(1)}, u32[]{:S(2)}, u32[]{:S(2)}) async-start(bf16[16,16,2048]{2,1,0:T(8,128)(2,1)} %broadcast_in_dim.77), calls=%async_computation | async-start | bytes 2097152 | tf_op jit(solution)/shard_map/all_to_all | solution.py:30
  12.1 24.5 %collective-permute-start.4 = (bf16[128,896]{1,0:T(8,128)(2,1)S(1)}, bf16[128,896]{1,0:T(8,128)(2,1)S(1)}, u32[]{:S(2)}, u32[]{:S(2)}) collective-permute-start(bf16[128,896]{1,0:T(8,128)(2,1)S(1)} %pad_maximum_fusion.2), channel_id=1, source_target_pairs={{0,64},{64,0},{1,65},{65,1},{2,66},{66,2},{3,67},{67,3},{4,68},{68... | collective-permute-start | bytes 688136 | tf_op jit(solution)/shard_map/ppermute | solution.py:17
  30.8 10.1 %collective-permute-start.1 = (bf16[64,896]{1,0:T(8,128)(2,1)S(1)}, bf16[64,896]{1,0:T(8,128)(2,1)S(1)}, u32[]{:S(2)}, u32[]{:S(2)}) collective-permute-start(bf16[64,896]{1,0:T(8,128)(2,1)S(1)} %get-tuple-element.17), channel_id=1, source_target_pairs={{0,1},{1,2},{2,3},{3,0},{4,5},{5,6},{6,7},{7,4},{8,9},{9,10},{10,1... | collective-permute-start | bytes 344072 | tf_op jit(solution)/shard_map/up_1/ppermute | solution.py:22
  32.5 8.4 %collective-permute-start.2 = (bf16[64,896]{1,0:T(8,128)(2,1)S(1)}, bf16[64,896]{1,0:T(8,128)(2,1)S(1)}, u32[]{:S(2)}, u32[]{:S(2)}) collective-permute-start(bf16[64,896]{1,0:T(8,128)(2,1)S(1)} %get-tuple-element.19), channel_id=1, source_target_pairs={{0,2},{1,3},{2,0},{3,1},{4,6},{5,7},{6,4},{7,5},{8,10},{9,11},{10,... | collective-permute-start | bytes 344072 | tf_op jit(solution)/shard_map/up_1/ppermute | solution.py:22
  36.7 27.3 %collective-permute-start.10 = (bf16[80,2048]{1,0:T(8,128)(2,1)S(1)}, bf16[80,2048]{1,0:T(8,128)(2,1)}, u32[]{:S(2)}, u32[]{:S(2)}) collective-permute-start(bf16[80,2048]{1,0:T(8,128)(2,1)S(1)} %pad_maximum_fusion), channel_id=1, source_target_pairs={{0,64},{64,0},{1,65},{65,1},{2,66},{66,2},{3,67},{67,3},{4,68},{68... | collective-permute-start | bytes 983048 | tf_op jit(solution)/shard_map/ppermute | solution.py:17
  42.2 5.2 %collective-permute-start.7 = (bf16[64,896]{1,0:T(8,128)(2,1)S(1)}, bf16[64,896]{1,0:T(8,128)(2,1)S(1)}, u32[]{:S(2)}, u32[]{:S(2)}) collective-permute-start(bf16[64,896]{1,0:T(8,128)(2,1)S(1)} %get-tuple-element.37), channel_id=1, source_target_pairs={{0,2},{1,3},{2,0},{3,1},{4,6},{5,7},{6,4},{7,5},{8,10},{9,11},{10,... | collective-permute-start | bytes 344072 | tf_op jit(solution)/shard_map/low_1/ppermute | solution.py:22
  52.7 17.7 %all-to-all-start.1 = ((bf16[16,16,2048]{2,1,0:T(8,128)(2,1)}), bf16[16,16,2048]{2,1,0:T(8,128)(2,1)S(1)}, u32[]{:S(2)}, u32[]{:S(2)}) async-start(bf16[16,16,2048]{2,1,0:T(8,128)(2,1)} %bitcast.18), calls=%async_computation.1 | async-start | bytes 2097152 | tf_op jit(solution)/shard_map/low_1/all_to_all | solution.py:36
  57.7 6.2 %collective-permute-start.5 = (bf16[80,64]{1,0:T(8,128)(2,1)S(1)}, bf16[80,64]{1,0:T(8,128)(2,1)S(1)}, u32[]{:S(2)}, u32[]{:S(2)}) collective-permute-start(bf16[80,64]{1,0:T(8,128)(2,1)S(1)} %pad_maximum_fusion.4), channel_id=1, source_target_pairs={{0,64},{64,0},{1,65},{65,1},{2,66},{66,2},{3,67},{67,3},{4,68},{68... | collective-permute-start | bytes 30728 | tf_op jit(solution)/shard_map/ppermute | solution.py:17
  72.6 16.3 %all-to-all-start.2 = ((bf16[16,16,2048]{2,1,0:T(8,128)(2,1)}), bf16[16,16,2048]{2,1,0:T(8,128)(2,1)S(1)}, u32[]{:S(2)}, u32[]{:S(2)}) async-start(bf16[16,16,2048]{2,1,0:T(8,128)(2,1)} %broadcast_in_dim.78), calls=%async_computation.2 | async-start | bytes 2097152 | tf_op jit(solution)/shard_map/low_1/all_to_all | solution.py:30
  83.3 13.0 %collective-permute-start.17 = (bf16[16,64]{1,0:T(8,128)(2,1)S(1)}, bf16[16,64]{1,0:T(8,128)(2,1)S(1)}, u32[]{:S(2)}, u32[]{:S(2)}) collective-permute-start(bf16[16,64]{1,0:T(8,128)(2,1)S(1)} %convolution_convert_fusion.4), channel_id=1, source_target_pairs={{0,1},{1,2},{2,3},{3,0},{4,5},{5,6},{6,7},{7,4},{8,9},{9,10},{10,1... | collective-permute-start | bytes 6152 | tf_op jit(solution)/shard_map/up_0/ppermute | solution.py:22
  84.0 13.7 %collective-permute-start.18 = (bf16[16,64]{1,0:T(8,128)(2,1)S(1)}, bf16[16,64]{1,0:T(8,128)(2,1)S(1)}, u32[]{:S(2)}, u32[]{:S(2)}) collective-permute-start(bf16[16,64]{1,0:T(8,128)(2,1)S(1)} %convolution_convert_fusion.4), channel_id=1, source_target_pairs={{0,2},{1,3},{2,0},{3,1},{4,6},{5,7},{6,4},{7,5},{8,10},{9,11},{10,... | collective-permute-start | bytes 6152 | tf_op jit(solution)/shard_map/up_0/ppermute | solution.py:22
  87.3 10.5 %collective-permute-start.19 = (bf16[16,64]{1,0:T(8,128)(2,1)S(1)}, bf16[16,64]{1,0:T(8,128)(2,1)S(1)}, u32[]{:S(2)}, u32[]{:S(2)}) collective-permute-start(bf16[16,64]{1,0:T(8,128)(2,1)S(1)} %convolution_convert_fusion.4), channel_id=1, source_target_pairs={{0,3},{1,0},{2,1},{3,2},{4,7},{5,4},{6,5},{7,6},{8,11},{9,8},{10,9... | collective-permute-start | bytes 6152 | tf_op jit(solution)/shard_map/up_0/ppermute | solution.py:22
  93.5 6.2 %collective-permute-start.12 = (bf16[64,896]{1,0:T(8,128)(2,1)S(1)}, bf16[64,896]{1,0:T(8,128)(2,1)S(1)}, u32[]{:S(2)}, u32[]{:S(2)}) collective-permute-start(bf16[64,896]{1,0:T(8,128)(2,1)S(1)} %get-tuple-element.16), channel_id=1, source_target_pairs={{0,2},{1,3},{2,0},{3,1},{4,6},{5,7},{6,4},{7,5},{8,10},{9,11},{10,... | collective-permute-start | bytes 344072 | tf_op jit(solution)/shard_map/up_0/ppermute | solution.py:22
  100.3 10.3 %collective-permute-start.20 = (bf16[64,896]{1,0:T(8,128)(2,1)S(1)}, bf16[64,896]{1,0:T(8,128)(2,1)S(1)}, u32[]{:S(2)}, u32[]{:S(2)}) collective-permute-start(bf16[64,896]{1,0:T(8,128)(2,1)S(1)} %get-tuple-element.39), channel_id=1, source_target_pairs={{0,1},{1,2},{2,3},{3,0},{4,5},{5,6},{6,7},{7,4},{8,9},{9,10},{10,1... | collective-permute-start | bytes 344072 | tf_op jit(solution)/shard_map/low_0/ppermute | solution.py:22
  101.8 8.9 %collective-permute-start.21 = (bf16[64,896]{1,0:T(8,128)(2,1)S(1)}, bf16[64,896]{1,0:T(8,128)(2,1)S(1)}, u32[]{:S(2)}, u32[]{:S(2)}) collective-permute-start(bf16[64,896]{1,0:T(8,128)(2,1)S(1)} %get-tuple-element.39), channel_id=1, source_target_pairs={{0,2},{1,3},{2,0},{3,1},{4,6},{5,7},{6,4},{7,5},{8,10},{9,11},{10,... | collective-permute-start | bytes 344072 | tf_op jit(solution)/shard_map/low_0/ppermute | solution.py:22
  104.0 6.8 %collective-permute-start.22 = (bf16[64,896]{1,0:T(8,128)(2,1)S(1)}, bf16[64,896]{1,0:T(8,128)(2,1)S(1)}, u32[]{:S(2)}, u32[]{:S(2)}) collective-permute-start(bf16[64,896]{1,0:T(8,128)(2,1)S(1)} %get-tuple-element.39), channel_id=1, source_target_pairs={{0,3},{1,0},{2,1},{3,2},{4,7},{5,4},{6,5},{7,6},{8,11},{9,8},{10,9... | collective-permute-start | bytes 344072 | tf_op jit(solution)/shard_map/low_0/ppermute | solution.py:22
  105.9 14.5 %all-to-all-start.3 = ((bf16[16,80,256]{2,1,0:T(8,128)(2,1)}), bf16[16,80,256]{2,1,0:T(8,128)(2,1)S(1)}, u32[]{:S(2)}, u32[]{:S(2)}) async-start(bf16[16,80,256]{2,1,0:T(8,128)(2,1)} %broadcast_in_dim.79), calls=%async_computation.3 | async-start | bytes 1310720 | tf_op jit(solution)/shard_map/low_0/all_to_all | solution.py:30
  120.5 7.4 %collective-permute-start.23 = (bf16[64,256]{1,0:T(8,128)(2,1)S(1)}, bf16[64,256]{1,0:T(8,128)(2,1)S(1)}, u32[]{:S(2)}, u32[]{:S(2)}) collective-permute-start(bf16[64,256]{1,0:T(8,128)(2,1)S(1)} %slice_reduce_fusion), channel_id=1, source_target_pairs={{0,1},{1,2},{2,3},{3,0},{4,5},{5,6},{6,7},{7,4},{8,9},{9,10},{10,1... | collective-permute-start | bytes 98312 | tf_op jit(solution)/shard_map/outputs/ppermute | solution.py:22
  121.5 6.3 %collective-permute-start.24 = (bf16[64,256]{1,0:T(8,128)(2,1)S(1)}, bf16[64,256]{1,0:T(8,128)(2,1)S(1)}, u32[]{:S(2)}, u32[]{:S(2)}) collective-permute-start(bf16[64,256]{1,0:T(8,128)(2,1)S(1)} %slice_reduce_fusion), channel_id=1, source_target_pairs={{0,2},{1,3},{2,0},{3,1},{4,6},{5,7},{6,4},{7,5},{8,10},{9,11},{10,... | collective-permute-start | bytes 98312 | tf_op jit(solution)/shard_map/outputs/ppermute | solution.py:22
  122.3 5.6 %collective-permute-start.25 = (bf16[64,256]{1,0:T(8,128)(2,1)S(1)}, bf16[64,256]{1,0:T(8,128)(2,1)S(1)}, u32[]{:S(2)}, u32[]{:S(2)}) collective-permute-start(bf16[64,256]{1,0:T(8,128)(2,1)S(1)} %slice_reduce_fusion), channel_id=1, source_target_pairs={{0,3},{1,0},{2,1},{3,2},{4,7},{5,4},{6,5},{7,6},{8,11},{9,8},{10,9... | collective-permute-start | bytes 98312 | tf_op jit(solution)/shard_map/outputs/ppermute | solution.py:22
  124.0 15.8 %all-to-all-start.4 = ((bf16[16,16,2048]{2,1,0:T(8,128)(2,1)}), bf16[16,16,2048]{2,1,0:T(8,128)(2,1)S(1)}, u32[]{:S(2)}, u32[]{:S(2)}) async-start(bf16[16,16,2048]{2,1,0:T(8,128)(2,1)} %bitcast.26), calls=%async_computation.4 | async-start | bytes 2097152 | tf_op jit(solution)/shard_map/low_0/all_to_all | solution.py:36
  140.9 15.4 %collective-permute-start.26 = (bf16[16,2048]{1,0:T(8,128)(2,1)S(1)}, bf16[16,2048]{1,0:T(8,128)(2,1)S(1)}, u32[]{:S(2)}, u32[]{:S(2)}) collective-permute-start(bf16[16,2048]{1,0:T(8,128)(2,1)S(1)} %broadcast_select_fusion.2), channel_id=1, source_target_pairs={{0,64},{64,0},{1,65},{65,1},{2,66},{66,2},{3,67},{67,3},{4,68},{68... | collective-permute-start | bytes 196616 | tf_op jit(solution)/shard_map/outputs/ppermute | solution.py:17
  (20 other events, 262.0 us)

commit v4 on v3

--- a/solution.py
+++ b/solution.py
@@ -158,11 +158,12 @@
     lows = []
     for section in range(last, -1, -1):
         with jax.named_scope(f"up_{section}"):
-            up = [times_t(grad, of_section(pout_up, section)).astype(BF16)]
+            ups.append(times_t(grad, of_section(pout_up, section)).astype(BF16))
             if section == last:
-                up += [of_section(left_up, s) for s in range(last, -1, -1)]
-            up = from_all_mp(jnp.concatenate(up, axis=1))
-            up = sum(part.astype(F32) for part in up).astype(BF16)
+                ups += [of_section(left_up, s) for s in range(last, -1, -1)]
+            if section == 0:
+                up = from_all_mp(jnp.concatenate(ups, axis=1))
+                up = sum(part.astype(F32) for part in up).astype(BF16)
             weight = of_section(weight_up, section)
             summed = scatter_sum_mp(times_t(gathered, weight).astype(BF16))
             scale = of_section(deriv_up, section).astype(F32)
@@ -171,11 +172,9 @@
             low = [times_t(middle, of_section(pout_low, section)).astype(BF16)]
             if section == last:
                 low += [of_section(left_low, s) for s in range(last, -1, -1)]
-            ups.append(up)
             lows += low
             if section == 0:
                 low = jnp.concatenate(lows, axis=1)
-                up = jnp.concatenate(ups, axis=1)
                 rows = low.shape[0]
                 both = gather_dp(jnp.concatenate([low, up], axis=0))
                 both = both.reshape(dp_count, rows + up.shape[0], up.shape[1])

time: 160 us -> 157 us (0.981)
  starting transfers between devices: 80.4 us -> 73.6 us
  waiting for transfers between devices: 44.2 us -> 48.2 us
    all_to_all x3, waiting for transfers between devices: 19 us -> 24 us  [gather_dp(): got = lax.all_to_all(copies, 'dp', 0, 0, tiled=True)]
    ppermute x21 -> x18, starting transfers between devices: 29.8 us -> 25.5 us  [shift_mp(): lax.ppermute(block, 'mp', [(i, (i + distance) % count) for i in range(cou...]
    ppermute x7, starting transfers between devices: 26.5 us -> 24.7 us  [swap_sections(): return lax.ppermute(block, 'section', [(0, 1), (1, 0)])]
    ppermute x21 -> x18, waiting for transfers between devices: 6.78 us -> 5.81 us  [shift_mp(): lax.ppermute(block, 'mp', [(i, (i + distance) % count) for i in range(cou...]
  transfers between devices with their start and end apart: 33 -> 30, of which waited for: 14 -> 13; matrix products, arithmetic and copies ran while one was open for 17% -> 18% of each run, Pallas kernels for 0% -> 0%
where the time goes in v4:
time: 157 us; the launch traced here: 156 us
  starting transfers between devices  73.6 us (47%)
  waiting for transfers between devices  48.2 us (31%)
  matrix products  22.3 us (14%)
  local copies, waits for them, and re-layouts  6.26 us (4%)
  other arithmetic  4.6 us (3%)
    ppermute x18, starting transfers between devices, shift_mp(): lax.ppermute(block, 'mp', [(i, (i + distance) % count) for i in range(cou...  25.5 us
    ppermute x7, starting transfers between devices, swap_sections(): return lax.ppermute(block, 'section', [(0, 1), (1, 0)])  24.7 us
    all_to_all x3, waiting for transfers between devices, gather_dp(): got = lax.all_to_all(copies, 'dp', 0, 0, tiled=True)  24 us
    dot_general x10, matrix products, times_t(): lax.dot_general(left, right, (((1,), (1,)), ((), ())), preferred_element_...  21.7 us
    all_to_all x2, waiting for transfers between devices, scatter_sum_dp(): got = lax.all_to_all(partial, 'dp', 0, 0, tiled=True)  16.9 us
    all_to_all x3, starting transfers between devices, gather_dp(): got = lax.all_to_all(copies, 'dp', 0, 0, tiled=True)  14.9 us
    all_to_all x2, starting transfers between devices, scatter_sum_dp(): got = lax.all_to_all(partial, 'dp', 0, 0, tiled=True)  8.49 us
    ppermute x18, waiting for transfers between devices, shift_mp(): lax.ppermute(block, 'mp', [(i, (i + distance) % count) for i in range(cou...  5.81 us
  transfers between devices with their start and end apart: 30, of which 13 were waited for; matrix products, arithmetic and copies ran while one was open for 18% of the time, Pallas kernels for 0%

profile of v4, /device:TPU:1, one launch (start us, length us, event | category | flops | bytes accessed | tf_op | source)
XLA Modules:
  0.0 156.2 jit_solution(2980891504400738684)
XLA Ops:
  4.3 6.8 %all-to-all-start = ((bf16[16,16,2048]{2,1,0:T(8,128)(2,1)}), bf16[16,16,2048]{2,1,0:T(8,128)(2,1)S(1)}, u32[]{:S(2)}, u32[]{:S(2)}) async-start(bf16[16,16,2048]{2,1,0:T(8,128)(2,1)} %broadcast_in_dim.77), calls=%async_computation | async-start | bytes 2097152 | tf_op jit(solution)/shard_map/all_to_all | solution.py:30
  12.9 14.5 %all-to-all-done = bf16[16,16,2048]{2,1,0:T(8,128)(2,1)S(1)} async-done(((bf16[16,16,2048]{2,1,0:T(8,128)(2,1)}), bf16[16,16,2048]{2,1,0:T(8,128)(2,1)S(1)}, u32[]{:S(2)}, u32[]{:S(2)}) %all-to-all-start) | async-done | bytes 1048608 | tf_op jit(solution)/shard_map/all_to_all | solution.py:30
  27.4 3.4 %fusion.18 = bf16[256,896]{1,0:T(8,128)(2,1)S(1)} fusion(bf16[256,2048]{1,0:T(8,128)(2,1)S(1)} %bitcast.124, bf16[896,2048]{1,0:T(8,128)(2,1)} %collective-permute-done, pred[]{:T(512)S(6)} %eq.80, bf16[1,896,2048]{2,1,0:T(8,128)(2,1)} %param.14), kind=kOutput, calls=%fused_computation.16 | convolution fusion | flops 941588480 | bytes 8847361 | tf_op jit(solution)/shard_map/up_1/dot_general | solution.py:11
  30.8 1.7 %collective-permute-start.1 = (bf16[64,896]{1,0:T(8,128)(2,1)S(1)}, bf16[64,896]{1,0:T(8,128)(2,1)S(1)}, u32[]{:S(2)}, u32[]{:S(2)}) collective-permute-start(bf16[64,896]{1,0:T(8,128)(2,1)S(1)} %get-tuple-element.17), channel_id=1, source_target_pairs={{0,1},{1,2},{2,3},{3,0},{4,5},{5,6},{6,7},{7,4},{8,9},{9,10},{10,1... | collective-permute-start | bytes 344072 | tf_op jit(solution)/shard_map/up_1/ppermute | solution.py:22
  32.5 3.3 %collective-permute-start.2 = (bf16[64,896]{1,0:T(8,128)(2,1)S(1)}, bf16[64,896]{1,0:T(8,128)(2,1)S(1)}, u32[]{:S(2)}, u32[]{:S(2)}) collective-permute-start(bf16[64,896]{1,0:T(8,128)(2,1)S(1)} %get-tuple-element.19), channel_id=1, source_target_pairs={{0,2},{1,3},{2,0},{3,1},{4,6},{5,7},{6,4},{7,5},{8,10},{9,11},{10,... | collective-permute-start | bytes 344072 | tf_op jit(solution)/shard_map/up_1/ppermute | solution.py:22
  36.7 4.2 %collective-permute-start.10 = (bf16[80,2048]{1,0:T(8,128)(2,1)S(1)}, bf16[80,2048]{1,0:T(8,128)(2,1)}, u32[]{:S(2)}, u32[]{:S(2)}) collective-permute-start(bf16[80,2048]{1,0:T(8,128)(2,1)S(1)} %pad_maximum_fusion), channel_id=1, source_target_pairs={{0,64},{64,0},{1,65},{65,1},{2,66},{66,2},{3,67},{67,3},{4,68},{68... | collective-permute-start | bytes 983048 | tf_op jit(solution)/shard_map/ppermute | solution.py:17
  48.3 4.4 %fusion.12 = bf16[256,2048]{1,0:T(8,128)(2,1)} fusion(bf16[256,896]{1,0:T(8,128)(2,1)S(1)} %constant_dynamic-update-slice_fusion.8, bf16[2048,896]{1,0:T(8,128)(2,1)} %collective-permute-done.9, pred[]{:T(512)S(6)} %eq.80, bf16[1,2048,896]{2,1,0:T(8,128)(2,1)} %param.15), kind=kOutput, calls=%fused_computation.12 | convolution fusion | flops 941883392 | bytes 8847361 | tf_op jit(solution)/shard_map/low_1/dot_general | solution.py:11
  52.7 4.8 %all-to-all-start.1 = ((bf16[16,16,2048]{2,1,0:T(8,128)(2,1)}), bf16[16,16,2048]{2,1,0:T(8,128)(2,1)S(1)}, u32[]{:S(2)}, u32[]{:S(2)}) async-start(bf16[16,16,2048]{2,1,0:T(8,128)(2,1)} %bitcast.18), calls=%async_computation.1 | async-start | bytes 2097152 | tf_op jit(solution)/shard_map/low_1/all_to_all | solution.py:36
  58.9 5.4 %collective-permute-start.5 = (bf16[80,64]{1,0:T(8,128)(2,1)S(1)}, bf16[80,64]{1,0:T(8,128)(2,1)S(1)}, u32[]{:S(2)}, u32[]{:S(2)}) collective-permute-start(bf16[80,64]{1,0:T(8,128)(2,1)S(1)} %pad_maximum_fusion.5), channel_id=1, source_target_pairs={{0,64},{64,0},{1,65},{65,1},{2,66},{66,2},{3,67},{67,3},{4,68},{68... | collective-permute-start | bytes 30728 | tf_op jit(solution)/shard_map/ppermute | solution.py:17
  65.1 5.2 %all-to-all-done.1 = bf16[16,16,2048]{2,1,0:T(8,128)(2,1)S(1)} async-done(((bf16[16,16,2048]{2,1,0:T(8,128)(2,1)}), bf16[16,16,2048]{2,1,0:T(8,128)(2,1)S(1)}, u32[]{:S(2)}, u32[]{:S(2)}) %all-to-all-start.1) | async-done | bytes 1048608 | tf_op jit(solution)/shard_map/low_1/all_to_all | solution.py:36
  72.5 3.8 %all-to-all-start.2 = ((bf16[16,16,2048]{2,1,0:T(8,128)(2,1)}), bf16[16,16,2048]{2,1,0:T(8,128)(2,1)S(1)}, u32[]{:S(2)}, u32[]{:S(2)}) async-start(bf16[16,16,2048]{2,1,0:T(8,128)(2,1)} %broadcast_in_dim.78), calls=%async_computation.2 | async-start | bytes 2097152 | tf_op jit(solution)/shard_map/low_1/all_to_all | solution.py:30
  79.0 2.9 %collective-permute-start.15 = (bf16[16,256]{1,0:T(8,128)(2,1)S(1)}, bf16[16,256]{1,0:T(8,128)(2,1)S(1)}, u32[]{:S(2)}, u32[]{:S(2)}) collective-permute-start(bf16[16,256]{1,0:T(8,128)(2,1)S(1)} %pad_maximum_fusion.6), channel_id=1, source_target_pairs={{0,2},{1,3},{2,0},{3,1},{4,6},{5,7},{6,4},{7,5},{8,10},{9,11},{10,... | collective-permute-start | bytes 24584 | tf_op jit(solution)/shard_map/up_0/ppermute | solution.py:22
  81.8 1.6 %collective-permute-start.16 = (bf16[16,256]{1,0:T(8,128)(2,1)S(1)}, bf16[16,256]{1,0:T(8,128)(2,1)S(1)}, u32[]{:S(2)}, u32[]{:S(2)}) collective-permute-start(bf16[16,256]{1,0:T(8,128)(2,1)S(1)} %pad_maximum_fusion.6), channel_id=1, source_target_pairs={{0,3},{1,0},{2,1},{3,2},{4,7},{5,4},{6,5},{7,6},{8,11},{9,8},{10,9... | collective-permute-start | bytes 24584 | tf_op jit(solution)/shard_map/up_0/ppermute | solution.py:22
  83.5 5.4 %all-to-all-done.2 = bf16[16,16,2048]{2,1,0:T(8,128)(2,1)S(1)} async-done(((bf16[16,16,2048]{2,1,0:T(8,128)(2,1)}), bf16[16,16,2048]{2,1,0:T(8,128)(2,1)S(1)}, u32[]{:S(2)}, u32[]{:S(2)}) %all-to-all-start.2) | async-done | bytes 1048608 | tf_op jit(solution)/shard_map/low_1/all_to_all | solution.py:30
  88.9 4.4 %fusion.21 = bf16[256,896]{1,0:T(8,128)(2,1)S(1)} fusion(bf16[256,2048]{1,0:T(8,128)(2,1)S(1)} %bitcast.125, bf16[896,2048]{1,0:T(8,128)(2,1)} %collective-permute-done, pred[]{:T(512)S(6)} %eq.79, bf16[1,896,2048]{2,1,0:T(8,128)(2,1)} %param.14), kind=kOutput, calls=%fused_computation.17 | convolution fusion | flops 941588480 | bytes 8847361 | tf_op jit(solution)/shard_map/up_0/dot_general | solution.py:11
  93.5 2.8 %collective-permute-start.12 = (bf16[64,896]{1,0:T(8,128)(2,1)S(1)}, bf16[64,896]{1,0:T(8,128)(2,1)S(1)}, u32[]{:S(2)}, u32[]{:S(2)}) collective-permute-start(bf16[64,896]{1,0:T(8,128)(2,1)S(1)} %get-tuple-element.16), channel_id=1, source_target_pairs={{0,2},{1,3},{2,0},{3,1},{4,6},{5,7},{6,4},{7,5},{8,10},{9,11},{10,... | collective-permute-start | bytes 344072 | tf_op jit(solution)/shard_map/up_0/ppermute | solution.py:22
  101.8 2.2 %collective-permute-start.18 = (bf16[64,896]{1,0:T(8,128)(2,1)S(1)}, bf16[64,896]{1,0:T(8,128)(2,1)S(1)}, u32[]{:S(2)}, u32[]{:S(2)}) collective-permute-start(bf16[64,896]{1,0:T(8,128)(2,1)S(1)} %get-tuple-element.39), channel_id=1, source_target_pairs={{0,2},{1,3},{2,0},{3,1},{4,6},{5,7},{6,4},{7,5},{8,10},{9,11},{10,... | collective-permute-start | bytes 344072 | tf_op jit(solution)/shard_map/low_0/ppermute | solution.py:22
  105.9 4.3 %all-to-all-start.3 = ((bf16[16,80,256]{2,1,0:T(8,128)(2,1)}), bf16[16,80,256]{2,1,0:T(8,128)(2,1)S(1)}, u32[]{:S(2)}, u32[]{:S(2)}) async-start(bf16[16,80,256]{2,1,0:T(8,128)(2,1)} %broadcast_in_dim.79), calls=%async_computation.3 | async-start | bytes 1310720 | tf_op jit(solution)/shard_map/low_0/all_to_all | solution.py:30
  110.3 5.4 %fusion.15 = bf16[256,2048]{1,0:T(8,128)(2,1)} fusion(bf16[256,896]{1,0:T(8,128)(2,1)S(1)} %constant_dynamic-update-slice_fusion.4, bf16[2048,896]{1,0:T(8,128)(2,1)} %collective-permute-done.9, pred[]{:T(512)S(6)} %eq.79, bf16[1,2048,896]{2,1,0:T(8,128)(2,1)} %param.15), kind=kOutput, calls=%fused_computation.13 | convolution fusion | flops 941883392 | bytes 8847361 | tf_op jit(solution)/shard_map/low_0/dot_general | solution.py:11
  115.7 4.1 %all-to-all-done.3 = bf16[16,80,256]{2,1,0:T(8,128)(2,1)S(1)} async-done(((bf16[16,80,256]{2,1,0:T(8,128)(2,1)}), bf16[16,80,256]{2,1,0:T(8,128)(2,1)S(1)}, u32[]{:S(2)}, u32[]{:S(2)}) %all-to-all-start.3) | async-done | bytes 655392 | tf_op jit(solution)/shard_map/low_0/all_to_all | solution.py:30
  121.2 1.8 %collective-permute-start.22 = (bf16[64,256]{1,0:T(8,128)(2,1)S(1)}, bf16[64,256]{1,0:T(8,128)(2,1)S(1)}, u32[]{:S(2)}, u32[]{:S(2)}) collective-permute-start(bf16[64,256]{1,0:T(8,128)(2,1)S(1)} %slice_reduce_fusion), channel_id=1, source_target_pairs={{0,3},{1,0},{2,1},{3,2},{4,7},{5,4},{6,5},{7,6},{8,11},{9,8},{10,9... | collective-permute-start | bytes 98312 | tf_op jit(solution)/shard_map/outputs/ppermute | solution.py:22
  123.1 3.7 %all-to-all-start.4 = ((bf16[16,16,2048]{2,1,0:T(8,128)(2,1)}), bf16[16,16,2048]{2,1,0:T(8,128)(2,1)S(1)}, u32[]{:S(2)}, u32[]{:S(2)}) async-start(bf16[16,16,2048]{2,1,0:T(8,128)(2,1)} %bitcast.26), calls=%async_computation.4 | async-start | bytes 2097152 | tf_op jit(solution)/shard_map/low_0/all_to_all | solution.py:36
  127.2 11.7 %all-to-all-done.4 = bf16[16,16,2048]{2,1,0:T(8,128)(2,1)S(1)} async-done(((bf16[16,16,2048]{2,1,0:T(8,128)(2,1)}), bf16[16,16,2048]{2,1,0:T(8,128)(2,1)S(1)}, u32[]{:S(2)}, u32[]{:S(2)}) %all-to-all-start.4) | async-done | bytes 1048608 | tf_op jit(solution)/shard_map/low_0/all_to_all | solution.py:36
  139.9 12.7 %collective-permute-start.23 = (bf16[16,2048]{1,0:T(8,128)(2,1)S(1)}, bf16[16,2048]{1,0:T(8,128)(2,1)S(1)}, u32[]{:S(2)}, u32[]{:S(2)}) collective-permute-start(bf16[16,2048]{1,0:T(8,128)(2,1)S(1)} %broadcast_select_fusion.2), channel_id=1, source_target_pairs={{0,64},{64,0},{1,65},{65,1},{2,66},{66,2},{3,67},{67,3},{4,68},{68... | collective-permute-start | bytes 196616 | tf_op jit(solution)/shard_map/outputs/ppermute | solution.py:17
  (130 shorter events, 34.2 us)
Async XLA Ops:
  0.7 26.7 %collective-permute-start = (bf16[896,2048]{1,0:T(8,128)(2,1)}, bf16[896,2048]{1,0:T(8,128)(2,1)}, u32[]{:S(2)}, u32[]{:S(2)}) collective-permute-start(bf16[896,2048]{1,0:T(8,128)(2,1)} %bitcast.151), channel_id=1, source_target_pairs={{0,64},{64,0},{1,65},{65,1},{2,66},{66,2},{3,67},{67,3},{4,68},{68... | collective-permute-start | bytes 11010056 | tf_op jit(solution)/shard_map/ppermute | solution.py:17
  2.2 46.1 %collective-permute-start.9 = (bf16[2048,896]{1,0:T(8,128)(2,1)}, bf16[2048,896]{1,0:T(8,128)(2,1)}, u32[]{:S(2)}, u32[]{:S(2)}) collective-permute-start(bf16[2048,896]{1,0:T(8,128)(2,1)} %bitcast.152), channel_id=1, source_target_pairs={{0,64},{64,0},{1,65},{65,1},{2,66},{66,2},{3,67},{67,3},{4,68},{68... | collective-permute-start | bytes 11010056 | tf_op jit(solution)/shard_map/ppermute | solution.py:17
  4.3 23.1 %all-to-all-start = ((bf16[16,16,2048]{2,1,0:T(8,128)(2,1)}), bf16[16,16,2048]{2,1,0:T(8,128)(2,1)S(1)}, u32[]{:S(2)}, u32[]{:S(2)}) async-start(bf16[16,16,2048]{2,1,0:T(8,128)(2,1)} %broadcast_in_dim.77), calls=%async_computation | async-start | bytes 2097152 | tf_op jit(solution)/shard_map/all_to_all | solution.py:30
  12.1 24.5 %collective-permute-start.4 = (bf16[128,896]{1,0:T(8,128)(2,1)S(1)}, bf16[128,896]{1,0:T(8,128)(2,1)S(1)}, u32[]{:S(2)}, u32[]{:S(2)}) collective-permute-start(bf16[128,896]{1,0:T(8,128)(2,1)S(1)} %pad_maximum_fusion.2), channel_id=1, source_target_pairs={{0,64},{64,0},{1,65},{65,1},{2,66},{66,2},{3,67},{67,3},{4,68},{68... | collective-permute-start | bytes 688136 | tf_op jit(solution)/shard_map/ppermute | solution.py:17
  30.8 10.1 %collective-permute-start.1 = (bf16[64,896]{1,0:T(8,128)(2,1)S(1)}, bf16[64,896]{1,0:T(8,128)(2,1)S(1)}, u32[]{:S(2)}, u32[]{:S(2)}) collective-permute-start(bf16[64,896]{1,0:T(8,128)(2,1)S(1)} %get-tuple-element.17), channel_id=1, source_target_pairs={{0,1},{1,2},{2,3},{3,0},{4,5},{5,6},{6,7},{7,4},{8,9},{9,10},{10,1... | collective-permute-start | bytes 344072 | tf_op jit(solution)/shard_map/up_1/ppermute | solution.py:22
  32.5 8.4 %collective-permute-start.2 = (bf16[64,896]{1,0:T(8,128)(2,1)S(1)}, bf16[64,896]{1,0:T(8,128)(2,1)S(1)}, u32[]{:S(2)}, u32[]{:S(2)}) collective-permute-start(bf16[64,896]{1,0:T(8,128)(2,1)S(1)} %get-tuple-element.19), channel_id=1, source_target_pairs={{0,2},{1,3},{2,0},{3,1},{4,6},{5,7},{6,4},{7,5},{8,10},{9,11},{10,... | collective-permute-start | bytes 344072 | tf_op jit(solution)/shard_map/up_1/ppermute | solution.py:22
  36.7 33.8 %collective-permute-start.10 = (bf16[80,2048]{1,0:T(8,128)(2,1)S(1)}, bf16[80,2048]{1,0:T(8,128)(2,1)}, u32[]{:S(2)}, u32[]{:S(2)}) collective-permute-start(bf16[80,2048]{1,0:T(8,128)(2,1)S(1)} %pad_maximum_fusion), channel_id=1, source_target_pairs={{0,64},{64,0},{1,65},{65,1},{2,66},{66,2},{3,67},{67,3},{4,68},{68... | collective-permute-start | bytes 983048 | tf_op jit(solution)/shard_map/ppermute | solution.py:17
  42.2 5.2 %collective-permute-start.7 = (bf16[64,896]{1,0:T(8,128)(2,1)S(1)}, bf16[64,896]{1,0:T(8,128)(2,1)S(1)}, u32[]{:S(2)}, u32[]{:S(2)}) collective-permute-start(bf16[64,896]{1,0:T(8,128)(2,1)S(1)} %get-tuple-element.37), channel_id=1, source_target_pairs={{0,2},{1,3},{2,0},{3,1},{4,6},{5,7},{6,4},{7,5},{8,10},{9,11},{10,... | collective-permute-start | bytes 344072 | tf_op jit(solution)/shard_map/low_1/ppermute | solution.py:22
  52.7 17.6 %all-to-all-start.1 = ((bf16[16,16,2048]{2,1,0:T(8,128)(2,1)}), bf16[16,16,2048]{2,1,0:T(8,128)(2,1)S(1)}, u32[]{:S(2)}, u32[]{:S(2)}) async-start(bf16[16,16,2048]{2,1,0:T(8,128)(2,1)} %bitcast.18), calls=%async_computation.1 | async-start | bytes 2097152 | tf_op jit(solution)/shard_map/low_1/all_to_all | solution.py:36
  58.9 6.2 %collective-permute-start.5 = (bf16[80,64]{1,0:T(8,128)(2,1)S(1)}, bf16[80,64]{1,0:T(8,128)(2,1)S(1)}, u32[]{:S(2)}, u32[]{:S(2)}) collective-permute-start(bf16[80,64]{1,0:T(8,128)(2,1)S(1)} %pad_maximum_fusion.5), channel_id=1, source_target_pairs={{0,64},{64,0},{1,65},{65,1},{2,66},{66,2},{3,67},{67,3},{4,68},{68... | collective-permute-start | bytes 30728 | tf_op jit(solution)/shard_map/ppermute | solution.py:17
  72.5 16.3 %all-to-all-start.2 = ((bf16[16,16,2048]{2,1,0:T(8,128)(2,1)}), bf16[16,16,2048]{2,1,0:T(8,128)(2,1)S(1)}, u32[]{:S(2)}, u32[]{:S(2)}) async-start(bf16[16,16,2048]{2,1,0:T(8,128)(2,1)} %broadcast_in_dim.78), calls=%async_computation.2 | async-start | bytes 2097152 | tf_op jit(solution)/shard_map/low_1/all_to_all | solution.py:30
  78.9 17.4 %collective-permute-start.14 = (bf16[16,256]{1,0:T(8,128)(2,1)S(1)}, bf16[16,256]{1,0:T(8,128)(2,1)S(1)}, u32[]{:S(2)}, u32[]{:S(2)}) collective-permute-start(bf16[16,256]{1,0:T(8,128)(2,1)S(1)} %pad_maximum_fusion.6), channel_id=1, source_target_pairs={{0,1},{1,2},{2,3},{3,0},{4,5},{5,6},{6,7},{7,4},{8,9},{9,10},{10,1... | collective-permute-start | bytes 24584 | tf_op jit(solution)/shard_map/up_0/ppermute | solution.py:22
  79.0 18.8 %collective-permute-start.15 = (bf16[16,256]{1,0:T(8,128)(2,1)S(1)}, bf16[16,256]{1,0:T(8,128)(2,1)S(1)}, u32[]{:S(2)}, u32[]{:S(2)}) collective-permute-start(bf16[16,256]{1,0:T(8,128)(2,1)S(1)} %pad_maximum_fusion.6), channel_id=1, source_target_pairs={{0,2},{1,3},{2,0},{3,1},{4,6},{5,7},{6,4},{7,5},{8,10},{9,11},{10,... | collective-permute-start | bytes 24584 | tf_op jit(solution)/shard_map/up_0/ppermute | solution.py:22
  81.8 15.9 %collective-permute-start.16 = (bf16[16,256]{1,0:T(8,128)(2,1)S(1)}, bf16[16,256]{1,0:T(8,128)(2,1)S(1)}, u32[]{:S(2)}, u32[]{:S(2)}) collective-permute-start(bf16[16,256]{1,0:T(8,128)(2,1)S(1)} %pad_maximum_fusion.6), channel_id=1, source_target_pairs={{0,3},{1,0},{2,1},{3,2},{4,7},{5,4},{6,5},{7,6},{8,11},{9,8},{10,9... | collective-permute-start | bytes 24584 | tf_op jit(solution)/shard_map/up_0/ppermute | solution.py:22
  93.5 6.2 %collective-permute-start.12 = (bf16[64,896]{1,0:T(8,128)(2,1)S(1)}, bf16[64,896]{1,0:T(8,128)(2,1)S(1)}, u32[]{:S(2)}, u32[]{:S(2)}) collective-permute-start(bf16[64,896]{1,0:T(8,128)(2,1)S(1)} %get-tuple-element.16), channel_id=1, source_target_pairs={{0,2},{1,3},{2,0},{3,1},{4,6},{5,7},{6,4},{7,5},{8,10},{9,11},{10,... | collective-permute-start | bytes 344072 | tf_op jit(solution)/shard_map/up_0/ppermute | solution.py:22
  100.3 9.9 %collective-permute-start.17 = (bf16[64,896]{1,0:T(8,128)(2,1)S(1)}, bf16[64,896]{1,0:T(8,128)(2,1)S(1)}, u32[]{:S(2)}, u32[]{:S(2)}) collective-permute-start(bf16[64,896]{1,0:T(8,128)(2,1)S(1)} %get-tuple-element.39), channel_id=1, source_target_pairs={{0,1},{1,2},{2,3},{3,0},{4,5},{5,6},{6,7},{7,4},{8,9},{9,10},{10,1... | collective-permute-start | bytes 344072 | tf_op jit(solution)/shard_map/low_0/ppermute | solution.py:22
  101.8 8.4 %collective-permute-start.18 = (bf16[64,896]{1,0:T(8,128)(2,1)S(1)}, bf16[64,896]{1,0:T(8,128)(2,1)S(1)}, u32[]{:S(2)}, u32[]{:S(2)}) collective-permute-start(bf16[64,896]{1,0:T(8,128)(2,1)S(1)} %get-tuple-element.39), channel_id=1, source_target_pairs={{0,2},{1,3},{2,0},{3,1},{4,6},{5,7},{6,4},{7,5},{8,10},{9,11},{10,... | collective-permute-start | bytes 344072 | tf_op jit(solution)/shard_map/low_0/ppermute | solution.py:22
  104.0 6.2 %collective-permute-start.19 = (bf16[64,896]{1,0:T(8,128)(2,1)S(1)}, bf16[64,896]{1,0:T(8,128)(2,1)S(1)}, u32[]{:S(2)}, u32[]{:S(2)}) collective-permute-start(bf16[64,896]{1,0:T(8,128)(2,1)S(1)} %get-tuple-element.39), channel_id=1, source_target_pairs={{0,3},{1,0},{2,1},{3,2},{4,7},{5,4},{6,5},{7,6},{8,11},{9,8},{10,9... | collective-permute-start | bytes 344072 | tf_op jit(solution)/shard_map/low_0/ppermute | solution.py:22
  105.9 14.0 %all-to-all-start.3 = ((bf16[16,80,256]{2,1,0:T(8,128)(2,1)}), bf16[16,80,256]{2,1,0:T(8,128)(2,1)S(1)}, u32[]{:S(2)}, u32[]{:S(2)}) async-start(bf16[16,80,256]{2,1,0:T(8,128)(2,1)} %broadcast_in_dim.79), calls=%async_computation.3 | async-start | bytes 1310720 | tf_op jit(solution)/shard_map/low_0/all_to_all | solution.py:30
  120.0 6.9 %collective-permute-start.20 = (bf16[64,256]{1,0:T(8,128)(2,1)S(1)}, bf16[64,256]{1,0:T(8,128)(2,1)S(1)}, u32[]{:S(2)}, u32[]{:S(2)}) collective-permute-start(bf16[64,256]{1,0:T(8,128)(2,1)S(1)} %slice_reduce_fusion), channel_id=1, source_target_pairs={{0,1},{1,2},{2,3},{3,0},{4,5},{5,6},{6,7},{7,4},{8,9},{9,10},{10,1... | collective-permute-start | bytes 98312 | tf_op jit(solution)/shard_map/outputs/ppermute | solution.py:22
  120.6 6.3 %collective-permute-start.21 = (bf16[64,256]{1,0:T(8,128)(2,1)S(1)}, bf16[64,256]{1,0:T(8,128)(2,1)S(1)}, u32[]{:S(2)}, u32[]{:S(2)}) collective-permute-start(bf16[64,256]{1,0:T(8,128)(2,1)S(1)} %slice_reduce_fusion), channel_id=1, source_target_pairs={{0,2},{1,3},{2,0},{3,1},{4,6},{5,7},{6,4},{7,5},{8,10},{9,11},{10,... | collective-permute-start | bytes 98312 | tf_op jit(solution)/shard_map/outputs/ppermute | solution.py:22
  121.2 5.7 %collective-permute-start.22 = (bf16[64,256]{1,0:T(8,128)(2,1)S(1)}, bf16[64,256]{1,0:T(8,128)(2,1)S(1)}, u32[]{:S(2)}, u32[]{:S(2)}) collective-permute-start(bf16[64,256]{1,0:T(8,128)(2,1)S(1)} %slice_reduce_fusion), channel_id=1, source_target_pairs={{0,3},{1,0},{2,1},{3,2},{4,7},{5,4},{6,5},{7,6},{8,11},{9,8},{10,9... | collective-permute-start | bytes 98312 | tf_op jit(solution)/shard_map/outputs/ppermute | solution.py:22
  123.1 15.8 %all-to-all-start.4 = ((bf16[16,16,2048]{2,1,0:T(8,128)(2,1)}), bf16[16,16,2048]{2,1,0:T(8,128)(2,1)S(1)}, u32[]{:S(2)}, u32[]{:S(2)}) async-start(bf16[16,16,2048]{2,1,0:T(8,128)(2,1)} %bitcast.26), calls=%async_computation.4 | async-start | bytes 2097152 | tf_op jit(solution)/shard_map/low_0/all_to_all | solution.py:36
  139.9 13.6 %collective-permute-start.23 = (bf16[16,2048]{1,0:T(8,128)(2,1)S(1)}, bf16[16,2048]{1,0:T(8,128)(2,1)S(1)}, u32[]{:S(2)}, u32[]{:S(2)}) collective-permute-start(bf16[16,2048]{1,0:T(8,128)(2,1)S(1)} %broadcast_select_fusion.2), channel_id=1, source_target_pairs={{0,64},{64,0},{1,65},{65,1},{2,66},{66,2},{3,67},{67,3},{4,68},{68... | collective-permute-start | bytes 196616 | tf_op jit(solution)/shard_map/outputs/ppermute | solution.py:17
  (17 other events, 227.5 us)

commit v5 on v4

--- a/solution.py
+++ b/solution.py
@@ -123,7 +123,7 @@
     mp_index = lax.axis_index("mp")
     tokens_mp = upper_deriv.shape[1]
 
-    grad, _ = halves(out_grad)
+    grad = jnp.where(core == 0, out_grad[:half], out_grad[half:])
     gathered = gather_dp(grad)
 
     deriv_up, deriv_up_sent = halves(upper_deriv[0])
@@ -153,6 +153,7 @@
     weight_low = (lower_w[0], swap_sections(lower_w[0]))
 
     last = sections - 1
+    scales_low = held(*[of_section(deriv_low, s).astype(F32) for s in range(sections)])
     grads = [None] * sections
     ups = []
     lows = []
@@ -165,6 +166,9 @@
                 up = from_all_mp(jnp.concatenate(ups, axis=1))
                 up = sum(part.astype(F32) for part in up).astype(BF16)
             weight = of_section(weight_up, section)
+            weight_last = of_section(weight_low, section)
+            if section == last:
+                weight, weight_last, gathered = held(weight, weight_last, gathered)
             summed = scatter_sum_mp(times_t(gathered, weight).astype(BF16))
             scale = of_section(deriv_up, section).astype(F32)
             middle = (summed * scale).astype(BF16)
@@ -182,13 +186,11 @@
                 up = both[:, rows:].reshape(tokens // sections, up.shape[1])
 
             middle_all = gather_mp(middle)
-            weight = of_section(weight_low, section)
-            partial = times_t(middle_all, weight).astype(BF16)
+            partial = times_t(middle_all, weight_last).astype(BF16)
             if section == 0:
                 low, up, partial = held(low, up, partial)
             summed = scatter_sum_dp(partial)
-            scale = of_section(deriv_low, section).astype(F32)
-            grad = (summed * scale).astype(BF16)
+            grad = (summed * scales_low[section]).astype(BF16)
             grads[section] = grad
             if section > 0:
                 gathered = gather_dp(grad)

time: 157 us -> 156 us (level)
  starting transfers between devices: 73.6 us -> 60.1 us
  other arithmetic: 4.6 us -> 11.4 us
  waiting for transfers between devices: 48.2 us -> 54.5 us
    ppermute x7, starting transfers between devices: 24.7 us -> 12.8 us  [swap_sections(): return lax.ppermute(block, 'section', [(0, 1), (1, 0)])]
    select_n x2 -> x4, other arithmetic: 0.02 us -> 6.81 us  [of_section(): return jnp.where(core == section, own, received)]
    all_to_all x2, waiting for transfers between devices: 16.9 us -> 22.6 us  [scatter_sum_dp(): got = lax.all_to_all(partial, 'dp', 0, 0, tiled=True)]
    ppermute x18, waiting for transfers between devices: 5.81 us -> 10.8 us  [shift_mp(): lax.ppermute(block, 'mp', [(i, (i + distance) % count) for i in range(cou...]
    all_to_all x3, waiting for transfers between devices: 24 us -> 19.6 us  [gather_dp(): got = lax.all_to_all(copies, 'dp', 0, 0, tiled=True)]
    ppermute x18, starting transfers between devices: 25.5 us -> 22.1 us  [shift_mp(): lax.ppermute(block, 'mp', [(i, (i + distance) % count) for i in range(cou...]
    all_to_all x2, starting transfers between devices: 8.49 us -> 10.4 us  [scatter_sum_dp(): got = lax.all_to_all(partial, 'dp', 0, 0, tiled=True)]
    broadcast_in_dim x4 -> x3, local copies, waits for them, and re-layouts: 4.08 us -> 3.2 us  [gather_dp(): copies = jnp.broadcast_to(block[None], (count,) + block.shape)]
  transfers between devices with their start and end apart: 30 -> 30, of which waited for: 13 -> 13; matrix products, arithmetic and copies ran while one was open for 18% -> 23% of each run, Pallas kernels for 0% -> 0%
where the time goes in v5:
time: 156 us; the launch traced here: 155 us
  starting transfers between devices  60.1 us (39%)
  waiting for transfers between devices  54.5 us (35%)
  matrix products  22.1 us (14%)
  other arithmetic  11.4 us (7%)
  local copies, waits for them, and re-layouts  5.38 us (3%)
    all_to_all x2, waiting for transfers between devices, scatter_sum_dp(): got = lax.all_to_all(partial, 'dp', 0, 0, tiled=True)  22.6 us
    ppermute x18, starting transfers between devices, shift_mp(): lax.ppermute(block, 'mp', [(i, (i + distance) % count) for i in range(cou...  22.1 us
    dot_general x10, matrix products, times_t(): lax.dot_general(left, right, (((1,), (1,)), ((), ())), preferred_element_...  21.5 us
    all_to_all x3, waiting for transfers between devices, gather_dp(): got = lax.all_to_all(copies, 'dp', 0, 0, tiled=True)  19.6 us
    all_to_all x3, starting transfers between devices, gather_dp(): got = lax.all_to_all(copies, 'dp', 0, 0, tiled=True)  14.7 us
    ppermute x7, starting transfers between devices, swap_sections(): return lax.ppermute(block, 'section', [(0, 1), (1, 0)])  12.8 us
    ppermute x18, waiting for transfers between devices, shift_mp(): lax.ppermute(block, 'mp', [(i, (i + distance) % count) for i in range(cou...  10.8 us
    all_to_all x2, starting transfers between devices, scatter_sum_dp(): got = lax.all_to_all(partial, 'dp', 0, 0, tiled=True)  10.4 us
  transfers between devices with their start and end apart: 30, of which 13 were waited for; matrix products, arithmetic and copies ran while one was open for 23% of the time, Pallas kernels for 0%

profile of v5, /device:TPU:1, one launch (start us, length us, event | category | flops | bytes accessed | tf_op | source)
XLA Modules:
  0.0 154.8 jit_solution(16276900771698614845)
XLA Ops:
  4.3 6.8 %all-to-all-start = ((bf16[16,16,2048]{2,1,0:T(8,128)(2,1)}), bf16[16,16,2048]{2,1,0:T(8,128)(2,1)S(1)}, u32[]{:S(2)}, u32[]{:S(2)}) async-start(bf16[16,16,2048]{2,1,0:T(8,128)(2,1)} %broadcast_in_dim.75), calls=%async_computation | async-start | bytes 2097152 | tf_op jit(solution)/shard_map/all_to_all | solution.py:30
  14.4 4.5 %broadcast_select_fusion = bf16[2048,896]{1,0:T(8,128)(2,1)} fusion(bf16[2048,896]{1,0:T(8,128)(2,1)} %collective-permute-done.1, pred[]{:T(512)S(6)} %eq.81, bf16[1,2048,896]{2,1,0:T(8,128)(2,1)} %param.15), kind=kLoop, calls=%fused_computation.6 | loop fusion | flops 1835008 | bytes 11010049 | tf_op jit(solution)/shard_map/up_1/jit(_where)/select_n | solution.py:117
  18.9 2.3 %broadcast_select_fusion.1 = bf16[896,2048]{1,0:T(8,128)(2,1)} fusion(bf16[896,2048]{1,0:T(8,128)(2,1)} %collective-permute-done, pred[]{:T(512)S(6)} %eq.81, bf16[1,896,2048]{2,1,0:T(8,128)(2,1)S(1)} %copy-done.1), kind=kLoop, calls=%fused_computation.7 | loop fusion | flops 1835008 | bytes 11010049 | tf_op jit(solution)/shard_map/up_1/jit(_where)/select_n | solution.py:117
  21.2 6.3 %all-to-all-done = bf16[16,16,2048]{2,1,0:T(8,128)(2,1)S(1)} async-done(((bf16[16,16,2048]{2,1,0:T(8,128)(2,1)}), bf16[16,16,2048]{2,1,0:T(8,128)(2,1)S(1)}, u32[]{:S(2)}, u32[]{:S(2)}) %all-to-all-start) | async-done | bytes 1048608 | tf_op jit(solution)/shard_map/all_to_all | solution.py:30
  27.4 3.3 %convolution_convert_fusion.1 = bf16[256,896]{1,0:T(8,128)(2,1)S(1)} fusion(bf16[256,2048]{1,0:T(8,128)(2,1)S(1)} %bitcast.119, bf16[896,2048]{1,0:T(8,128)(2,1)} %broadcast_select_fusion.1), kind=kOutput, calls=%fused_computation.13 | convolution fusion | flops 939753472 | bytes 5177344 | tf_op jit(solution)/shard_map/up_1/dot_general | solution.py:11
  32.5 3.3 %collective-permute-start.3 = (bf16[64,896]{1,0:T(8,128)(2,1)S(1)}, bf16[64,896]{1,0:T(8,128)(2,1)S(1)}, u32[]{:S(2)}, u32[]{:S(2)}) collective-permute-start(bf16[64,896]{1,0:T(8,128)(2,1)S(1)} %get-tuple-element.31), channel_id=1, source_target_pairs={{0,2},{1,3},{2,0},{3,1},{4,6},{5,7},{6,4},{7,5},{8,10},{9,11},{10,... | collective-permute-start | bytes 344072 | tf_op jit(solution)/shard_map/up_1/ppermute | solution.py:22
  36.8 2.5 %collective-permute-done.3 = bf16[64,896]{1,0:T(8,128)(2,1)S(1)} collective-permute-done((bf16[64,896]{1,0:T(8,128)(2,1)S(1)}, bf16[64,896]{1,0:T(8,128)(2,1)S(1)}, u32[]{:S(2)}, u32[]{:S(2)}) %collective-permute-start.3) | collective-permute-done | bytes 114720 | tf_op jit(solution)/shard_map/up_1/ppermute | solution.py:22
  40.8 2.6 %collective-permute-start.8 = (bf16[64,896]{1,0:T(8,128)(2,1)S(1)}, bf16[64,896]{1,0:T(8,128)(2,1)S(1)}, u32[]{:S(2)}, u32[]{:S(2)}) collective-permute-start(bf16[64,896]{1,0:T(8,128)(2,1)S(1)} %get-tuple-element.49), channel_id=1, source_target_pairs={{0,2},{1,3},{2,0},{3,1},{4,6},{5,7},{6,4},{7,5},{8,10},{9,11},{10,... | collective-permute-start | bytes 344072 | tf_op jit(solution)/shard_map/low_1/ppermute | solution.py:22
  44.2 2.5 %collective-permute-done.7 = bf16[64,896]{1,0:T(8,128)(2,1)S(1)} collective-permute-done((bf16[64,896]{1,0:T(8,128)(2,1)S(1)}, bf16[64,896]{1,0:T(8,128)(2,1)S(1)}, u32[]{:S(2)}, u32[]{:S(2)}) %collective-permute-start.7) | collective-permute-done | bytes 114720 | tf_op jit(solution)/shard_map/low_1/ppermute | solution.py:22
  47.5 4.3 %convolution_convert_fusion = bf16[256,2048]{1,0:T(8,128)(2,1)} fusion(bf16[256,896]{1,0:T(8,128)(2,1)S(1)} %constant_dynamic-update-slice_fusion.8, bf16[2048,896]{1,0:T(8,128)(2,1)} %broadcast_select_fusion), kind=kOutput, calls=%fused_computation.9 | convolution fusion | flops 940048384 | bytes 5177344 | tf_op jit(solution)/shard_map/low_1/dot_general | solution.py:11
  51.8 6.8 %all-to-all-start.1 = ((bf16[16,16,2048]{2,1,0:T(8,128)(2,1)}), bf16[16,16,2048]{2,1,0:T(8,128)(2,1)S(1)}, u32[]{:S(2)}, u32[]{:S(2)}) async-start(bf16[16,16,2048]{2,1,0:T(8,128)(2,1)} %bitcast.16), calls=%async_computation.1 | async-start | bytes 2097152 | tf_op jit(solution)/shard_map/low_1/all_to_all | solution.py:36
  58.6 2.4 %collective-permute-start.6 = (bf16[80,64]{1,0:T(8,128)(2,1)S(1)}, bf16[80,64]{1,0:T(8,128)(2,1)S(1)}, u32[]{:S(2)}, u32[]{:S(2)}) collective-permute-start(bf16[80,64]{1,0:T(8,128)(2,1)S(1)} %pad_maximum_fusion.5), channel_id=1, source_target_pairs={{0,64},{64,0},{1,65},{65,1},{2,66},{66,2},{3,67},{67,3},{4,68},{68... | collective-permute-start | bytes 30728 | tf_op jit(solution)/shard_map/ppermute | solution.py:17
  62.8 10.8 %all-to-all-done.1 = bf16[16,16,2048]{2,1,0:T(8,128)(2,1)S(1)} async-done(((bf16[16,16,2048]{2,1,0:T(8,128)(2,1)}), bf16[16,16,2048]{2,1,0:T(8,128)(2,1)S(1)}, u32[]{:S(2)}, u32[]{:S(2)}) %all-to-all-start.1) | async-done | bytes 1048608 | tf_op jit(solution)/shard_map/low_1/all_to_all | solution.py:36
  74.9 4.1 %all-to-all-start.2 = ((bf16[16,16,2048]{2,1,0:T(8,128)(2,1)}), bf16[16,16,2048]{2,1,0:T(8,128)(2,1)S(1)}, u32[]{:S(2)}, u32[]{:S(2)}) async-start(bf16[16,16,2048]{2,1,0:T(8,128)(2,1)} %broadcast_in_dim.76), calls=%async_computation.2 | async-start | bytes 2097152 | tf_op jit(solution)/shard_map/low_1/all_to_all | solution.py:30
  84.4 9.1 %all-to-all-done.2 = bf16[16,16,2048]{2,1,0:T(8,128)(2,1)S(1)} async-done(((bf16[16,16,2048]{2,1,0:T(8,128)(2,1)}), bf16[16,16,2048]{2,1,0:T(8,128)(2,1)S(1)}, u32[]{:S(2)}, u32[]{:S(2)}) %all-to-all-start.2) | async-done | bytes 1048608 | tf_op jit(solution)/shard_map/low_1/all_to_all | solution.py:30
  93.4 4.5 %fusion.9 = bf16[256,896]{1,0:T(8,128)(2,1)S(1)} fusion(bf16[256,2048]{1,0:T(8,128)(2,1)S(1)} %bitcast.120, bf16[896,2048]{1,0:T(8,128)(2,1)} %collective-permute-done, pred[]{:T(512)S(6)} %eq.80, bf16[1,896,2048]{2,1,0:T(8,128)(2,1)} %param.14), kind=kOutput, calls=%fused_computation.12 | convolution fusion | flops 941588480 | bytes 8847361 | tf_op jit(solution)/shard_map/up_0/dot_general | solution.py:11
  100.7 3.4 %collective-permute-done.11 = bf16[64,896]{1,0:T(8,128)(2,1)S(1)} collective-permute-done((bf16[64,896]{1,0:T(8,128)(2,1)S(1)}, bf16[64,896]{1,0:T(8,128)(2,1)S(1)}, u32[]{:S(2)}, u32[]{:S(2)}) %collective-permute-start.11) | collective-permute-done | bytes 114720 | tf_op jit(solution)/shard_map/up_0/ppermute | solution.py:22
  105.4 2.8 %collective-permute-start.18 = (bf16[64,896]{1,0:T(8,128)(2,1)S(1)}, bf16[64,896]{1,0:T(8,128)(2,1)S(1)}, u32[]{:S(2)}, u32[]{:S(2)}) collective-permute-start(bf16[64,896]{1,0:T(8,128)(2,1)S(1)} %get-tuple-element.51), channel_id=1, source_target_pairs={{0,2},{1,3},{2,0},{3,1},{4,6},{5,7},{6,4},{7,5},{8,10},{9,11},{10,... | collective-permute-start | bytes 344072 | tf_op jit(solution)/shard_map/low_0/ppermute | solution.py:22
  109.4 3.8 %all-to-all-start.3 = ((bf16[16,80,256]{2,1,0:T(8,128)(2,1)}), bf16[16,80,256]{2,1,0:T(8,128)(2,1)S(1)}, u32[]{:S(2)}, u32[]{:S(2)}) async-start(bf16[16,80,256]{2,1,0:T(8,128)(2,1)} %broadcast_in_dim.77), calls=%async_computation.3 | async-start | bytes 1310720 | tf_op jit(solution)/shard_map/low_0/all_to_all | solution.py:30
  113.3 5.4 %fusion.6 = bf16[256,2048]{1,0:T(8,128)(2,1)} fusion(bf16[256,896]{1,0:T(8,128)(2,1)S(1)} %constant_dynamic-update-slice_fusion.4, bf16[2048,896]{1,0:T(8,128)(2,1)} %collective-permute-done.1, pred[]{:T(512)S(6)} %eq.80, bf16[1,2048,896]{2,1,0:T(8,128)(2,1)} %param.15), kind=kOutput, calls=%fused_computation.8 | convolution fusion | flops 941883392 | bytes 8847361 | tf_op jit(solution)/shard_map/low_0/dot_general | solution.py:11
  118.7 4.2 %all-to-all-done.3 = bf16[16,80,256]{2,1,0:T(8,128)(2,1)S(1)} async-done(((bf16[16,80,256]{2,1,0:T(8,128)(2,1)}), bf16[16,80,256]{2,1,0:T(8,128)(2,1)S(1)}, u32[]{:S(2)}, u32[]{:S(2)}) %all-to-all-start.3) | async-done | bytes 655392 | tf_op jit(solution)/shard_map/low_0/all_to_all | solution.py:30
  127.3 3.7 %all-to-all-start.4 = ((bf16[16,16,2048]{2,1,0:T(8,128)(2,1)}), bf16[16,16,2048]{2,1,0:T(8,128)(2,1)S(1)}, u32[]{:S(2)}, u32[]{:S(2)}) async-start(bf16[16,16,2048]{2,1,0:T(8,128)(2,1)} %bitcast.24), calls=%async_computation.4 | async-start | bytes 2097152 | tf_op jit(solution)/shard_map/low_0/all_to_all | solution.py:36
  131.4 11.8 %all-to-all-done.4 = bf16[16,16,2048]{2,1,0:T(8,128)(2,1)S(1)} async-done(((bf16[16,16,2048]{2,1,0:T(8,128)(2,1)}), bf16[16,16,2048]{2,1,0:T(8,128)(2,1)S(1)}, u32[]{:S(2)}, u32[]{:S(2)}) %all-to-all-start.4) | async-done | bytes 1048608 | tf_op jit(solution)/shard_map/low_0/all_to_all | solution.py:36
  143.4 7.8 %collective-permute-start.23 = (bf16[16,2048]{1,0:T(8,128)(2,1)S(1)}, bf16[16,2048]{1,0:T(8,128)(2,1)S(1)}, u32[]{:S(2)}, u32[]{:S(2)}) collective-permute-start(bf16[16,2048]{1,0:T(8,128)(2,1)S(1)} %broadcast_select_fusion.4), channel_id=1, source_target_pairs={{0,64},{64,0},{1,65},{65,1},{2,66},{66,2},{3,67},{67,3},{4,68},{68... | collective-permute-start | bytes 196616 | tf_op jit(solution)/shard_map/outputs/ppermute | solution.py:17
  (135 shorter events, 34.6 us)
Async XLA Ops:
  0.7 13.7 %collective-permute-start.1 = (bf16[2048,896]{1,0:T(8,128)(2,1)}, bf16[2048,896]{1,0:T(8,128)(2,1)}, u32[]{:S(2)}, u32[]{:S(2)}) collective-permute-start(bf16[2048,896]{1,0:T(8,128)(2,1)} %bitcast.118), channel_id=1, source_target_pairs={{0,64},{64,0},{1,65},{65,1},{2,66},{66,2},{3,67},{67,3},{4,68},{68... | collective-permute-start | bytes 11010056 | tf_op jit(solution)/shard_map/ppermute | solution.py:17
  2.2 16.7 %collective-permute-start = (bf16[896,2048]{1,0:T(8,128)(2,1)}, bf16[896,2048]{1,0:T(8,128)(2,1)}, u32[]{:S(2)}, u32[]{:S(2)}) collective-permute-start(bf16[896,2048]{1,0:T(8,128)(2,1)} %bitcast.117), channel_id=1, source_target_pairs={{0,64},{64,0},{1,65},{65,1},{2,66},{66,2},{3,67},{67,3},{4,68},{68... | collective-permute-start | bytes 11010056 | tf_op jit(solution)/shard_map/ppermute | solution.py:17
  4.3 23.1 %all-to-all-start = ((bf16[16,16,2048]{2,1,0:T(8,128)(2,1)}), bf16[16,16,2048]{2,1,0:T(8,128)(2,1)S(1)}, u32[]{:S(2)}, u32[]{:S(2)}) async-start(bf16[16,16,2048]{2,1,0:T(8,128)(2,1)} %broadcast_in_dim.75), calls=%async_computation | async-start | bytes 2097152 | tf_op jit(solution)/shard_map/all_to_all | solution.py:30
  12.2 24.6 %collective-permute-start.5 = (bf16[128,896]{1,0:T(8,128)(2,1)S(1)}, bf16[128,896]{1,0:T(8,128)(2,1)S(1)}, u32[]{:S(2)}, u32[]{:S(2)}) collective-permute-start(bf16[128,896]{1,0:T(8,128)(2,1)S(1)} %pad_maximum_fusion.2), channel_id=1, source_target_pairs={{0,64},{64,0},{1,65},{65,1},{2,66},{66,2},{3,67},{67,3},{4,68},{68... | collective-permute-start | bytes 688136 | tf_op jit(solution)/shard_map/ppermute | solution.py:17
  13.0 48.9 %collective-permute-start.10 = (bf16[80,2048]{1,0:T(8,128)(2,1)S(1)}, bf16[80,2048]{1,0:T(8,128)(2,1)}, u32[]{:S(2)}, u32[]{:S(2)}) collective-permute-start(bf16[80,2048]{1,0:T(8,128)(2,1)S(1)} %pad_maximum_fusion), channel_id=1, source_target_pairs={{0,64},{64,0},{1,65},{65,1},{2,66},{66,2},{3,67},{67,3},{4,68},{68... | collective-permute-start | bytes 983048 | tf_op jit(solution)/shard_map/ppermute | solution.py:17
  30.8 6.0 %collective-permute-start.2 = (bf16[64,896]{1,0:T(8,128)(2,1)S(1)}, bf16[64,896]{1,0:T(8,128)(2,1)S(1)}, u32[]{:S(2)}, u32[]{:S(2)}) collective-permute-start(bf16[64,896]{1,0:T(8,128)(2,1)S(1)} %get-tuple-element.29), channel_id=1, source_target_pairs={{0,1},{1,2},{2,3},{3,0},{4,5},{5,6},{6,7},{7,4},{8,9},{9,10},{10,1... | collective-permute-start | bytes 344072 | tf_op jit(solution)/shard_map/up_1/ppermute | solution.py:22
  32.5 6.8 %collective-permute-start.3 = (bf16[64,896]{1,0:T(8,128)(2,1)S(1)}, bf16[64,896]{1,0:T(8,128)(2,1)S(1)}, u32[]{:S(2)}, u32[]{:S(2)}) collective-permute-start(bf16[64,896]{1,0:T(8,128)(2,1)S(1)} %get-tuple-element.31), channel_id=1, source_target_pairs={{0,2},{1,3},{2,0},{3,1},{4,6},{5,7},{6,4},{7,5},{8,10},{9,11},{10,... | collective-permute-start | bytes 344072 | tf_op jit(solution)/shard_map/up_1/ppermute | solution.py:22
  40.5 6.2 %collective-permute-start.7 = (bf16[64,896]{1,0:T(8,128)(2,1)S(1)}, bf16[64,896]{1,0:T(8,128)(2,1)S(1)}, u32[]{:S(2)}, u32[]{:S(2)}) collective-permute-start(bf16[64,896]{1,0:T(8,128)(2,1)S(1)} %get-tuple-element.49), channel_id=1, source_target_pairs={{0,1},{1,2},{2,3},{3,0},{4,5},{5,6},{6,7},{7,4},{8,9},{9,10},{10,1... | collective-permute-start | bytes 344072 | tf_op jit(solution)/shard_map/low_1/ppermute | solution.py:22
  40.8 5.9 %collective-permute-start.8 = (bf16[64,896]{1,0:T(8,128)(2,1)S(1)}, bf16[64,896]{1,0:T(8,128)(2,1)S(1)}, u32[]{:S(2)}, u32[]{:S(2)}) collective-permute-start(bf16[64,896]{1,0:T(8,128)(2,1)S(1)} %get-tuple-element.49), channel_id=1, source_target_pairs={{0,2},{1,3},{2,0},{3,1},{4,6},{5,7},{6,4},{7,5},{8,10},{9,11},{10,... | collective-permute-start | bytes 344072 | tf_op jit(solution)/shard_map/low_1/ppermute | solution.py:22
  51.8 21.8 %all-to-all-start.1 = ((bf16[16,16,2048]{2,1,0:T(8,128)(2,1)}), bf16[16,16,2048]{2,1,0:T(8,128)(2,1)S(1)}, u32[]{:S(2)}, u32[]{:S(2)}) async-start(bf16[16,16,2048]{2,1,0:T(8,128)(2,1)} %bitcast.16), calls=%async_computation.1 | async-start | bytes 2097152 | tf_op jit(solution)/shard_map/low_1/all_to_all | solution.py:36
  74.9 18.5 %all-to-all-start.2 = ((bf16[16,16,2048]{2,1,0:T(8,128)(2,1)}), bf16[16,16,2048]{2,1,0:T(8,128)(2,1)S(1)}, u32[]{:S(2)}, u32[]{:S(2)}) async-start(bf16[16,16,2048]{2,1,0:T(8,128)(2,1)} %broadcast_in_dim.76), calls=%async_computation.2 | async-start | bytes 2097152 | tf_op jit(solution)/shard_map/low_1/all_to_all | solution.py:30
  81.7 17.3 %collective-permute-start.14 = (bf16[16,256]{1,0:T(8,128)(2,1)S(1)}, bf16[16,256]{1,0:T(8,128)(2,1)S(1)}, u32[]{:S(2)}, u32[]{:S(2)}) collective-permute-start(bf16[16,256]{1,0:T(8,128)(2,1)S(1)} %pad_maximum_fusion.6), channel_id=1, source_target_pairs={{0,1},{1,2},{2,3},{3,0},{4,5},{5,6},{6,7},{7,4},{8,9},{9,10},{10,1... | collective-permute-start | bytes 24584 | tf_op jit(solution)/shard_map/up_0/ppermute | solution.py:22
  81.7 19.0 %collective-permute-start.15 = (bf16[16,256]{1,0:T(8,128)(2,1)S(1)}, bf16[16,256]{1,0:T(8,128)(2,1)S(1)}, u32[]{:S(2)}, u32[]{:S(2)}) collective-permute-start(bf16[16,256]{1,0:T(8,128)(2,1)S(1)} %pad_maximum_fusion.6), channel_id=1, source_target_pairs={{0,2},{1,3},{2,0},{3,1},{4,6},{5,7},{6,4},{7,5},{8,10},{9,11},{10,... | collective-permute-start | bytes 24584 | tf_op jit(solution)/shard_map/up_0/ppermute | solution.py:22
  83.6 17.1 %collective-permute-start.16 = (bf16[16,256]{1,0:T(8,128)(2,1)S(1)}, bf16[16,256]{1,0:T(8,128)(2,1)S(1)}, u32[]{:S(2)}, u32[]{:S(2)}) collective-permute-start(bf16[16,256]{1,0:T(8,128)(2,1)S(1)} %pad_maximum_fusion.6), channel_id=1, source_target_pairs={{0,3},{1,0},{2,1},{3,2},{4,7},{5,4},{6,5},{7,6},{8,11},{9,8},{10,9... | collective-permute-start | bytes 24584 | tf_op jit(solution)/shard_map/up_0/ppermute | solution.py:22
  97.9 6.2 %collective-permute-start.11 = (bf16[64,896]{1,0:T(8,128)(2,1)S(1)}, bf16[64,896]{1,0:T(8,128)(2,1)S(1)}, u32[]{:S(2)}, u32[]{:S(2)}) collective-permute-start(bf16[64,896]{1,0:T(8,128)(2,1)S(1)} %get-tuple-element.24), channel_id=1, source_target_pairs={{0,1},{1,2},{2,3},{3,0},{4,5},{5,6},{6,7},{7,4},{8,9},{9,10},{10,1... | collective-permute-start | bytes 344072 | tf_op jit(solution)/shard_map/up_0/ppermute | solution.py:22
  98.0 6.1 %collective-permute-start.12 = (bf16[64,896]{1,0:T(8,128)(2,1)S(1)}, bf16[64,896]{1,0:T(8,128)(2,1)S(1)}, u32[]{:S(2)}, u32[]{:S(2)}) collective-permute-start(bf16[64,896]{1,0:T(8,128)(2,1)S(1)} %get-tuple-element.26), channel_id=1, source_target_pairs={{0,2},{1,3},{2,0},{3,1},{4,6},{5,7},{6,4},{7,5},{8,10},{9,11},{10,... | collective-permute-start | bytes 344072 | tf_op jit(solution)/shard_map/up_0/ppermute | solution.py:22
  104.9 8.3 %collective-permute-start.17 = (bf16[64,896]{1,0:T(8,128)(2,1)S(1)}, bf16[64,896]{1,0:T(8,128)(2,1)S(1)}, u32[]{:S(2)}, u32[]{:S(2)}) collective-permute-start(bf16[64,896]{1,0:T(8,128)(2,1)S(1)} %get-tuple-element.51), channel_id=1, source_target_pairs={{0,1},{1,2},{2,3},{3,0},{4,5},{5,6},{6,7},{7,4},{8,9},{9,10},{10,1... | collective-permute-start | bytes 344072 | tf_op jit(solution)/shard_map/low_0/ppermute | solution.py:22
  105.4 7.8 %collective-permute-start.18 = (bf16[64,896]{1,0:T(8,128)(2,1)S(1)}, bf16[64,896]{1,0:T(8,128)(2,1)S(1)}, u32[]{:S(2)}, u32[]{:S(2)}) collective-permute-start(bf16[64,896]{1,0:T(8,128)(2,1)S(1)} %get-tuple-element.51), channel_id=1, source_target_pairs={{0,2},{1,3},{2,0},{3,1},{4,6},{5,7},{6,4},{7,5},{8,10},{9,11},{10,... | collective-permute-start | bytes 344072 | tf_op jit(solution)/shard_map/low_0/ppermute | solution.py:22
  109.4 13.6 %all-to-all-start.3 = ((bf16[16,80,256]{2,1,0:T(8,128)(2,1)}), bf16[16,80,256]{2,1,0:T(8,128)(2,1)S(1)}, u32[]{:S(2)}, u32[]{:S(2)}) async-start(bf16[16,80,256]{2,1,0:T(8,128)(2,1)} %broadcast_in_dim.77), calls=%async_computation.3 | async-start | bytes 1310720 | tf_op jit(solution)/shard_map/low_0/all_to_all | solution.py:30
  123.1 8.0 %collective-permute-start.20 = (bf16[64,256]{1,0:T(8,128)(2,1)S(1)}, bf16[64,256]{1,0:T(8,128)(2,1)S(1)}, u32[]{:S(2)}, u32[]{:S(2)}) collective-permute-start(bf16[64,256]{1,0:T(8,128)(2,1)S(1)} %slice_reduce_fusion), channel_id=1, source_target_pairs={{0,1},{1,2},{2,3},{3,0},{4,5},{5,6},{6,7},{7,4},{8,9},{9,10},{10,1... | collective-permute-start | bytes 98312 | tf_op jit(solution)/shard_map/outputs/ppermute | solution.py:22
  124.5 6.6 %collective-permute-start.21 = (bf16[64,256]{1,0:T(8,128)(2,1)S(1)}, bf16[64,256]{1,0:T(8,128)(2,1)S(1)}, u32[]{:S(2)}, u32[]{:S(2)}) collective-permute-start(bf16[64,256]{1,0:T(8,128)(2,1)S(1)} %slice_reduce_fusion), channel_id=1, source_target_pairs={{0,2},{1,3},{2,0},{3,1},{4,6},{5,7},{6,4},{7,5},{8,10},{9,11},{10,... | collective-permute-start | bytes 98312 | tf_op jit(solution)/shard_map/outputs/ppermute | solution.py:22
  125.3 5.8 %collective-permute-start.22 = (bf16[64,256]{1,0:T(8,128)(2,1)S(1)}, bf16[64,256]{1,0:T(8,128)(2,1)S(1)}, u32[]{:S(2)}, u32[]{:S(2)}) collective-permute-start(bf16[64,256]{1,0:T(8,128)(2,1)S(1)} %slice_reduce_fusion), channel_id=1, source_target_pairs={{0,3},{1,0},{2,1},{3,2},{4,7},{5,4},{6,5},{7,6},{8,11},{9,8},{10,9... | collective-permute-start | bytes 98312 | tf_op jit(solution)/shard_map/outputs/ppermute | solution.py:22
  127.3 15.9 %all-to-all-start.4 = ((bf16[16,16,2048]{2,1,0:T(8,128)(2,1)}), bf16[16,16,2048]{2,1,0:T(8,128)(2,1)S(1)}, u32[]{:S(2)}, u32[]{:S(2)}) async-start(bf16[16,16,2048]{2,1,0:T(8,128)(2,1)} %bitcast.24), calls=%async_computation.4 | async-start | bytes 2097152 | tf_op jit(solution)/shard_map/low_0/all_to_all | solution.py:36
  143.4 8.7 %collective-permute-start.23 = (bf16[16,2048]{1,0:T(8,128)(2,1)S(1)}, bf16[16,2048]{1,0:T(8,128)(2,1)S(1)}, u32[]{:S(2)}, u32[]{:S(2)}) collective-permute-start(bf16[16,2048]{1,0:T(8,128)(2,1)S(1)} %broadcast_select_fusion.4), channel_id=1, source_target_pairs={{0,64},{64,0},{1,65},{65,1},{2,66},{66,2},{3,67},{67,3},{4,68},{68... | collective-permute-start | bytes 196616 | tf_op jit(solution)/shard_map/outputs/ppermute | solution.py:17
  (18 other events, 236.1 us)

commit v6 on v5

--- a/solution.py
+++ b/solution.py
@@ -60,11 +60,15 @@
 
 
 def gather_mp(block):
+    return in_order(from_all_mp(block))
+
+
+def in_order(blocks):
     count = lax.axis_size("mp")
     mine = lax.axis_index("mp")
-    rows = block.shape[0]
-    whole = jnp.zeros((count * rows, block.shape[1]), block.dtype)
-    for distance, got in enumerate(from_all_mp(block)):
+    rows, width = blocks[0].shape
+    whole = jnp.zeros((count * rows, width), blocks[0].dtype)
+    for distance, got in enumerate(blocks):
         whole = lax.dynamic_update_slice_in_dim(
             whole, got, ((mine - distance) % count) * rows, 0
         )
@@ -153,6 +157,7 @@
     weight_low = (lower_w[0], swap_sections(lower_w[0]))
 
     last = sections - 1
+    pouts_low = held(*[of_section(pout_low, s) for s in range(sections)])
     scales_low = held(*[of_section(deriv_low, s).astype(F32) for s in range(sections)])
     grads = [None] * sections
     ups = []
@@ -173,7 +178,7 @@
             scale = of_section(deriv_up, section).astype(F32)
             middle = (summed * scale).astype(BF16)
         with jax.named_scope(f"low_{section}"):
-            low = [times_t(middle, of_section(pout_low, section)).astype(BF16)]
+            low = [times_t(middle, pouts_low[section]).astype(BF16)]
             if section == last:
                 low += [of_section(left_low, s) for s in range(last, -1, -1)]
             lows += low
@@ -196,7 +201,8 @@
                 gathered = gather_dp(grad)
 
     with jax.named_scope("outputs"):
-        low = gather_mp(low)
+        *blocks, grads[0] = held(*from_all_mp(low), grads[0])
+        low = in_order(blocks)
 
         def columns(array, section):
             turn = last - section
@@ -213,7 +219,6 @@
         ]
         mine = jnp.where(core == 0, pair[0], pair[1])
         other = jnp.where(core == 0, pair[1], pair[0])
-        other, grads[0] = held(other, grads[0])
         got = swap_sections(other)
 
         def joined(own, received, rows):

time: 156 us -> 151 us (0.968)
  waiting for transfers between devices: 54.5 us -> 47.6 us
  starting transfers between devices: 60.1 us -> 62 us
    all_to_all x2, waiting for transfers between devices: 22.6 us -> 18.3 us  [scatter_sum_dp(): got = lax.all_to_all(partial, 'dp', 0, 0, tiled=True)]
    ppermute x18, waiting for transfers between devices: 10.8 us -> 7.95 us  [shift_mp(): lax.ppermute(block, 'mp', [(i, (i + distance) % count) for i in range(cou...]
    ppermute x7, starting transfers between devices: 12.8 us -> 14.8 us  [swap_sections(): return lax.ppermute(block, 'section', [(0, 1), (1, 0)])]
    select_n x4 -> x5, other arithmetic: 6.81 us -> 6.84 us  [of_section(): return jnp.where(core == section, own, received)]
  transfers between devices with their start and end apart: 30 -> 30, of which waited for: 13 -> 12; matrix products, arithmetic and copies ran while one was open for 23% -> 23% of each run, Pallas kernels for 0% -> 0%
where the time goes in v6:
time: 151 us; the launch traced here: 150 us
  starting transfers between devices  62 us (41%)
  waiting for transfers between devices  47.6 us (32%)
  matrix products  22.2 us (15%)
  other arithmetic  10.6 us (7%)
  local copies, waits for them, and re-layouts  6.09 us (4%)
    ppermute x18, starting transfers between devices, shift_mp(): lax.ppermute(block, 'mp', [(i, (i + distance) % count) for i in range(cou...  22.1 us
    dot_general x10, matrix products, times_t(): lax.dot_general(left, right, (((1,), (1,)), ((), ())), preferred_element_...  21.6 us
    all_to_all x3, waiting for transfers between devices, gather_dp(): got = lax.all_to_all(copies, 'dp', 0, 0, tiled=True)  19.4 us
    all_to_all x2, waiting for transfers between devices, scatter_sum_dp(): got = lax.all_to_all(partial, 'dp', 0, 0, tiled=True)  18.3 us
    all_to_all x3, starting transfers between devices, gather_dp(): got = lax.all_to_all(copies, 'dp', 0, 0, tiled=True)  14.8 us
    ppermute x7, starting transfers between devices, swap_sections(): return lax.ppermute(block, 'section', [(0, 1), (1, 0)])  14.8 us
    all_to_all x2, starting transfers between devices, scatter_sum_dp(): got = lax.all_to_all(partial, 'dp', 0, 0, tiled=True)  10.3 us
    ppermute x18, waiting for transfers between devices, shift_mp(): lax.ppermute(block, 'mp', [(i, (i + distance) % count) for i in range(cou...  7.95 us
  transfers between devices with their start and end apart: 30, of which 12 were waited for; matrix products, arithmetic and copies ran while one was open for 23% of the time, Pallas kernels for 0%

profile of v6, /device:TPU:1, one launch (start us, length us, event | category | flops | bytes accessed | tf_op | source)
XLA Modules:
  0.0 149.8 jit_solution(13868207330789064133)
XLA Ops:
  4.3 6.8 %all-to-all-start = ((bf16[16,16,2048]{2,1,0:T(8,128)(2,1)}), bf16[16,16,2048]{2,1,0:T(8,128)(2,1)S(1)}, u32[]{:S(2)}, u32[]{:S(2)}) async-start(bf16[16,16,2048]{2,1,0:T(8,128)(2,1)} %broadcast_in_dim.74), calls=%async_computation | async-start | bytes 2097152 | tf_op jit(solution)/shard_map/all_to_all | solution.py:30
  14.5 4.5 %broadcast_select_fusion = bf16[2048,896]{1,0:T(8,128)(2,1)} fusion(bf16[2048,896]{1,0:T(8,128)(2,1)} %collective-permute-done.1, pred[]{:T(512)S(6)} %eq.81, bf16[1,2048,896]{2,1,0:T(8,128)(2,1)} %param.15), kind=kLoop, calls=%fused_computation.6 | loop fusion | flops 1835008 | bytes 11010049 | tf_op jit(solution)/shard_map/up_1/jit(_where)/select_n | solution.py:121
  19.0 2.3 %broadcast_select_fusion.1 = bf16[896,2048]{1,0:T(8,128)(2,1)} fusion(bf16[896,2048]{1,0:T(8,128)(2,1)} %collective-permute-done, pred[]{:T(512)S(6)} %eq.81, bf16[1,896,2048]{2,1,0:T(8,128)(2,1)S(1)} %copy-done.1), kind=kLoop, calls=%fused_computation.7 | loop fusion | flops 1835008 | bytes 11010049 | tf_op jit(solution)/shard_map/up_1/jit(_where)/select_n | solution.py:121
  21.3 6.1 %all-to-all-done = bf16[16,16,2048]{2,1,0:T(8,128)(2,1)S(1)} async-done(((bf16[16,16,2048]{2,1,0:T(8,128)(2,1)}), bf16[16,16,2048]{2,1,0:T(8,128)(2,1)S(1)}, u32[]{:S(2)}, u32[]{:S(2)}) %all-to-all-start) | async-done | bytes 1048608 | tf_op jit(solution)/shard_map/all_to_all | solution.py:30
  27.4 3.4 %convolution_convert_fusion.1 = bf16[256,896]{1,0:T(8,128)(2,1)S(1)} fusion(bf16[256,2048]{1,0:T(8,128)(2,1)S(1)} %bitcast.115, bf16[896,2048]{1,0:T(8,128)(2,1)} %broadcast_select_fusion.1), kind=kOutput, calls=%fused_computation.13 | convolution fusion | flops 939753472 | bytes 5177344 | tf_op jit(solution)/shard_map/up_1/dot_general | solution.py:11
  32.5 3.3 %collective-permute-start.3 = (bf16[64,896]{1,0:T(8,128)(2,1)S(1)}, bf16[64,896]{1,0:T(8,128)(2,1)S(1)}, u32[]{:S(2)}, u32[]{:S(2)}) collective-permute-start(bf16[64,896]{1,0:T(8,128)(2,1)S(1)} %get-tuple-element.41), channel_id=1, source_target_pairs={{0,2},{1,3},{2,0},{3,1},{4,6},{5,7},{6,4},{7,5},{8,10},{9,11},{10,... | collective-permute-start | bytes 344072 | tf_op jit(solution)/shard_map/up_1/ppermute | solution.py:22
  36.6 3.1 %collective-permute-start.6 = (bf16[80,64]{1,0:T(8,128)(2,1)S(1)}, bf16[80,64]{1,0:T(8,128)(2,1)S(1)}, u32[]{:S(2)}, u32[]{:S(2)}) collective-permute-start(bf16[80,64]{1,0:T(8,128)(2,1)S(1)} %pad_maximum_fusion.5), channel_id=1, source_target_pairs={{0,64},{64,0},{1,65},{65,1},{2,66},{66,2},{3,67},{67,3},{4,68},{68... | collective-permute-start | bytes 30728 | tf_op jit(solution)/shard_map/ppermute | solution.py:17
  40.7 2.5 %collective-permute-start.8 = (bf16[64,896]{1,0:T(8,128)(2,1)S(1)}, bf16[64,896]{1,0:T(8,128)(2,1)S(1)}, u32[]{:S(2)}, u32[]{:S(2)}) collective-permute-start(bf16[64,896]{1,0:T(8,128)(2,1)S(1)} %get-tuple-element.61), channel_id=1, source_target_pairs={{0,2},{1,3},{2,0},{3,1},{4,6},{5,7},{6,4},{7,5},{8,10},{9,11},{10,... | collective-permute-start | bytes 344072 | tf_op jit(solution)/shard_map/low_1/ppermute | solution.py:22
  44.0 2.6 %collective-permute-done.7 = bf16[64,896]{1,0:T(8,128)(2,1)S(1)} collective-permute-done((bf16[64,896]{1,0:T(8,128)(2,1)S(1)}, bf16[64,896]{1,0:T(8,128)(2,1)S(1)}, u32[]{:S(2)}, u32[]{:S(2)}) %collective-permute-start.7) | collective-permute-done | bytes 114720 | tf_op jit(solution)/shard_map/low_1/ppermute | solution.py:22
  47.4 4.4 %convolution_convert_fusion = bf16[256,2048]{1,0:T(8,128)(2,1)} fusion(bf16[256,896]{1,0:T(8,128)(2,1)S(1)} %constant_dynamic-update-slice_fusion.8, bf16[2048,896]{1,0:T(8,128)(2,1)} %broadcast_select_fusion), kind=kOutput, calls=%fused_computation.9 | convolution fusion | flops 940048384 | bytes 5177344 | tf_op jit(solution)/shard_map/low_1/dot_general | solution.py:11
  51.8 6.6 %all-to-all-start.1 = ((bf16[16,16,2048]{2,1,0:T(8,128)(2,1)}), bf16[16,16,2048]{2,1,0:T(8,128)(2,1)S(1)}, u32[]{:S(2)}, u32[]{:S(2)}) async-start(bf16[16,16,2048]{2,1,0:T(8,128)(2,1)} %bitcast.16), calls=%async_computation.1 | async-start | bytes 2097152 | tf_op jit(solution)/shard_map/low_1/all_to_all | solution.py:36
  58.5 2.4 %collective-permute-start.10 = (bf16[80,2048]{1,0:T(8,128)(2,1)S(1)}, bf16[80,2048]{1,0:T(8,128)(2,1)S(1)}, u32[]{:S(2)}, u32[]{:S(2)}) collective-permute-start(bf16[80,2048]{1,0:T(8,128)(2,1)S(1)} %pad_maximum_fusion), channel_id=1, source_target_pairs={{0,64},{64,0},{1,65},{65,1},{2,66},{66,2},{3,67},{67,3},{4,68},{68... | collective-permute-start | bytes 983048 | tf_op jit(solution)/shard_map/ppermute | solution.py:17
  62.9 10.5 %all-to-all-done.1 = bf16[16,16,2048]{2,1,0:T(8,128)(2,1)S(1)} async-done(((bf16[16,16,2048]{2,1,0:T(8,128)(2,1)}), bf16[16,16,2048]{2,1,0:T(8,128)(2,1)S(1)}, u32[]{:S(2)}, u32[]{:S(2)}) %all-to-all-start.1) | async-done | bytes 1048608 | tf_op jit(solution)/shard_map/low_1/all_to_all | solution.py:36
  74.7 4.2 %all-to-all-start.2 = ((bf16[16,16,2048]{2,1,0:T(8,128)(2,1)}), bf16[16,16,2048]{2,1,0:T(8,128)(2,1)S(1)}, u32[]{:S(2)}, u32[]{:S(2)}) async-start(bf16[16,16,2048]{2,1,0:T(8,128)(2,1)} %broadcast_in_dim.75), calls=%async_computation.2 | async-start | bytes 2097152 | tf_op jit(solution)/shard_map/low_1/all_to_all | solution.py:30
  84.2 9.1 %all-to-all-done.2 = bf16[16,16,2048]{2,1,0:T(8,128)(2,1)S(1)} async-done(((bf16[16,16,2048]{2,1,0:T(8,128)(2,1)}), bf16[16,16,2048]{2,1,0:T(8,128)(2,1)S(1)}, u32[]{:S(2)}, u32[]{:S(2)}) %all-to-all-start.2) | async-done | bytes 1048608 | tf_op jit(solution)/shard_map/low_1/all_to_all | solution.py:30
  93.3 4.4 %fusion.9 = bf16[256,896]{1,0:T(8,128)(2,1)S(1)} fusion(bf16[256,2048]{1,0:T(8,128)(2,1)S(1)} %bitcast.116, bf16[896,2048]{1,0:T(8,128)(2,1)} %collective-permute-done, pred[]{:T(512)S(6)} %eq.80, bf16[1,896,2048]{2,1,0:T(8,128)(2,1)} %param.14), kind=kOutput, calls=%fused_computation.12 | convolution fusion | flops 941588480 | bytes 8847361 | tf_op jit(solution)/shard_map/up_0/dot_general | solution.py:11
  100.6 3.4 %collective-permute-done.11 = bf16[64,896]{1,0:T(8,128)(2,1)S(1)} collective-permute-done((bf16[64,896]{1,0:T(8,128)(2,1)S(1)}, bf16[64,896]{1,0:T(8,128)(2,1)S(1)}, u32[]{:S(2)}, u32[]{:S(2)}) %collective-permute-start.11) | collective-permute-done | bytes 114720 | tf_op jit(solution)/shard_map/up_0/ppermute | solution.py:22
  105.3 2.8 %collective-permute-start.18 = (bf16[64,896]{1,0:T(8,128)(2,1)S(1)}, bf16[64,896]{1,0:T(8,128)(2,1)S(1)}, u32[]{:S(2)}, u32[]{:S(2)}) collective-permute-start(bf16[64,896]{1,0:T(8,128)(2,1)S(1)} %get-tuple-element.63), channel_id=1, source_target_pairs={{0,2},{1,3},{2,0},{3,1},{4,6},{5,7},{6,4},{7,5},{8,10},{9,11},{10,... | collective-permute-start | bytes 344072 | tf_op jit(solution)/shard_map/low_0/ppermute | solution.py:22
  109.3 3.8 %all-to-all-start.3 = ((bf16[16,80,256]{2,1,0:T(8,128)(2,1)}), bf16[16,80,256]{2,1,0:T(8,128)(2,1)S(1)}, u32[]{:S(2)}, u32[]{:S(2)}) async-start(bf16[16,80,256]{2,1,0:T(8,128)(2,1)} %broadcast_in_dim.76), calls=%async_computation.3 | async-start | bytes 1310720 | tf_op jit(solution)/shard_map/low_0/all_to_all | solution.py:30
  113.2 5.5 %fusion.6 = bf16[256,2048]{1,0:T(8,128)(2,1)} fusion(bf16[256,896]{1,0:T(8,128)(2,1)S(1)} %constant_dynamic-update-slice_fusion.4, bf16[2048,896]{1,0:T(8,128)(2,1)} %collective-permute-done.1, pred[]{:T(512)S(6)} %eq.80, bf16[1,2048,896]{2,1,0:T(8,128)(2,1)} %param.15), kind=kOutput, calls=%fused_computation.8 | convolution fusion | flops 941883392 | bytes 8847361 | tf_op jit(solution)/shard_map/low_0/dot_general | solution.py:11
  118.6 4.2 %all-to-all-done.3 = bf16[16,80,256]{2,1,0:T(8,128)(2,1)S(1)} async-done(((bf16[16,80,256]{2,1,0:T(8,128)(2,1)}), bf16[16,80,256]{2,1,0:T(8,128)(2,1)S(1)}, u32[]{:S(2)}, u32[]{:S(2)}) %all-to-all-start.3) | async-done | bytes 655392 | tf_op jit(solution)/shard_map/low_0/all_to_all | solution.py:30
  122.9 3.7 %all-to-all-start.4 = ((bf16[16,16,2048]{2,1,0:T(8,128)(2,1)}), bf16[16,16,2048]{2,1,0:T(8,128)(2,1)S(1)}, u32[]{:S(2)}, u32[]{:S(2)}) async-start(bf16[16,16,2048]{2,1,0:T(8,128)(2,1)} %bitcast.24), calls=%async_computation.4 | async-start | bytes 2097152 | tf_op jit(solution)/shard_map/low_0/all_to_all | solution.py:36
  131.2 7.8 %all-to-all-done.4 = bf16[16,16,2048]{2,1,0:T(8,128)(2,1)S(1)} async-done(((bf16[16,16,2048]{2,1,0:T(8,128)(2,1)}), bf16[16,16,2048]{2,1,0:T(8,128)(2,1)S(1)}, u32[]{:S(2)}, u32[]{:S(2)}) %all-to-all-start.4) | async-done | bytes 1048608 | tf_op jit(solution)/shard_map/low_0/all_to_all | solution.py:36
  139.4 6.8 %collective-permute-start.23 = (bf16[16,2048]{1,0:T(8,128)(2,1)S(1)}, bf16[16,2048]{1,0:T(8,128)(2,1)S(1)}, u32[]{:S(2)}, u32[]{:S(2)}) collective-permute-start(bf16[16,2048]{1,0:T(8,128)(2,1)S(1)} %broadcast_select_fusion.6), channel_id=1, source_target_pairs={{0,64},{64,0},{1,65},{65,1},{2,66},{66,2},{3,67},{67,3},{4,68},{68... | collective-permute-start | bytes 196616 | tf_op jit(solution)/shard_map/outputs/ppermute | solution.py:17
  (132 shorter events, 34.3 us)
Async XLA Ops:
  0.7 13.8 %collective-permute-start.1 = (bf16[2048,896]{1,0:T(8,128)(2,1)}, bf16[2048,896]{1,0:T(8,128)(2,1)}, u32[]{:S(2)}, u32[]{:S(2)}) collective-permute-start(bf16[2048,896]{1,0:T(8,128)(2,1)} %bitcast.114), channel_id=1, source_target_pairs={{0,64},{64,0},{1,65},{65,1},{2,66},{66,2},{3,67},{67,3},{4,68},{68... | collective-permute-start | bytes 11010056 | tf_op jit(solution)/shard_map/ppermute | solution.py:17
  2.2 16.8 %collective-permute-start = (bf16[896,2048]{1,0:T(8,128)(2,1)}, bf16[896,2048]{1,0:T(8,128)(2,1)}, u32[]{:S(2)}, u32[]{:S(2)}) collective-permute-start(bf16[896,2048]{1,0:T(8,128)(2,1)} %bitcast.113), channel_id=1, source_target_pairs={{0,64},{64,0},{1,65},{65,1},{2,66},{66,2},{3,67},{67,3},{4,68},{68... | collective-permute-start | bytes 11010056 | tf_op jit(solution)/shard_map/ppermute | solution.py:17
  4.3 23.1 %all-to-all-start = ((bf16[16,16,2048]{2,1,0:T(8,128)(2,1)}), bf16[16,16,2048]{2,1,0:T(8,128)(2,1)S(1)}, u32[]{:S(2)}, u32[]{:S(2)}) async-start(bf16[16,16,2048]{2,1,0:T(8,128)(2,1)} %broadcast_in_dim.74), calls=%async_computation | async-start | bytes 2097152 | tf_op jit(solution)/shard_map/all_to_all | solution.py:30
  12.2 27.5 %collective-permute-start.5 = (bf16[128,896]{1,0:T(8,128)(2,1)S(1)}, bf16[128,896]{1,0:T(8,128)(2,1)S(1)}, u32[]{:S(2)}, u32[]{:S(2)}) collective-permute-start(bf16[128,896]{1,0:T(8,128)(2,1)S(1)} %pad_maximum_fusion.2), channel_id=1, source_target_pairs={{0,64},{64,0},{1,65},{65,1},{2,66},{66,2},{3,67},{67,3},{4,68},{68... | collective-permute-start | bytes 688136 | tf_op jit(solution)/shard_map/ppermute | solution.py:17
  30.8 8.9 %collective-permute-start.2 = (bf16[64,896]{1,0:T(8,128)(2,1)S(1)}, bf16[64,896]{1,0:T(8,128)(2,1)S(1)}, u32[]{:S(2)}, u32[]{:S(2)}) collective-permute-start(bf16[64,896]{1,0:T(8,128)(2,1)S(1)} %get-tuple-element.39), channel_id=1, source_target_pairs={{0,1},{1,2},{2,3},{3,0},{4,5},{5,6},{6,7},{7,4},{8,9},{9,10},{10,1... | collective-permute-start | bytes 344072 | tf_op jit(solution)/shard_map/up_1/ppermute | solution.py:22
  32.5 7.2 %collective-permute-start.3 = (bf16[64,896]{1,0:T(8,128)(2,1)S(1)}, bf16[64,896]{1,0:T(8,128)(2,1)S(1)}, u32[]{:S(2)}, u32[]{:S(2)}) collective-permute-start(bf16[64,896]{1,0:T(8,128)(2,1)S(1)} %get-tuple-element.41), channel_id=1, source_target_pairs={{0,2},{1,3},{2,0},{3,1},{4,6},{5,7},{6,4},{7,5},{8,10},{9,11},{10,... | collective-permute-start | bytes 344072 | tf_op jit(solution)/shard_map/up_1/ppermute | solution.py:22
  36.6 24.3 %collective-permute-start.6 = (bf16[80,64]{1,0:T(8,128)(2,1)S(1)}, bf16[80,64]{1,0:T(8,128)(2,1)S(1)}, u32[]{:S(2)}, u32[]{:S(2)}) collective-permute-start(bf16[80,64]{1,0:T(8,128)(2,1)S(1)} %pad_maximum_fusion.5), channel_id=1, source_target_pairs={{0,64},{64,0},{1,65},{65,1},{2,66},{66,2},{3,67},{67,3},{4,68},{68... | collective-permute-start | bytes 30728 | tf_op jit(solution)/shard_map/ppermute | solution.py:17
  40.5 6.2 %collective-permute-start.7 = (bf16[64,896]{1,0:T(8,128)(2,1)S(1)}, bf16[64,896]{1,0:T(8,128)(2,1)S(1)}, u32[]{:S(2)}, u32[]{:S(2)}) collective-permute-start(bf16[64,896]{1,0:T(8,128)(2,1)S(1)} %get-tuple-element.61), channel_id=1, source_target_pairs={{0,1},{1,2},{2,3},{3,0},{4,5},{5,6},{6,7},{7,4},{8,9},{9,10},{10,1... | collective-permute-start | bytes 344072 | tf_op jit(solution)/shard_map/low_1/ppermute | solution.py:22
  40.7 6.0 %collective-permute-start.8 = (bf16[64,896]{1,0:T(8,128)(2,1)S(1)}, bf16[64,896]{1,0:T(8,128)(2,1)S(1)}, u32[]{:S(2)}, u32[]{:S(2)}) collective-permute-start(bf16[64,896]{1,0:T(8,128)(2,1)S(1)} %get-tuple-element.61), channel_id=1, source_target_pairs={{0,2},{1,3},{2,0},{3,1},{4,6},{5,7},{6,4},{7,5},{8,10},{9,11},{10,... | collective-permute-start | bytes 344072 | tf_op jit(solution)/shard_map/low_1/ppermute | solution.py:22
  51.8 21.6 %all-to-all-start.1 = ((bf16[16,16,2048]{2,1,0:T(8,128)(2,1)}), bf16[16,16,2048]{2,1,0:T(8,128)(2,1)S(1)}, u32[]{:S(2)}, u32[]{:S(2)}) async-start(bf16[16,16,2048]{2,1,0:T(8,128)(2,1)} %bitcast.16), calls=%async_computation.1 | async-start | bytes 2097152 | tf_op jit(solution)/shard_map/low_1/all_to_all | solution.py:36
  74.7 18.5 %all-to-all-start.2 = ((bf16[16,16,2048]{2,1,0:T(8,128)(2,1)}), bf16[16,16,2048]{2,1,0:T(8,128)(2,1)S(1)}, u32[]{:S(2)}, u32[]{:S(2)}) async-start(bf16[16,16,2048]{2,1,0:T(8,128)(2,1)} %broadcast_in_dim.75), calls=%async_computation.2 | async-start | bytes 2097152 | tf_op jit(solution)/shard_map/low_1/all_to_all | solution.py:30
  81.5 17.3 %collective-permute-start.14 = (bf16[16,256]{1,0:T(8,128)(2,1)S(1)}, bf16[16,256]{1,0:T(8,128)(2,1)S(1)}, u32[]{:S(2)}, u32[]{:S(2)}) collective-permute-start(bf16[16,256]{1,0:T(8,128)(2,1)S(1)} %pad_maximum_fusion.6), channel_id=1, source_target_pairs={{0,1},{1,2},{2,3},{3,0},{4,5},{5,6},{6,7},{7,4},{8,9},{9,10},{10,1... | collective-permute-start | bytes 24584 | tf_op jit(solution)/shard_map/up_0/ppermute | solution.py:22
  81.5 19.0 %collective-permute-start.15 = (bf16[16,256]{1,0:T(8,128)(2,1)S(1)}, bf16[16,256]{1,0:T(8,128)(2,1)S(1)}, u32[]{:S(2)}, u32[]{:S(2)}) collective-permute-start(bf16[16,256]{1,0:T(8,128)(2,1)S(1)} %pad_maximum_fusion.6), channel_id=1, source_target_pairs={{0,2},{1,3},{2,0},{3,1},{4,6},{5,7},{6,4},{7,5},{8,10},{9,11},{10,... | collective-permute-start | bytes 24584 | tf_op jit(solution)/shard_map/up_0/ppermute | solution.py:22
  83.4 17.2 %collective-permute-start.16 = (bf16[16,256]{1,0:T(8,128)(2,1)S(1)}, bf16[16,256]{1,0:T(8,128)(2,1)S(1)}, u32[]{:S(2)}, u32[]{:S(2)}) collective-permute-start(bf16[16,256]{1,0:T(8,128)(2,1)S(1)} %pad_maximum_fusion.6), channel_id=1, source_target_pairs={{0,3},{1,0},{2,1},{3,2},{4,7},{5,4},{6,5},{7,6},{8,11},{9,8},{10,9... | collective-permute-start | bytes 24584 | tf_op jit(solution)/shard_map/up_0/ppermute | solution.py:22
  97.8 6.2 %collective-permute-start.11 = (bf16[64,896]{1,0:T(8,128)(2,1)S(1)}, bf16[64,896]{1,0:T(8,128)(2,1)S(1)}, u32[]{:S(2)}, u32[]{:S(2)}) collective-permute-start(bf16[64,896]{1,0:T(8,128)(2,1)S(1)} %get-tuple-element.34), channel_id=1, source_target_pairs={{0,1},{1,2},{2,3},{3,0},{4,5},{5,6},{6,7},{7,4},{8,9},{9,10},{10,1... | collective-permute-start | bytes 344072 | tf_op jit(solution)/shard_map/up_0/ppermute | solution.py:22
  97.9 6.1 %collective-permute-start.12 = (bf16[64,896]{1,0:T(8,128)(2,1)S(1)}, bf16[64,896]{1,0:T(8,128)(2,1)S(1)}, u32[]{:S(2)}, u32[]{:S(2)}) collective-permute-start(bf16[64,896]{1,0:T(8,128)(2,1)S(1)} %get-tuple-element.36), channel_id=1, source_target_pairs={{0,2},{1,3},{2,0},{3,1},{4,6},{5,7},{6,4},{7,5},{8,10},{9,11},{10,... | collective-permute-start | bytes 344072 | tf_op jit(solution)/shard_map/up_0/ppermute | solution.py:22
  104.7 8.3 %collective-permute-start.17 = (bf16[64,896]{1,0:T(8,128)(2,1)S(1)}, bf16[64,896]{1,0:T(8,128)(2,1)S(1)}, u32[]{:S(2)}, u32[]{:S(2)}) collective-permute-start(bf16[64,896]{1,0:T(8,128)(2,1)S(1)} %get-tuple-element.63), channel_id=1, source_target_pairs={{0,1},{1,2},{2,3},{3,0},{4,5},{5,6},{6,7},{7,4},{8,9},{9,10},{10,1... | collective-permute-start | bytes 344072 | tf_op jit(solution)/shard_map/low_0/ppermute | solution.py:22
  105.3 7.8 %collective-permute-start.18 = (bf16[64,896]{1,0:T(8,128)(2,1)S(1)}, bf16[64,896]{1,0:T(8,128)(2,1)S(1)}, u32[]{:S(2)}, u32[]{:S(2)}) collective-permute-start(bf16[64,896]{1,0:T(8,128)(2,1)S(1)} %get-tuple-element.63), channel_id=1, source_target_pairs={{0,2},{1,3},{2,0},{3,1},{4,6},{5,7},{6,4},{7,5},{8,10},{9,11},{10,... | collective-permute-start | bytes 344072 | tf_op jit(solution)/shard_map/low_0/ppermute | solution.py:22
  109.3 13.6 %all-to-all-start.3 = ((bf16[16,80,256]{2,1,0:T(8,128)(2,1)}), bf16[16,80,256]{2,1,0:T(8,128)(2,1)S(1)}, u32[]{:S(2)}, u32[]{:S(2)}) async-start(bf16[16,80,256]{2,1,0:T(8,128)(2,1)} %broadcast_in_dim.76), calls=%async_computation.3 | async-start | bytes 1310720 | tf_op jit(solution)/shard_map/low_0/all_to_all | solution.py:30
  122.9 16.0 %all-to-all-start.4 = ((bf16[16,16,2048]{2,1,0:T(8,128)(2,1)}), bf16[16,16,2048]{2,1,0:T(8,128)(2,1)S(1)}, u32[]{:S(2)}, u32[]{:S(2)}) async-start(bf16[16,16,2048]{2,1,0:T(8,128)(2,1)} %bitcast.24), calls=%async_computation.4 | async-start | bytes 2097152 | tf_op jit(solution)/shard_map/low_0/all_to_all | solution.py:36
  126.9 12.3 %collective-permute-start.20 = (bf16[64,256]{1,0:T(8,128)(2,1)S(1)}, bf16[64,256]{1,0:T(8,128)(2,1)S(1)}, u32[]{:S(2)}, u32[]{:S(2)}) collective-permute-start(bf16[64,256]{1,0:T(8,128)(2,1)S(1)} %slice_reduce_fusion), channel_id=1, source_target_pairs={{0,1},{1,2},{2,3},{3,0},{4,5},{5,6},{6,7},{7,4},{8,9},{9,10},{10,1... | collective-permute-start | bytes 98312 | tf_op jit(solution)/shard_map/outputs/ppermute | solution.py:22
  128.3 10.9 %collective-permute-start.21 = (bf16[64,256]{1,0:T(8,128)(2,1)S(1)}, bf16[64,256]{1,0:T(8,128)(2,1)S(1)}, u32[]{:S(2)}, u32[]{:S(2)}) collective-permute-start(bf16[64,256]{1,0:T(8,128)(2,1)S(1)} %slice_reduce_fusion), channel_id=1, source_target_pairs={{0,2},{1,3},{2,0},{3,1},{4,6},{5,7},{6,4},{7,5},{8,10},{9,11},{10,... | collective-permute-start | bytes 98312 | tf_op jit(solution)/shard_map/outputs/ppermute | solution.py:22
  129.1 10.1 %collective-permute-start.22 = (bf16[64,256]{1,0:T(8,128)(2,1)S(1)}, bf16[64,256]{1,0:T(8,128)(2,1)S(1)}, u32[]{:S(2)}, u32[]{:S(2)}) collective-permute-start(bf16[64,256]{1,0:T(8,128)(2,1)S(1)} %slice_reduce_fusion), channel_id=1, source_target_pairs={{0,3},{1,0},{2,1},{3,2},{4,7},{5,4},{6,5},{7,6},{8,11},{9,8},{10,9... | collective-permute-start | bytes 98312 | tf_op jit(solution)/shard_map/outputs/ppermute | solution.py:22
  139.4 7.7 %collective-permute-start.23 = (bf16[16,2048]{1,0:T(8,128)(2,1)S(1)}, bf16[16,2048]{1,0:T(8,128)(2,1)S(1)}, u32[]{:S(2)}, u32[]{:S(2)}) collective-permute-start(bf16[16,2048]{1,0:T(8,128)(2,1)S(1)} %broadcast_select_fusion.6), channel_id=1, source_target_pairs={{0,64},{64,0},{1,65},{65,1},{2,66},{66,2},{3,67},{67,3},{4,68},{68... | collective-permute-start | bytes 196616 | tf_op jit(solution)/shard_map/outputs/ppermute | solution.py:17
  (16 other events, 130.0 us)

commit v7 on v6

--- a/solution.py
+++ b/solution.py
@@ -60,7 +60,8 @@
 
 
 def gather_mp(block):
-    return in_order(from_all_mp(block))
+    got = {distance: shift_mp(block, distance) for distance in (2, 1, 3)}
+    return in_order([block] + [got[distance] for distance in range(1, len(got) + 1)])
 
 
 def in_order(blocks):
@@ -128,7 +129,13 @@
     tokens_mp = upper_deriv.shape[1]
 
     grad = jnp.where(core == 0, out_grad[:half], out_grad[half:])
-    gathered = gather_dp(grad)
+    copies = jnp.where(
+        core == 0,
+        jnp.broadcast_to(out_grad[None, :half], (dp_count, half, width)),
+        jnp.broadcast_to(out_grad[None, half:], (dp_count, half, width)),
+    )
+    gathered = lax.all_to_all(copies, "dp", 0, 0, tiled=True)
+    gathered = gathered.reshape(tokens // sections, width)
 
     deriv_up, deriv_up_sent = halves(upper_deriv[0])
     deriv_low, deriv_low_sent = halves(lower_deriv[0])
@@ -201,25 +208,27 @@
                 gathered = gather_dp(grad)
 
     with jax.named_scope("outputs"):
-        *blocks, grads[0] = held(*from_all_mp(low), grads[0])
-        low = in_order(blocks)
-
         def columns(array, section):
             turn = last - section
             left = 1 + turn
             right = 0 if turn == 0 else sections + turn
-            return [
-                array[:, left * rank : (left + 1) * rank],
-                array[:, right * rank : (right + 1) * rank],
-            ]
-
-        pair = [
-            jnp.concatenate(columns(low, s) + columns(up, s), axis=1)
-            for s in range(sections)
-        ]
-        mine = jnp.where(core == 0, pair[0], pair[1])
-        other = jnp.where(core == 0, pair[1], pair[0])
-        got = swap_sections(other)
+            return jnp.concatenate(
+                [
+                    array[:, left * rank : (left + 1) * rank],
+                    array[:, right * rank : (right + 1) * rank],
+                ],
+                axis=1,
+            )
+
+        def exchanged_columns(array):
+            first, second = columns(array, 0), columns(array, 1)
+            mine = jnp.where(core == 0, first, second)
+            return mine, swap_sections(jnp.where(core == 0, second, first))
+
+        blocks = from_all_mp(low)
+        up_mine, up_got = exchanged_columns(up)
+        *blocks, up_got, grads[0] = held(*blocks, up_got, grads[0])
+        low_mine, low_got = exchanged_columns(in_order(blocks))
 
         def joined(own, received, rows):
             own = own.reshape(-1, rows, own.shape[1])
@@ -233,7 +242,9 @@
             )
             return stack.reshape(-1, own.shape[2])
 
-        factors = joined(mine, got, half)
+        factors = jnp.concatenate(
+            [joined(low_mine, low_got, half), joined(up_mine, up_got, half)], axis=1
+        )
         mine = jnp.where(core == 0, grads[0], grads[1])
         other = jnp.where(core == 0, grads[1], grads[0])
         grads_out = joined(mine, swap_sections(other), half)

time: 151 us -> 150 us (level)
  starting transfers between devices: 62 us -> 68.8 us
  waiting for transfers between devices: 47.6 us -> 42.8 us
  matrix products: 22.2 us -> 20.3 us
    all_to_all x3 -> x2, starting transfers between devices: 14.8 us -> 7.95 us  [gather_dp(): got = lax.all_to_all(copies, 'dp', 0, 0, tiled=True)]
    all_to_all x0 -> x1, starting transfers between devices: none -> 6.84 us  [body(): gathered = lax.all_to_all(copies, 'dp', 0, 0, tiled=True)]
    ppermute x7 -> x8, starting transfers between devices: 14.8 us -> 21.5 us  [swap_sections(): return lax.ppermute(block, 'section', [(0, 1), (1, 0)])]
    all_to_all x2, waiting for transfers between devices: 18.3 us -> 12.2 us  [scatter_sum_dp(): got = lax.all_to_all(partial, 'dp', 0, 0, tiled=True)]
    all_to_all x0 -> x1, waiting for transfers between devices: none -> 6.12 us  [body(): gathered = lax.all_to_all(copies, 'dp', 0, 0, tiled=True)]
    all_to_all x3 -> x2, waiting for transfers between devices: 19.4 us -> 15.2 us  [gather_dp(): got = lax.all_to_all(copies, 'dp', 0, 0, tiled=True)]
    dot_general x10, matrix products: 21.6 us -> 19.7 us  [times_t(): lax.dot_general(left, right, (((1,), (1,)), ((), ())), preferred_element_...]
    broadcast_in_dim x3 -> x2, local copies, waits for them, and re-layouts: 3.21 us -> 2.09 us  [gather_dp(): copies = jnp.broadcast_to(block[None], (count,) + block.shape)]
  transfers between devices with their start and end apart: 30 -> 31, of which waited for: 12 -> 12; matrix products, arithmetic and copies ran while one was open for 23% -> 23% of each run, Pallas kernels for 0% -> 0%
where the time goes in v7:
time: 150 us; the launch traced here: 149 us
  starting transfers between devices  68.8 us (46%)
  waiting for transfers between devices  42.8 us (29%)
  matrix products  20.3 us (14%)
  other arithmetic  10.7 us (7%)
  local copies, waits for them, and re-layouts  5.34 us (4%)
    ppermute x18, starting transfers between devices, shift_mp(): lax.ppermute(block, 'mp', [(i, (i + distance) % count) for i in range(cou...  22.1 us
    ppermute x8, starting transfers between devices, swap_sections(): return lax.ppermute(block, 'section', [(0, 1), (1, 0)])  21.5 us
    dot_general x10, matrix products, times_t(): lax.dot_general(left, right, (((1,), (1,)), ((), ())), preferred_element_...  19.7 us
    all_to_all x2, waiting for transfers between devices, gather_dp(): got = lax.all_to_all(copies, 'dp', 0, 0, tiled=True)  15.2 us
    all_to_all x2, waiting for transfers between devices, scatter_sum_dp(): got = lax.all_to_all(partial, 'dp', 0, 0, tiled=True)  12.2 us
    all_to_all x2, starting transfers between devices, scatter_sum_dp(): got = lax.all_to_all(partial, 'dp', 0, 0, tiled=True)  10.3 us
    ppermute x18, waiting for transfers between devices, shift_mp(): lax.ppermute(block, 'mp', [(i, (i + distance) % count) for i in range(cou...  7.95 us
    all_to_all x2, starting transfers between devices, gather_dp(): got = lax.all_to_all(copies, 'dp', 0, 0, tiled=True)  7.95 us
  transfers between devices with their start and end apart: 31, of which 12 were waited for; matrix products, arithmetic and copies ran while one was open for 23% of the time, Pallas kernels for 0%

profile of v7, /device:TPU:1, one launch (start us, length us, event | category | flops | bytes accessed | tf_op | source)
XLA Modules:
  0.0 149.2 jit_solution(10013270917988240215)
XLA Ops:
  4.3 6.8 %all-to-all-start = ((bf16[16,16,2048]{2,1,0:T(8,128)(2,1)}), bf16[16,16,2048]{2,1,0:T(8,128)(2,1)S(1)}, u32[]{:S(2)}, u32[]{:S(2)}) async-start(bf16[16,16,2048]{2,1,0:T(8,128)(2,1)} %broadcast_in_dim.78), calls=%async_computation | async-start | bytes 2097152 | tf_op jit(solution)/shard_map/all_to_all | solution.py:137
  14.5 4.5 %broadcast_select_fusion = bf16[2048,896]{1,0:T(8,128)(2,1)} fusion(bf16[2048,896]{1,0:T(8,128)(2,1)} %collective-permute-done.1, pred[]{:T(512)S(6)} %eq.42, bf16[1,2048,896]{2,1,0:T(8,128)(2,1)} %param.15), kind=kLoop, calls=%fused_computation.6 | loop fusion | flops 1835008 | bytes 11010049 | tf_op jit(solution)/shard_map/up_1/jit(_where)/select_n | solution.py:122
  19.0 2.3 %broadcast_select_fusion.1 = bf16[896,2048]{1,0:T(8,128)(2,1)} fusion(bf16[896,2048]{1,0:T(8,128)(2,1)} %collective-permute-done, pred[]{:T(512)S(6)} %eq.42, bf16[1,896,2048]{2,1,0:T(8,128)(2,1)S(1)} %copy-done.1), kind=kLoop, calls=%fused_computation.7 | loop fusion | flops 1835008 | bytes 11010049 | tf_op jit(solution)/shard_map/up_1/jit(_where)/select_n | solution.py:122
  21.3 6.1 %all-to-all-done = bf16[16,16,2048]{2,1,0:T(8,128)(2,1)S(1)} async-done(((bf16[16,16,2048]{2,1,0:T(8,128)(2,1)}), bf16[16,16,2048]{2,1,0:T(8,128)(2,1)S(1)}, u32[]{:S(2)}, u32[]{:S(2)}) %all-to-all-start) | async-done | bytes 1048608 | tf_op jit(solution)/shard_map/all_to_all | solution.py:137
  27.4 3.4 %convolution_convert_fusion.1 = bf16[256,896]{1,0:T(8,128)(2,1)S(1)} fusion(bf16[256,2048]{1,0:T(8,128)(2,1)S(1)} %bitcast.118, bf16[896,2048]{1,0:T(8,128)(2,1)} %broadcast_select_fusion.1), kind=kOutput, calls=%fused_computation.13 | convolution fusion | flops 939753472 | bytes 5177344 | tf_op jit(solution)/shard_map/up_1/dot_general | solution.py:11
  32.5 3.3 %collective-permute-start.3 = (bf16[64,896]{1,0:T(8,128)(2,1)S(1)}, bf16[64,896]{1,0:T(8,128)(2,1)S(1)}, u32[]{:S(2)}, u32[]{:S(2)}) collective-permute-start(bf16[64,896]{1,0:T(8,128)(2,1)S(1)} %get-tuple-element.41), channel_id=1, source_target_pairs={{0,2},{1,3},{2,0},{3,1},{4,6},{5,7},{6,4},{7,5},{8,10},{9,11},{10,... | collective-permute-start | bytes 344072 | tf_op jit(solution)/shard_map/up_1/ppermute | solution.py:22
  36.6 3.1 %collective-permute-start.6 = (bf16[80,64]{1,0:T(8,128)(2,1)S(1)}, bf16[80,64]{1,0:T(8,128)(2,1)S(1)}, u32[]{:S(2)}, u32[]{:S(2)}) collective-permute-start(bf16[80,64]{1,0:T(8,128)(2,1)S(1)} %pad_maximum_fusion.8), channel_id=1, source_target_pairs={{0,64},{64,0},{1,65},{65,1},{2,66},{66,2},{3,67},{67,3},{4,68},{68... | collective-permute-start | bytes 30728 | tf_op jit(solution)/shard_map/ppermute | solution.py:17
  40.7 2.5 %collective-permute-start.8 = (bf16[64,896]{1,0:T(8,128)(2,1)S(1)}, bf16[64,896]{1,0:T(8,128)(2,1)S(1)}, u32[]{:S(2)}, u32[]{:S(2)}) collective-permute-start(bf16[64,896]{1,0:T(8,128)(2,1)S(1)} %get-tuple-element.63), channel_id=1, source_target_pairs={{0,2},{1,3},{2,0},{3,1},{4,6},{5,7},{6,4},{7,5},{8,10},{9,11},{10,... | collective-permute-start | bytes 344072 | tf_op jit(solution)/shard_map/low_1/ppermute | solution.py:22
  44.0 2.6 %collective-permute-done.7 = bf16[64,896]{1,0:T(8,128)(2,1)S(1)} collective-permute-done((bf16[64,896]{1,0:T(8,128)(2,1)S(1)}, bf16[64,896]{1,0:T(8,128)(2,1)S(1)}, u32[]{:S(2)}, u32[]{:S(2)}) %collective-permute-start.7) | collective-permute-done | bytes 114720 | tf_op jit(solution)/shard_map/low_1/ppermute | solution.py:22
  47.4 4.4 %convolution_convert_fusion = bf16[256,2048]{1,0:T(8,128)(2,1)} fusion(bf16[256,896]{1,0:T(8,128)(2,1)S(1)} %constant_dynamic-update-slice_fusion.8, bf16[2048,896]{1,0:T(8,128)(2,1)} %broadcast_select_fusion), kind=kOutput, calls=%fused_computation.9 | convolution fusion | flops 940048384 | bytes 5177344 | tf_op jit(solution)/shard_map/low_1/dot_general | solution.py:11
  51.8 6.6 %all-to-all-start.1 = ((bf16[16,16,2048]{2,1,0:T(8,128)(2,1)}), bf16[16,16,2048]{2,1,0:T(8,128)(2,1)S(1)}, u32[]{:S(2)}, u32[]{:S(2)}) async-start(bf16[16,16,2048]{2,1,0:T(8,128)(2,1)} %bitcast.16), calls=%async_computation.1 | async-start | bytes 2097152 | tf_op jit(solution)/shard_map/low_1/all_to_all | solution.py:36
  58.5 2.4 %collective-permute-start.10 = (bf16[80,2048]{1,0:T(8,128)(2,1)S(1)}, bf16[80,2048]{1,0:T(8,128)(2,1)S(1)}, u32[]{:S(2)}, u32[]{:S(2)}) collective-permute-start(bf16[80,2048]{1,0:T(8,128)(2,1)S(1)} %pad_maximum_fusion), channel_id=1, source_target_pairs={{0,64},{64,0},{1,65},{65,1},{2,66},{66,2},{3,67},{67,3},{4,68},{68... | collective-permute-start | bytes 983048 | tf_op jit(solution)/shard_map/ppermute | solution.py:17
  62.2 11.3 %all-to-all-done.1 = bf16[16,16,2048]{2,1,0:T(8,128)(2,1)S(1)} async-done(((bf16[16,16,2048]{2,1,0:T(8,128)(2,1)}), bf16[16,16,2048]{2,1,0:T(8,128)(2,1)S(1)}, u32[]{:S(2)}, u32[]{:S(2)}) %all-to-all-start.1) | async-done | bytes 1048608 | tf_op jit(solution)/shard_map/low_1/all_to_all | solution.py:36
  74.7 4.2 %all-to-all-start.2 = ((bf16[16,16,2048]{2,1,0:T(8,128)(2,1)}), bf16[16,16,2048]{2,1,0:T(8,128)(2,1)S(1)}, u32[]{:S(2)}, u32[]{:S(2)}) async-start(bf16[16,16,2048]{2,1,0:T(8,128)(2,1)} %broadcast_in_dim.79), calls=%async_computation.2 | async-start | bytes 2097152 | tf_op jit(solution)/shard_map/low_1/all_to_all | solution.py:30
  82.3 11.0 %all-to-all-done.2 = bf16[16,16,2048]{2,1,0:T(8,128)(2,1)S(1)} async-done(((bf16[16,16,2048]{2,1,0:T(8,128)(2,1)}), bf16[16,16,2048]{2,1,0:T(8,128)(2,1)S(1)}, u32[]{:S(2)}, u32[]{:S(2)}) %all-to-all-start.2) | async-done | bytes 1048608 | tf_op jit(solution)/shard_map/low_1/all_to_all | solution.py:30
  93.3 4.4 %fusion.9 = bf16[256,896]{1,0:T(8,128)(2,1)S(1)} fusion(bf16[256,2048]{1,0:T(8,128)(2,1)S(1)} %bitcast.119, bf16[896,2048]{1,0:T(8,128)(2,1)} %collective-permute-done, pred[]{:T(512)S(6)} %eq.41, bf16[1,896,2048]{2,1,0:T(8,128)(2,1)} %param.14), kind=kOutput, calls=%fused_computation.12 | convolution fusion | flops 941588480 | bytes 8847361 | tf_op jit(solution)/shard_map/up_0/dot_general | solution.py:11
  100.6 3.4 %collective-permute-done.11 = bf16[64,896]{1,0:T(8,128)(2,1)S(1)} collective-permute-done((bf16[64,896]{1,0:T(8,128)(2,1)S(1)}, bf16[64,896]{1,0:T(8,128)(2,1)S(1)}, u32[]{:S(2)}, u32[]{:S(2)}) %collective-permute-start.11) | collective-permute-done | bytes 114720 | tf_op jit(solution)/shard_map/up_0/ppermute | solution.py:22
  105.3 2.8 %collective-permute-start.18 = (bf16[64,896]{1,0:T(8,128)(2,1)S(1)}, bf16[64,896]{1,0:T(8,128)(2,1)S(1)}, u32[]{:S(2)}, u32[]{:S(2)}) collective-permute-start(bf16[64,896]{1,0:T(8,128)(2,1)S(1)} %get-tuple-element.65), channel_id=1, source_target_pairs={{0,2},{1,3},{2,0},{3,1},{4,6},{5,7},{6,4},{7,5},{8,10},{9,11},{10,... | collective-permute-start | bytes 344072 | tf_op jit(solution)/shard_map/low_0/ppermute | solution.py:22
  109.3 3.8 %all-to-all-start.3 = ((bf16[16,80,256]{2,1,0:T(8,128)(2,1)}), bf16[16,80,256]{2,1,0:T(8,128)(2,1)S(1)}, u32[]{:S(2)}, u32[]{:S(2)}) async-start(bf16[16,80,256]{2,1,0:T(8,128)(2,1)} %broadcast_in_dim.80), calls=%async_computation.3 | async-start | bytes 1310720 | tf_op jit(solution)/shard_map/low_0/all_to_all | solution.py:30
  113.2 5.4 %fusion.6 = bf16[256,2048]{1,0:T(8,128)(2,1)} fusion(bf16[256,896]{1,0:T(8,128)(2,1)S(1)} %constant_dynamic-update-slice_fusion.4, bf16[2048,896]{1,0:T(8,128)(2,1)} %collective-permute-done.1, pred[]{:T(512)S(6)} %eq.41, bf16[1,2048,896]{2,1,0:T(8,128)(2,1)} %param.15), kind=kOutput, calls=%fused_computation.8 | convolution fusion | flops 941883392 | bytes 8847361 | tf_op jit(solution)/shard_map/low_0/dot_general | solution.py:11
  118.6 4.2 %all-to-all-done.3 = bf16[16,80,256]{2,1,0:T(8,128)(2,1)S(1)} async-done(((bf16[16,80,256]{2,1,0:T(8,128)(2,1)}), bf16[16,80,256]{2,1,0:T(8,128)(2,1)S(1)}, u32[]{:S(2)}, u32[]{:S(2)}) %all-to-all-start.3) | async-done | bytes 655392 | tf_op jit(solution)/shard_map/low_0/all_to_all | solution.py:30
  122.9 3.7 %all-to-all-start.4 = ((bf16[16,16,2048]{2,1,0:T(8,128)(2,1)}), bf16[16,16,2048]{2,1,0:T(8,128)(2,1)S(1)}, u32[]{:S(2)}, u32[]{:S(2)}) async-start(bf16[16,16,2048]{2,1,0:T(8,128)(2,1)} %bitcast.24), calls=%async_computation.4 | async-start | bytes 2097152 | tf_op jit(solution)/shard_map/low_0/all_to_all | solution.py:36
  131.3 6.8 %collective-permute-start.23 = (bf16[256,128]{1,0:T(8,128)(2,1)S(1)}, bf16[256,128]{1,0:T(8,128)(2,1)S(1)}, u32[]{:S(2)}, u32[]{:S(2)}) collective-permute-start(bf16[256,128]{1,0:T(8,128)(2,1)S(1)} %broadcast_select_fusion.11), channel_id=1, source_target_pairs={{0,64},{64,0},{1,65},{65,1},{2,66},{66,2},{3,67},{67,3},{4,68},{68... | collective-permute-start | bytes 196616 | tf_op jit(solution)/shard_map/outputs/ppermute | solution.py:17
  139.5 6.8 %collective-permute-start.25 = (bf16[256,128]{1,0:T(8,128)(2,1)S(1)}, bf16[256,128]{1,0:T(8,128)(2,1)S(1)}, u32[]{:S(2)}, u32[]{:S(2)}) collective-permute-start(bf16[256,128]{1,0:T(8,128)(2,1)S(1)} %broadcast_select_fusion.9), channel_id=1, source_target_pairs={{0,64},{64,0},{1,65},{65,1},{2,66},{66,2},{3,67},{67,3},{4,68},{68... | collective-permute-start | bytes 196616 | tf_op jit(solution)/shard_map/outputs/ppermute | solution.py:17
  (133 shorter events, 32.2 us)
Async XLA Ops:
  0.7 13.8 %collective-permute-start.1 = (bf16[2048,896]{1,0:T(8,128)(2,1)}, bf16[2048,896]{1,0:T(8,128)(2,1)}, u32[]{:S(2)}, u32[]{:S(2)}) collective-permute-start(bf16[2048,896]{1,0:T(8,128)(2,1)} %bitcast.114), channel_id=1, source_target_pairs={{0,64},{64,0},{1,65},{65,1},{2,66},{66,2},{3,67},{67,3},{4,68},{68... | collective-permute-start | bytes 11010056 | tf_op jit(solution)/shard_map/ppermute | solution.py:17
  2.2 16.8 %collective-permute-start = (bf16[896,2048]{1,0:T(8,128)(2,1)}, bf16[896,2048]{1,0:T(8,128)(2,1)}, u32[]{:S(2)}, u32[]{:S(2)}) collective-permute-start(bf16[896,2048]{1,0:T(8,128)(2,1)} %bitcast.113), channel_id=1, source_target_pairs={{0,64},{64,0},{1,65},{65,1},{2,66},{66,2},{3,67},{67,3},{4,68},{68... | collective-permute-start | bytes 11010056 | tf_op jit(solution)/shard_map/ppermute | solution.py:17
  4.3 23.1 %all-to-all-start = ((bf16[16,16,2048]{2,1,0:T(8,128)(2,1)}), bf16[16,16,2048]{2,1,0:T(8,128)(2,1)S(1)}, u32[]{:S(2)}, u32[]{:S(2)}) async-start(bf16[16,16,2048]{2,1,0:T(8,128)(2,1)} %broadcast_in_dim.78), calls=%async_computation | async-start | bytes 2097152 | tf_op jit(solution)/shard_map/all_to_all | solution.py:137
  12.2 27.5 %collective-permute-start.5 = (bf16[128,896]{1,0:T(8,128)(2,1)S(1)}, bf16[128,896]{1,0:T(8,128)(2,1)S(1)}, u32[]{:S(2)}, u32[]{:S(2)}) collective-permute-start(bf16[128,896]{1,0:T(8,128)(2,1)S(1)} %pad_maximum_fusion.1), channel_id=1, source_target_pairs={{0,64},{64,0},{1,65},{65,1},{2,66},{66,2},{3,67},{67,3},{4,68},{68... | collective-permute-start | bytes 688136 | tf_op jit(solution)/shard_map/ppermute | solution.py:17
  30.8 8.9 %collective-permute-start.2 = (bf16[64,896]{1,0:T(8,128)(2,1)S(1)}, bf16[64,896]{1,0:T(8,128)(2,1)S(1)}, u32[]{:S(2)}, u32[]{:S(2)}) collective-permute-start(bf16[64,896]{1,0:T(8,128)(2,1)S(1)} %get-tuple-element.39), channel_id=1, source_target_pairs={{0,1},{1,2},{2,3},{3,0},{4,5},{5,6},{6,7},{7,4},{8,9},{9,10},{10,1... | collective-permute-start | bytes 344072 | tf_op jit(solution)/shard_map/up_1/ppermute | solution.py:22
  32.5 7.2 %collective-permute-start.3 = (bf16[64,896]{1,0:T(8,128)(2,1)S(1)}, bf16[64,896]{1,0:T(8,128)(2,1)S(1)}, u32[]{:S(2)}, u32[]{:S(2)}) collective-permute-start(bf16[64,896]{1,0:T(8,128)(2,1)S(1)} %get-tuple-element.41), channel_id=1, source_target_pairs={{0,2},{1,3},{2,0},{3,1},{4,6},{5,7},{6,4},{7,5},{8,10},{9,11},{10,... | collective-permute-start | bytes 344072 | tf_op jit(solution)/shard_map/up_1/ppermute | solution.py:22
  36.6 24.3 %collective-permute-start.6 = (bf16[80,64]{1,0:T(8,128)(2,1)S(1)}, bf16[80,64]{1,0:T(8,128)(2,1)S(1)}, u32[]{:S(2)}, u32[]{:S(2)}) collective-permute-start(bf16[80,64]{1,0:T(8,128)(2,1)S(1)} %pad_maximum_fusion.8), channel_id=1, source_target_pairs={{0,64},{64,0},{1,65},{65,1},{2,66},{66,2},{3,67},{67,3},{4,68},{68... | collective-permute-start | bytes 30728 | tf_op jit(solution)/shard_map/ppermute | solution.py:17
  40.5 6.2 %collective-permute-start.7 = (bf16[64,896]{1,0:T(8,128)(2,1)S(1)}, bf16[64,896]{1,0:T(8,128)(2,1)S(1)}, u32[]{:S(2)}, u32[]{:S(2)}) collective-permute-start(bf16[64,896]{1,0:T(8,128)(2,1)S(1)} %get-tuple-element.63), channel_id=1, source_target_pairs={{0,1},{1,2},{2,3},{3,0},{4,5},{5,6},{6,7},{7,4},{8,9},{9,10},{10,1... | collective-permute-start | bytes 344072 | tf_op jit(solution)/shard_map/low_1/ppermute | solution.py:22
  51.8 21.6 %all-to-all-start.1 = ((bf16[16,16,2048]{2,1,0:T(8,128)(2,1)}), bf16[16,16,2048]{2,1,0:T(8,128)(2,1)S(1)}, u32[]{:S(2)}, u32[]{:S(2)}) async-start(bf16[16,16,2048]{2,1,0:T(8,128)(2,1)} %bitcast.16), calls=%async_computation.1 | async-start | bytes 2097152 | tf_op jit(solution)/shard_map/low_1/all_to_all | solution.py:36
  74.7 18.5 %all-to-all-start.2 = ((bf16[16,16,2048]{2,1,0:T(8,128)(2,1)}), bf16[16,16,2048]{2,1,0:T(8,128)(2,1)S(1)}, u32[]{:S(2)}, u32[]{:S(2)}) async-start(bf16[16,16,2048]{2,1,0:T(8,128)(2,1)} %broadcast_in_dim.79), calls=%async_computation.2 | async-start | bytes 2097152 | tf_op jit(solution)/shard_map/low_1/all_to_all | solution.py:30
  79.6 19.2 %collective-permute-start.14 = (bf16[16,256]{1,0:T(8,128)(2,1)S(1)}, bf16[16,256]{1,0:T(8,128)(2,1)S(1)}, u32[]{:S(2)}, u32[]{:S(2)}) collective-permute-start(bf16[16,256]{1,0:T(8,128)(2,1)S(1)} %pad_maximum_fusion.9), channel_id=1, source_target_pairs={{0,1},{1,2},{2,3},{3,0},{4,5},{5,6},{6,7},{7,4},{8,9},{9,10},{10,1... | collective-permute-start | bytes 24584 | tf_op jit(solution)/shard_map/up_0/ppermute | solution.py:22
  79.6 20.9 %collective-permute-start.15 = (bf16[16,256]{1,0:T(8,128)(2,1)S(1)}, bf16[16,256]{1,0:T(8,128)(2,1)S(1)}, u32[]{:S(2)}, u32[]{:S(2)}) collective-permute-start(bf16[16,256]{1,0:T(8,128)(2,1)S(1)} %pad_maximum_fusion.9), channel_id=1, source_target_pairs={{0,2},{1,3},{2,0},{3,1},{4,6},{5,7},{6,4},{7,5},{8,10},{9,11},{10,... | collective-permute-start | bytes 24584 | tf_op jit(solution)/shard_map/up_0/ppermute | solution.py:22
  81.5 19.1 %collective-permute-start.16 = (bf16[16,256]{1,0:T(8,128)(2,1)S(1)}, bf16[16,256]{1,0:T(8,128)(2,1)S(1)}, u32[]{:S(2)}, u32[]{:S(2)}) collective-permute-start(bf16[16,256]{1,0:T(8,128)(2,1)S(1)} %pad_maximum_fusion.9), channel_id=1, source_target_pairs={{0,3},{1,0},{2,1},{3,2},{4,7},{5,4},{6,5},{7,6},{8,11},{9,8},{10,9... | collective-permute-start | bytes 24584 | tf_op jit(solution)/shard_map/up_0/ppermute | solution.py:22
  97.8 6.2 %collective-permute-start.11 = (bf16[64,896]{1,0:T(8,128)(2,1)S(1)}, bf16[64,896]{1,0:T(8,128)(2,1)S(1)}, u32[]{:S(2)}, u32[]{:S(2)}) collective-permute-start(bf16[64,896]{1,0:T(8,128)(2,1)S(1)} %get-tuple-element.34), channel_id=1, source_target_pairs={{0,1},{1,2},{2,3},{3,0},{4,5},{5,6},{6,7},{7,4},{8,9},{9,10},{10,1... | collective-permute-start | bytes 344072 | tf_op jit(solution)/shard_map/up_0/ppermute | solution.py:22
  97.9 6.1 %collective-permute-start.12 = (bf16[64,896]{1,0:T(8,128)(2,1)S(1)}, bf16[64,896]{1,0:T(8,128)(2,1)S(1)}, u32[]{:S(2)}, u32[]{:S(2)}) collective-permute-start(bf16[64,896]{1,0:T(8,128)(2,1)S(1)} %get-tuple-element.36), channel_id=1, source_target_pairs={{0,2},{1,3},{2,0},{3,1},{4,6},{5,7},{6,4},{7,5},{8,10},{9,11},{10,... | collective-permute-start | bytes 344072 | tf_op jit(solution)/shard_map/up_0/ppermute | solution.py:22
  104.7 8.3 %collective-permute-start.17 = (bf16[64,896]{1,0:T(8,128)(2,1)S(1)}, bf16[64,896]{1,0:T(8,128)(2,1)S(1)}, u32[]{:S(2)}, u32[]{:S(2)}) collective-permute-start(bf16[64,896]{1,0:T(8,128)(2,1)S(1)} %get-tuple-element.65), channel_id=1, source_target_pairs={{0,1},{1,2},{2,3},{3,0},{4,5},{5,6},{6,7},{7,4},{8,9},{9,10},{10,1... | collective-permute-start | bytes 344072 | tf_op jit(solution)/shard_map/low_0/ppermute | solution.py:22
  105.3 7.8 %collective-permute-start.18 = (bf16[64,896]{1,0:T(8,128)(2,1)S(1)}, bf16[64,896]{1,0:T(8,128)(2,1)S(1)}, u32[]{:S(2)}, u32[]{:S(2)}) collective-permute-start(bf16[64,896]{1,0:T(8,128)(2,1)S(1)} %get-tuple-element.65), channel_id=1, source_target_pairs={{0,2},{1,3},{2,0},{3,1},{4,6},{5,7},{6,4},{7,5},{8,10},{9,11},{10,... | collective-permute-start | bytes 344072 | tf_op jit(solution)/shard_map/low_0/ppermute | solution.py:22
  109.3 13.6 %all-to-all-start.3 = ((bf16[16,80,256]{2,1,0:T(8,128)(2,1)}), bf16[16,80,256]{2,1,0:T(8,128)(2,1)S(1)}, u32[]{:S(2)}, u32[]{:S(2)}) async-start(bf16[16,80,256]{2,1,0:T(8,128)(2,1)} %broadcast_in_dim.80), calls=%async_computation.3 | async-start | bytes 1310720 | tf_op jit(solution)/shard_map/low_0/all_to_all | solution.py:30
  122.9 16.0 %all-to-all-start.4 = ((bf16[16,16,2048]{2,1,0:T(8,128)(2,1)}), bf16[16,16,2048]{2,1,0:T(8,128)(2,1)S(1)}, u32[]{:S(2)}, u32[]{:S(2)}) async-start(bf16[16,16,2048]{2,1,0:T(8,128)(2,1)} %bitcast.24), calls=%async_computation.4 | async-start | bytes 2097152 | tf_op jit(solution)/shard_map/low_0/all_to_all | solution.py:36
  126.9 12.3 %collective-permute-start.20 = (bf16[64,256]{1,0:T(8,128)(2,1)S(1)}, bf16[64,256]{1,0:T(8,128)(2,1)S(1)}, u32[]{:S(2)}, u32[]{:S(2)}) collective-permute-start(bf16[64,256]{1,0:T(8,128)(2,1)S(1)} %slice_reduce_fusion), channel_id=1, source_target_pairs={{0,1},{1,2},{2,3},{3,0},{4,5},{5,6},{6,7},{7,4},{8,9},{9,10},{10,1... | collective-permute-start | bytes 98312 | tf_op jit(solution)/shard_map/outputs/ppermute | solution.py:22
  128.3 10.9 %collective-permute-start.21 = (bf16[64,256]{1,0:T(8,128)(2,1)S(1)}, bf16[64,256]{1,0:T(8,128)(2,1)S(1)}, u32[]{:S(2)}, u32[]{:S(2)}) collective-permute-start(bf16[64,256]{1,0:T(8,128)(2,1)S(1)} %slice_reduce_fusion), channel_id=1, source_target_pairs={{0,2},{1,3},{2,0},{3,1},{4,6},{5,7},{6,4},{7,5},{8,10},{9,11},{10,... | collective-permute-start | bytes 98312 | tf_op jit(solution)/shard_map/outputs/ppermute | solution.py:22
  129.1 10.1 %collective-permute-start.22 = (bf16[64,256]{1,0:T(8,128)(2,1)S(1)}, bf16[64,256]{1,0:T(8,128)(2,1)S(1)}, u32[]{:S(2)}, u32[]{:S(2)}) collective-permute-start(bf16[64,256]{1,0:T(8,128)(2,1)S(1)} %slice_reduce_fusion), channel_id=1, source_target_pairs={{0,3},{1,0},{2,1},{3,2},{4,7},{5,4},{6,5},{7,6},{8,11},{9,8},{10,9... | collective-permute-start | bytes 98312 | tf_op jit(solution)/shard_map/outputs/ppermute | solution.py:22
  131.3 7.9 %collective-permute-start.23 = (bf16[256,128]{1,0:T(8,128)(2,1)S(1)}, bf16[256,128]{1,0:T(8,128)(2,1)S(1)}, u32[]{:S(2)}, u32[]{:S(2)}) collective-permute-start(bf16[256,128]{1,0:T(8,128)(2,1)S(1)} %broadcast_select_fusion.11), channel_id=1, source_target_pairs={{0,64},{64,0},{1,65},{65,1},{2,66},{66,2},{3,67},{67,3},{4,68},{68... | collective-permute-start | bytes 196616 | tf_op jit(solution)/shard_map/outputs/ppermute | solution.py:17
  139.5 7.7 %collective-permute-start.25 = (bf16[256,128]{1,0:T(8,128)(2,1)S(1)}, bf16[256,128]{1,0:T(8,128)(2,1)S(1)}, u32[]{:S(2)}, u32[]{:S(2)}) collective-permute-start(bf16[256,128]{1,0:T(8,128)(2,1)S(1)} %broadcast_select_fusion.9), channel_id=1, source_target_pairs={{0,64},{64,0},{1,65},{65,1},{2,66},{66,2},{3,67},{67,3},{4,68},{68... | collective-permute-start | bytes 196616 | tf_op jit(solution)/shard_map/outputs/ppermute | solution.py:17
  (16 other events, 135.4 us)
